TPU v7x, 32 devices: a whole 2x2x4 slice. The times are simulated.
32 devices in a mesh: dp: 4 (over y, x), tensor: 8 (over z, core).
Axes of the slice: x: 2, y: 2, z: 4, core: 2. Of those that a mesh axis runs over, the one named last changes fastest.
Arguments:
- inputs: bfloat16 [16384, 2048], P(('dp', 'tensor')), may hold values from -6 to 6
- block_ids: int32 [16, 1024], P('dp'), may hold values from 0 to 4, never falling along the last dimension, each value on 1 to 256 neighbouring positions
- norm_gain: bfloat16 [2048], replicated, may hold values from 0.5 to 1.5
- norm_bias: bfloat16 [2048], replicated, may hold values from -3 to 3
- query_weight: bfloat16 [2048, 2048], P('dp', 'tensor'), may hold values from -0.125 to 0.125
- query_bias: bfloat16 [2048], P('tensor'), may hold values from -3 to 3
- key_weight: bfloat16 [2048, 2048], P('dp', 'tensor'), may hold values from -0.125 to 0.125
- key_bias: bfloat16 [2048], P('tensor'), may hold values from -3 to 3
- value_weight: bfloat16 [2048, 2048], P('dp', 'tensor'), may hold values from -0.125 to 0.125
- value_bias: bfloat16 [2048], P('tensor'), may hold values from -3 to 3
- out_weight: bfloat16 [2048, 2048], P('tensor', 'dp'), may hold values from -3 to 3
- out_bias: bfloat16 [2048], replicated, may hold values from -3 to 3
- up_weight: bfloat16 [2048, 8192], P('dp', 'tensor'), may hold values from -0.125 to 0.125
- up_bias: bfloat16 [8192], P('tensor'), may hold values from -3 to 3
- down_weight: bfloat16 [8192, 2048], P('tensor', 'dp'), may hold values from -0.09375 to 0.09375
- down_bias: bfloat16 [2048], replicated, may hold values from -3 to 3
- grad_out: bfloat16 [16384, 2048], P(('dp', 'tensor')), may hold values from -6 to 6
Outputs:
- output: bfloat16 [16384, 2048], P(('dp', 'tensor'))
- input_grad: bfloat16 [16384, 2048], P(('dp', 'tensor'))
- norm_gain_grad: float32 [2048], replicated
- norm_bias_grad: float32 [2048], replicated
- query_weight_grad: float32 [2048, 2048], P('dp', 'tensor')
- query_bias_grad: float32 [2048], P('tensor')
- key_weight_grad: float32 [2048, 2048], P('dp', 'tensor')
- key_bias_grad: float32 [2048], P('tensor')
- value_weight_grad: float32 [2048, 2048], P('dp', 'tensor')
- value_bias_grad: float32 [2048], P('tensor')
- out_weight_grad: float32 [2048, 2048], P('tensor', 'dp')
- out_bias_grad: float32 [2048], replicated
- up_weight_grad: float32 [2048, 8192], P('dp', 'tensor')
- up_bias_grad: float32 [8192], P('tensor')
- down_weight_grad: float32 [8192, 2048], P('tensor', 'dp')
- down_bias_grad: float32 [2048], replicated
Inputs may be any that keep to these rules, and one draw needn't show every extreme that they name: `block_ids`: in each sequence the block numbers never fall along the positions; a block spans 1 to 256 positions, and one block of each sequence spans exactly 256.
All inputs are finite; a program needn't handle non-finite values.
Results may differ from a plain program's by a relative error of at most 0.012.
The roundings to bfloat16 on the way count: a program that leaves them out, or rounds other values in their place, can miss the bound.
Values may be sent and summed in bfloat16 or wider, within the bound.
A program may use at most 320 MiB of HBM per device.

v0:
```python
import jax
import jax.numpy as jnp
from jax import lax
from jax.sharding import PartitionSpec as P

HEAD_DIM = 64
ROT = 32


eps_norm = 1e-05


def normalize(values, gain_in, shift_in):
    center = jnp.mean(values, axis=-1, keepdims=True)
    centered = values - center
    variance = jnp.mean(centered * centered, axis=-1, keepdims=True)
    return centered * lax.rsqrt(variance + eps_norm) * gain_in + shift_in


def rotary_tables(length, rot_width):
    halves = rot_width // 2
    exponent = jnp.arange(halves, dtype=jnp.float32) * (2.0 / rot_width)
    frequency = jnp.power(10000.0, -exponent)
    angles = jnp.arange(length, dtype=jnp.float32)[:, None] * frequency[None, :]
    angles = jnp.concatenate([angles, angles], axis=1)
    return (jnp.cos(angles), jnp.sin(angles))


def rotate(per_head, cos_table, sin_table):
    rot_width = cos_table.shape[-1]
    halves = rot_width // 2
    first_half = per_head[..., :halves]
    second_half = per_head[..., halves:rot_width]
    turned = jnp.concatenate([-second_half, first_half], axis=-1)
    rotated = per_head[..., :rot_width] * cos_table[:, None, :] + turned * sin_table[:, None, :]
    return jnp.concatenate([rotated, per_head[..., rot_width:]], axis=-1)


def masked_scores(query_block, key_block, query_ids, key_ids):
    raw_scores = jnp.einsum(
        "qhd,khd->hqk", query_block, key_block, preferred_element_type=jnp.float32
    ) * HEAD_DIM ** (-0.5)
    allowed = key_ids[None, None, :] <= query_ids[None, :, None]
    return jnp.where(allowed, raw_scores, -1000000000.0)


def gelu_tanh(values):
    return jax.nn.gelu(values, approximate=True)


def per_device(
    inputs,
    block_ids,
    norm_gain,
    norm_bias,
    query_weight,
    query_bias,
    key_weight,
    key_bias,
    value_weight,
    value_bias,
    out_weight,
    out_bias,
    up_weight,
    up_bias,
    down_weight,
    down_bias,
    grad_out,
):
    seq_count, length = block_ids.shape
    local_width = query_weight.shape[1]
    local_heads = local_width // HEAD_DIM
    block_rows = min(512, length)
    per_sequence = length // block_rows
    all_rows = seq_count * length
    score_scale = HEAD_DIM ** (-0.5)
    gain_float = norm_gain.astype(jnp.float32)
    shift_float = norm_bias.astype(jnp.float32)
    inputs_float = inputs.astype(jnp.float32)
    normed = normalize(inputs_float, gain_float, shift_float).astype(jnp.bfloat16)
    full_query, full_key, full_value, full_up, full_out, full_down = (
        lax.all_gather(query_weight, "dp", axis=0, tiled=True),
        lax.all_gather(key_weight, "dp", axis=0, tiled=True),
        lax.all_gather(value_weight, "dp", axis=0, tiled=True),
        lax.all_gather(up_weight, "dp", axis=0, tiled=True),
        lax.all_gather(out_weight, "dp", axis=1, tiled=True),
        lax.all_gather(down_weight, "dp", axis=1, tiled=True),
    )
    group_rows = lax.all_gather(normed, "tensor", axis=0, tiled=True)
    cos_table, sin_table = rotary_tables(length, ROT)

    def project(weight_part, bias_part):
        return jnp.dot(
            group_rows, weight_part, preferred_element_type=jnp.float32
        ) + bias_part.astype(jnp.float32)

    def split_heads(values):
        return values.reshape(seq_count, length, local_heads, HEAD_DIM)

    queries = rotate(split_heads(project(full_query, query_bias)), cos_table, sin_table).astype(
        jnp.bfloat16
    )
    key_rows = rotate(split_heads(project(full_key, key_bias)), cos_table, sin_table).astype(
        jnp.bfloat16
    )
    value_rows = split_heads(project(full_value, value_bias)).astype(jnp.bfloat16)

    def forward_block(block_index):
        sequence = block_index // per_sequence
        offset = block_index % per_sequence * block_rows
        seq_ids = block_ids[sequence]
        query_block = lax.dynamic_slice_in_dim(queries[sequence], offset, block_rows, 0)
        query_ids = lax.dynamic_slice_in_dim(seq_ids, offset, block_rows, 0)
        scores = masked_scores(query_block, key_rows[sequence], query_ids, seq_ids)
        highest = jnp.max(scores, axis=2, keepdims=True)
        shifted = jnp.exp(scores - highest)
        totals = jnp.sum(shifted, axis=2, keepdims=True)
        weights_low = (shifted / totals).astype(jnp.bfloat16)
        mixed_rows = jnp.einsum(
            "hqk,khd->qhd", weights_low, value_rows[sequence], preferred_element_type=jnp.float32
        )
        return (mixed_rows, (highest + jnp.log(totals))[:, :, 0])

    attended, log_sums = lax.map(forward_block, jnp.arange(seq_count * per_sequence))
    attended_low = attended.reshape(all_rows, local_width).astype(jnp.bfloat16)
    hidden = project(full_up, up_bias)
    active = gelu_tanh(hidden).astype(jnp.bfloat16)
    branch_rows = lax.psum_scatter(
        jnp.dot(attended_low, full_out, preferred_element_type=jnp.float32)
        + jnp.dot(active, full_down, preferred_element_type=jnp.float32),
        "tensor",
        scatter_dimension=0,
        tiled=True,
    )
    output = (
        inputs_float + branch_rows + out_bias.astype(jnp.float32) + down_bias.astype(jnp.float32)
    ).astype(jnp.bfloat16)
    back_query, back_key, back_value, back_up, back_out, back_down = (
        lax.all_gather(query_weight, "dp", axis=0, tiled=True),
        lax.all_gather(key_weight, "dp", axis=0, tiled=True),
        lax.all_gather(value_weight, "dp", axis=0, tiled=True),
        lax.all_gather(up_weight, "dp", axis=0, tiled=True),
        lax.all_gather(out_weight, "dp", axis=1, tiled=True),
        lax.all_gather(down_weight, "dp", axis=1, tiled=True),
    )
    back_rows = lax.all_gather(normed, "tensor", axis=0, tiled=True)
    upstream = lax.all_gather(grad_out, "tensor", axis=0, tiled=True)
    out_wgrad = jnp.einsum("rk,rd->kd", attended_low, upstream, preferred_element_type=jnp.float32)
    down_wgrad = jnp.einsum("rf,rd->fd", active, upstream, preferred_element_type=jnp.float32)
    attended_grad = jnp.einsum(
        "rd,kd->rk", upstream, back_out, preferred_element_type=jnp.float32
    ).astype(jnp.bfloat16)
    active_grad = jnp.einsum("rd,fd->rf", upstream, back_down, preferred_element_type=jnp.float32)
    unused_value, gelu_pull = jax.vjp(gelu_tanh, hidden)
    hidden_grad = gelu_pull(active_grad)[0].astype(jnp.bfloat16)
    grad_heads = split_heads(attended_grad)
    sums_grouped = log_sums.reshape(seq_count, per_sequence, local_heads, block_rows)

    def backward_sequence(sequence):
        seq_ids = block_ids[sequence]
        seq_queries = queries[sequence]
        seq_keys = key_rows[sequence]
        seq_values = value_rows[sequence]
        seq_grads = grad_heads[sequence]
        seq_sums = sums_grouped[sequence]

        def backward_block(running, block_number):
            key_total, value_total = running
            offset = block_number * block_rows
            query_block = lax.dynamic_slice_in_dim(seq_queries, offset, block_rows, 0)
            query_ids = lax.dynamic_slice_in_dim(seq_ids, offset, block_rows, 0)
            grad_block = lax.dynamic_slice_in_dim(seq_grads, offset, block_rows, 0)
            scores = masked_scores(query_block, seq_keys, query_ids, seq_ids)
            prob_rows = jnp.exp(scores - seq_sums[block_number][:, :, None])
            value_total = value_total + jnp.einsum(
                "hqk,qhd->khd",
                prob_rows.astype(jnp.bfloat16),
                grad_block,
                preferred_element_type=jnp.float32,
            )
            prob_grad = jnp.einsum(
                "qhd,khd->hqk", grad_block, seq_values, preferred_element_type=jnp.float32
            )
            row_inner = jnp.sum(prob_grad * prob_rows, axis=2, keepdims=True)
            score_grad = (prob_rows * (prob_grad - row_inner)).astype(jnp.bfloat16)
            query_part = (
                jnp.einsum("hqk,khd->qhd", score_grad, seq_keys, preferred_element_type=jnp.float32)
                * score_scale
            )
            key_total = (
                key_total
                + jnp.einsum(
                    "hqk,qhd->khd", score_grad, query_block, preferred_element_type=jnp.float32
                )
                * score_scale
            )
            return ((key_total, value_total), query_part)

        zero_total = jnp.zeros((length, local_heads, HEAD_DIM), jnp.float32)
        (key_total, value_total), query_parts = lax.scan(
            backward_block, (zero_total, zero_total), jnp.arange(per_sequence)
        )
        return (query_parts.reshape(length, local_heads, HEAD_DIM), key_total, value_total)

    query_grad_rot, key_grad_rot, value_grad_all = lax.map(backward_sequence, jnp.arange(seq_count))
    query_grad = (
        rotate(query_grad_rot, cos_table, -sin_table)
        .reshape(all_rows, local_width)
        .astype(jnp.bfloat16)
    )
    key_grad = (
        rotate(key_grad_rot, cos_table, -sin_table)
        .reshape(all_rows, local_width)
        .astype(jnp.bfloat16)
    )
    value_grad = value_grad_all.reshape(all_rows, local_width).astype(jnp.bfloat16)
    query_wgrad = jnp.einsum("rd,rk->dk", back_rows, query_grad, preferred_element_type=jnp.float32)
    key_wgrad = jnp.einsum("rd,rk->dk", back_rows, key_grad, preferred_element_type=jnp.float32)
    value_wgrad = jnp.einsum("rd,rk->dk", back_rows, value_grad, preferred_element_type=jnp.float32)
    up_wgrad = jnp.einsum("rd,rf->df", back_rows, hidden_grad, preferred_element_type=jnp.float32)
    normed_grad = lax.psum_scatter(
        jnp.einsum("rk,dk->rd", query_grad, back_query, preferred_element_type=jnp.float32)
        + jnp.einsum("rk,dk->rd", key_grad, back_key, preferred_element_type=jnp.float32)
        + jnp.einsum("rk,dk->rd", value_grad, back_value, preferred_element_type=jnp.float32)
        + jnp.einsum("rf,df->rd", hidden_grad, back_up, preferred_element_type=jnp.float32),
        "tensor",
        scatter_dimension=0,
        tiled=True,
    )
    unused_norm, norm_pull = jax.vjp(normalize, inputs_float, gain_float, shift_float)
    input_part, gain_part, shift_part = norm_pull(normed_grad)
    input_grad = (grad_out.astype(jnp.float32) + input_part).astype(jnp.bfloat16)
    bias_part = jnp.sum(grad_out, axis=0, dtype=jnp.float32)
    gain_grad, shift_grad, outer_bias_grad = lax.psum(
        (gain_part, shift_part, bias_part), ("dp", "tensor")
    )
    query_bias_grad, key_bias_grad, value_bias_grad, up_bias_grad = lax.psum(
        (
            jnp.sum(query_grad, axis=0, dtype=jnp.float32),
            jnp.sum(key_grad, axis=0, dtype=jnp.float32),
            jnp.sum(value_grad, axis=0, dtype=jnp.float32),
            jnp.sum(hidden_grad, axis=0, dtype=jnp.float32),
        ),
        "dp",
    )
    (
        query_weight_grad,
        key_weight_grad,
        value_weight_grad,
        up_weight_grad,
        out_weight_grad,
        down_weight_grad,
    ) = (
        lax.psum_scatter(query_wgrad, "dp", scatter_dimension=0, tiled=True),
        lax.psum_scatter(key_wgrad, "dp", scatter_dimension=0, tiled=True),
        lax.psum_scatter(value_wgrad, "dp", scatter_dimension=0, tiled=True),
        lax.psum_scatter(up_wgrad, "dp", scatter_dimension=0, tiled=True),
        lax.psum_scatter(out_wgrad, "dp", scatter_dimension=1, tiled=True),
        lax.psum_scatter(down_wgrad, "dp", scatter_dimension=1, tiled=True),
    )
    return (
        output,
        input_grad,
        gain_grad,
        shift_grad,
        query_weight_grad,
        query_bias_grad,
        key_weight_grad,
        key_bias_grad,
        value_weight_grad,
        value_bias_grad,
        out_weight_grad,
        outer_bias_grad,
        up_weight_grad,
        up_bias_grad,
        down_weight_grad,
        outer_bias_grad,
    )


def solution(mesh):
    return jax.shard_map(
        per_device,
        mesh=mesh,
        in_specs=(
            P(("dp", "tensor"), None),
            P("dp", None),
            P(),
            P(),
            P("dp", "tensor"),
            P("tensor"),
            P("dp", "tensor"),
            P("tensor"),
            P("dp", "tensor"),
            P("tensor"),
            P("tensor", "dp"),
            P(),
            P("dp", "tensor"),
            P("tensor"),
            P("tensor", "dp"),
            P(),
            P(("dp", "tensor"), None),
        ),
        out_specs=(
            P(("dp", "tensor"), None),
            P(("dp", "tensor"), None),
            P(),
            P(),
            P("dp", "tensor"),
            P("tensor"),
            P("dp", "tensor"),
            P("tensor"),
            P("dp", "tensor"),
            P("tensor"),
            P("tensor", "dp"),
            P(),
            P("dp", "tensor"),
            P("tensor"),
            P("tensor", "dp"),
            P(),
        ),
        check_vma=False,
    )
```

profile of v0, /device:TPU:0, one launch (start us, length us, event | category | flops | bytes accessed | tf_op | source)
XLA Modules:
  0.0 2073.7 jit_solution(4787446761198307838)
XLA Ops:
  39.2 153.3 %all-gather.9.cloned.1.call-done = bf16[4096,2048]{1,0:T(8,128)(2,1)} async-done(((bf16[512,2048]{1,0:T(8,128)(2,1)}), bf16[4096,2048]{1,0:T(8,128)(2,1)}) %all-gather.9.cloned.1.call-update) | async-done | bytes 16777232 | tf_op jit(solution)/shard_map/all_gather | solution.py:89
  279.0 149.5 %all-gather.23.cloned.1.call-done = bf16[4096,2048]{1,0:T(8,128)(2,1)} async-done(((bf16[512,2048]{1,0:T(8,128)(2,1)}), bf16[4096,2048]{1,0:T(8,128)(2,1)}) %all-gather.23.cloned.1.call-update) | async-done | bytes 16777232 | tf_op jit(solution)/shard_map/all_gather | solution.py:147
  466.1 102.8 %while.44 = (s32[]{:T(128)}, bf16[8,512,4,64]{1,3,2,0:T(8,128)(2,1)S(1)}, f32[8,4,512]{2,1,0:T(4,128)S(1)}, s32[8]{0:T(128)S(1)}, bf16[4,1024,4,64]{1,3,2,0:T(8,...) while((s32[]{:T(128)}, ...), condition=%wide.region_5.6_spmd, body=%wide.region_2.5_spmd.sunk | while | flops 562558976 | bytes 29182452 | solution.py:124
  570.1 342.8 %while.46 = (s32[]{:T(128)}, f32[4,1024,4,64]{1,0,3,2:T(4,128)}, f32[4,1024,4,64]{1,0,3,2:T(4,128)}, bf16[4,1024,4,64]{1,3,2,0:T(8,128)(2,1)}, s32[4]{0:T(128)S(...) while((s32[]{:T(128)}, f32[4,1024,4,64]{1,0,3,2:T(4,128)}, ...), condition=%wide.region_11.12_spmd, body=%wide.region_7.11_spmd.sunk | while | flops 1375598592 | bytes 110209856 | solution.py:205
  575.8 33.3 %while.47 = (s32[]{:T(128)}, f32[1024,4,64]{0,2,1:T(8,128)S(1)}, f32[1024,4,64]{0,2,1:T(8,128)}, f32[2,512,4,64]{1,3,2,0:T(8,128)}, s32[2]{0:T(128)S(1)}, /*inde...) while((s32[]{:T(128)}, f32[1024,4,64]{0,2,1:T(8,128)S(1)}, ...), condition=%wide.region_10.10_spmd.clone, body=%wide.region_8.9_spmd.clone.sunk | while | flops 1375598592 | bytes 89196952 | solution.py:200
  661.3 33.3 %while.47 = (s32[]{:T(128)}, f32[1024,4,64]{0,2,1:T(8,128)S(1)}, f32[1024,4,64]{0,2,1:T(8,128)}, f32[2,512,4,64]{1,3,2,0:T(8,128)}, s32[2]{0:T(128)S(1)}, /*inde...) while((s32[]{:T(128)}, f32[1024,4,64]{0,2,1:T(8,128)S(1)}, ...), condition=%wide.region_10.10_spmd.clone, body=%wide.region_8.9_spmd.clone.sunk | while | flops 1375598592 | bytes 89196952 | solution.py:200
  746.9 33.3 %while.47 = (s32[]{:T(128)}, f32[1024,4,64]{0,2,1:T(8,128)S(1)}, f32[1024,4,64]{0,2,1:T(8,128)}, f32[2,512,4,64]{1,3,2,0:T(8,128)}, s32[2]{0:T(128)S(1)}, /*inde...) while((s32[]{:T(128)}, f32[1024,4,64]{0,2,1:T(8,128)S(1)}, ...), condition=%wide.region_10.10_spmd.clone, body=%wide.region_8.9_spmd.clone.sunk | while | flops 1375598592 | bytes 89196952 | solution.py:200
  807.3 19.9 dynamic_update_slice.45
  832.5 33.3 %while.47 = (s32[]{:T(128)}, f32[1024,4,64]{0,2,1:T(8,128)S(1)}, f32[1024,4,64]{0,2,1:T(8,128)}, f32[2,512,4,64]{1,3,2,0:T(8,128)}, s32[2]{0:T(128)S(1)}, /*inde...) while((s32[]{:T(128)}, f32[1024,4,64]{0,2,1:T(8,128)S(1)}, ...), condition=%wide.region_10.10_spmd.clone, body=%wide.region_8.9_spmd.clone.sunk | while | flops 1375598592 | bytes 89196952 | solution.py:200
  892.9 19.9 dynamic_update_slice.45
  972.6 23.4 %fusion.80 = f32[4096,1024]{1,0:T(8,128)} fusion(bf16[4096,2048]{1,0:T(8,128)(2,1)} %all-gather.9.cloned.1.call-done, bf16[2048,1024]{1,0:T(8,128)(2,1)} %all-gather.19.cloned.1.call-done), kind=kOutput, calls=%fused_computation.136 | convolution fusion | flops 17179869184 | bytes 37748736 | tf_op jit(solution)/shard_map/dot_general | solution.py:93
  996.0 36.7 %convert_reduce_fusion = (f32[1024]{0:T(1024)}, bf16[4096,1024]{1,0:T(8,128)(2,1)}) fusion(f32[4096,1024]{1,0:T(8,128)} %fusion.80, f32[1024]{0:T(1024)S(1)} %copy-done.40, bf16[4096,2048]{1,0:T(8,128)(2,1)} %all-gather.23.cloned.1.call-done, bf16[1024,2048]{1,0:T(8,128)(2,1)} %all-gather.21.cloned.1.call-done), kind=kOutput, calls=%fused_computation.68 | convolution fusion | flops 17276338176 | bytes 46145536 | tf_op jit(solution)/shard_map/rd,fd->rf/dot_general | solution.py:153
  1032.7 48.6 %add_add_fusion = f32[4096,2048]{1,0:T(8,128)} fusion(f32[4096,2048]{1,0:T(8,128)} %fusion.83, f32[4096,2048]{1,0:T(8,128)} %fusion.81, f32[4096,2048]{1,0:T(8,128)} %fusion.82, bf16[4096,1024]{1,0:T(8,128)(2,1)} %get-tuple-element.433, bf16[2048,1024]{1,0:T(8,128)(2,1)} %all-gather.19.cloned.1.call-done), kind=kOutput, calls=%fused_computation.57 | convolution fusion | flops 17205035008 | bytes 146800640 | tf_op jit(solution)/shard_map/rf,df->rd/dot_general | solution.py:225
  1099.7 34.0 %convolution_add_fusion = f32[4096,2048]{1,0:T(8,128)} fusion(f32[4096,2048]{1,0:T(8,128)} %fusion.79, bf16[1024,2048]{1,0:T(8,128)(2,1)S(1)} %copy-done.42, f32[4096,1024]{1,0:T(8,128)} %fusion.80, f32[1024]{0:T(1024)S(1)} %copy-done.40), kind=kOutput, calls=%fused_computation.60 | convolution fusion | flops 17230200832 | bytes 88084480 | tf_op jit(solution)/shard_map/dot_general | solution.py:130
  1179.8 24.2 %fusion.88 = f32[2048,1024]{1,0:T(8,128)} fusion(bf16[4096,2048]{1,0:T(8,128)(2,1)} %all-gather.9.cloned.1.call-done, bf16[4096,1024]{1,0:T(8,128)(2,1)} %get-tuple-element.433), kind=kOutput, calls=%fused_computation.144 | convolution fusion | flops 17179869184 | bytes 33554432 | tf_op jit(solution)/shard_map/rd,rf->df/dot_general | solution.py:220
  1204.1 28.9 %fusion.76 = f32[1024,2048]{1,0:T(8,128)} fusion(bf16[4096,2048]{1,0:T(8,128)(2,1)} %all-gather.23.cloned.1.call-done, f32[4096,1024]{1,0:T(8,128)} %fusion.80, f32[1024]{0:T(1024)S(1)} %copy-done.40), kind=kOutput, calls=%fused_computation.133 | convolution fusion | flops 17221812224 | bytes 41947136 | tf_op jit(solution)/shard_map/rf,rd->fd/dot_general | solution.py:149
  1247.1 158.1 %reduce-scatter.11.cloned.1.call-done = f32[512,2048]{1,0:T(8,128)} async-done(((f32[4096,2048]{1,0:T(8,128)}), f32[512,2048]{1,0:T(8,128)}) %reduce-scatter.11.cloned.1.call-update) | async-done | bytes 4194320 | tf_op jit(solution)/shard_map/reduce_scatter | solution.py:221
  1410.6 320.8 %reduce-scatter.9.cloned.1.call-done = f32[512,2048]{1,0:T(8,128)} async-done(((f32[4096,2048]{1,0:T(8,128)}), f32[512,2048]{1,0:T(8,128)}) %reduce-scatter.9.cloned.1.call-update) | async-done | bytes 4194320 | tf_op jit(solution)/shard_map/reduce_scatter | solution.py:128
  1739.0 38.3 %all-reduce = (f32[2048]{0:T(1024)}, f32[2048]{0:T(1024)}, f32[2048]{0:T(1024)S(1)}) all-reduce(f32[2048]{0:T(1024)S(1)} %get-tuple-element.359, f32[2048]{0:T(1024)S(1)} %get-tuple-element.361, f32[2048]{0:T(1024)S(1)} %get-tuple-element.458), channel_id=1, replica_groups=mesh['dp'=4,'tensor'=8] {'dp','tensor'}, use_global_device_ids=true, to_apply=%region_16.17 | all-reduce | flops 6144 | bytes 49152 | tf_op jit(solution)/shard_map/psum | solution.py:234
  1777.4 30.9 %reduce-scatter.17.cloned.1.call-done = f32[512,256]{1,0:T(8,128)} async-done(((f32[2048,256]{1,0:T(8,128)}), f32[512,256]{1,0:T(8,128)}) %reduce-scatter.17.cloned.1.call-update) | async-done | bytes 524304 | tf_op jit(solution)/shard_map/reduce_scatter | solution.py:256
  1808.3 38.7 %reduce-scatter.15.cloned.1.call-done = f32[512,256]{1,0:T(8,128)} async-done(((f32[2048,256]{1,0:T(8,128)}), f32[512,256]{1,0:T(8,128)}) %reduce-scatter.15.cloned.1.call-update) | async-done | bytes 524304 | tf_op jit(solution)/shard_map/reduce_scatter | solution.py:255
  1847.0 38.9 %reduce-scatter.13.cloned.1.call-done = f32[512,256]{1,0:T(8,128)} async-done(((f32[2048,256]{1,0:T(8,128)}), f32[512,256]{1,0:T(8,128)}) %reduce-scatter.13.cloned.1.call-update) | async-done | bytes 524304 | tf_op jit(solution)/shard_map/reduce_scatter | solution.py:254
  1885.9 89.9 %reduce-scatter.21.cloned.1.call-done = f32[512,1024]{1,0:T(8,128)} async-done(((f32[2048,1024]{1,0:T(8,128)}), f32[512,1024]{1,0:T(8,128)}) %reduce-scatter.21.cloned.1.call-update) | async-done | bytes 2097168 | tf_op jit(solution)/shard_map/reduce_scatter | solution.py:257
  1975.8 90.2 %reduce-scatter.23.cloned.1.call-done = f32[1024,512]{1,0:T(8,128)} async-done(((f32[1024,2048]{1,0:T(8,128)}), f32[1024,512]{1,0:T(8,128)}) %reduce-scatter.23.cloned.1.call-update) | async-done | bytes 2097168 | tf_op jit(solution)/shard_map/reduce_scatter | solution.py:259
  (468 shorter events, 662.9 us)
Async XLA Ops:
  7.2 32.0 %all-gather.15.cloned.1.call-start = ((), (), s32[]{:S(2)}) async-start(), calls=%async_computation.11 | async-start | bytes 1310720 | tf_op jit(solution)/shard_map/all_gather | solution.py:83
  7.9 184.6 %all-gather.9.cloned.1.call-start = ((), (), s32[]{:S(2)}) async-start(), calls=%async_computation.8 | async-start | bytes 18874368 | tf_op jit(solution)/shard_map/all_gather | solution.py:89
  17.0 205.6 %all-gather.13.cloned.1.call-start = ((), (), s32[]{:S(2)}) async-start(), calls=%async_computation.10 | async-start | bytes 1310720 | tf_op jit(solution)/shard_map/all_gather | solution.py:82
  17.7 235.1 %all-gather.11.cloned.1.call-start = ((), (), s32[]{:S(2)}) async-start(), calls=%async_computation.9 | async-start | bytes 1310720 | tf_op jit(solution)/shard_map/all_gather | solution.py:84
  18.3 260.7 %all-gather.17.cloned.1.call-start = ((), (), s32[]{:S(2)}) async-start(), calls=%async_computation.12 | async-start | bytes 1310720 | tf_op jit(solution)/shard_map/all_gather | solution.py:86
  18.9 409.6 %all-gather.23.cloned.1.call-start = ((), (), s32[]{:S(2)}) async-start(), calls=%async_computation.16 | async-start | bytes 18874368 | tf_op jit(solution)/shard_map/all_gather | solution.py:147
  19.4 953.1 %all-gather.19.cloned.1.call-start = ((), (), s32[]{:S(2)}) async-start(), calls=%async_computation.13 | async-start | bytes 5242880 | tf_op jit(solution)/shard_map/all_gather | solution.py:85
  20.2 975.8 %all-gather.21.cloned.1.call-start = ((), (), s32[]{:S(2)}) async-start(), calls=%async_computation.14 | async-start | bytes 5242880 | tf_op jit(solution)/shard_map/all_gather | solution.py:87
  20.9 1384.2 %reduce-scatter.11.cloned.1.call-start = ((), (), s32[]{:S(2)}) async-start(), calls=%async_computation.17 | async-start | bytes 37748736 | tf_op jit(solution)/shard_map/reduce_scatter | solution.py:221
  22.7 431.9 %copy-start.20 = (f32[1024,32]{0,1:T(8,128)}, f32[1024,32]{0,1:T(8,128)S(1)}, u32[]{:S(2)}) copy-start(f32[1024,32]{0,1:T(8,128)S(1)} %get-tuple-element.467) | copy-start | bytes 393220
  972.6 23.4 %copy-start.40 = (f32[1024]{0:T(1024)S(1)}, f32[1024]{0:T(1024)}, u32[]{:S(2)}) copy-start(f32[1024]{0:T(1024)} %convert_element_type.123) | copy-start | bytes 12292
  1081.3 650.1 %reduce-scatter.9.cloned.1.call-start = ((), (), s32[]{:S(2)}) async-start(), calls=%async_computation.15 | async-start | bytes 37748736 | tf_op jit(solution)/shard_map/reduce_scatter | solution.py:128
  1133.7 643.6 %reduce-scatter.19.cloned.1.call-start = ((), (), s32[]{:S(2)}) async-start(), calls=%async_computation.21 | async-start | bytes 2621440 | tf_op jit(solution)/shard_map/reduce_scatter | solution.py:258
  1146.4 661.9 %reduce-scatter.17.cloned.1.call-start = ((), (), s32[]{:S(2)}) async-start(), calls=%async_computation.20 | async-start | bytes 2621440 | tf_op jit(solution)/shard_map/reduce_scatter | solution.py:256
  1156.5 690.5 %reduce-scatter.15.cloned.1.call-start = ((), (), s32[]{:S(2)}) async-start(), calls=%async_computation.19 | async-start | bytes 2621440 | tf_op jit(solution)/shard_map/reduce_scatter | solution.py:255
  1169.6 716.3 %reduce-scatter.13.cloned.1.call-start = ((), (), s32[]{:S(2)}) async-start(), calls=%async_computation.18 | async-start | bytes 2621440 | tf_op jit(solution)/shard_map/reduce_scatter | solution.py:254
  1179.5 796.3 %reduce-scatter.21.cloned.1.call-start = ((), (), s32[]{:S(2)}) async-start(), calls=%async_computation.22 | async-start | bytes 10485760 | tf_op jit(solution)/shard_map/reduce_scatter | solution.py:257
  1204.1 862.0 %reduce-scatter.23.cloned.1.call-start = ((), (), s32[]{:S(2)}) async-start(), calls=%async_computation.23 | async-start | bytes 10485760 | tf_op jit(solution)/shard_map/reduce_scatter | solution.py:259
  1233.0 172.2 %copy-start.2 = (bf16[512,2048]{1,0:T(8,128)(2,1)S(1)}, bf16[512,2048]{1,0:T(8,128)(2,1)}, u32[]{:S(2)}) copy-start(bf16[512,2048]{1,0:T(8,128)(2,1)} %param.23) | copy-start | bytes 6291460
  1233.0 172.2 %copy-start.26 = (f32[2048]{0:T(1024)S(1)}, f32[2048]{0:T(1024)}, u32[]{:S(2)}) copy-start(f32[2048]{0:T(1024)} %copy-done.25) | copy-start | bytes 24580
  1233.0 172.1 %copy-start.29 = (f32[512]{0:T(512)S(1)}, f32[512]{0:T(512)}, u32[]{:S(2)}) copy-start(f32[512]{0:T(512)} %copy-done.28) | copy-start | bytes 6148
  1233.7 174.8 %copy-start.33 = (f32[512]{0:T(512)S(1)}, f32[512]{0:T(512)}, u32[]{:S(2)}) copy-start(f32[512]{0:T(512)} %copy-done.32) | copy-start | bytes 6148
  1233.7 174.8 %copy-start.31 = (f32[512]{0:T(512)S(1)}, f32[512]{0:T(512)}, u32[]{:S(2)}) copy-start(f32[512]{0:T(512)} %copy-done.30) | copy-start | bytes 6148
  1777.3 289.3 %copy-start.36 = (f32[2048]{0:T(1024)}, f32[2048]{0:T(1024)S(1)}, u32[]{:S(2)}) copy-start(f32[2048]{0:T(1024)S(1)} %get-tuple-element.893) | copy-start | bytes 24580
  (69 other events, 317.2 us)
Sparse Core Ops, SparseCore 0:
  9.9 29.3 all-gather.14
  41.4 151.0 all-gather.8
  194.4 24.8 all-gather.12
  221.0 26.6 all-gather.10
  249.3 26.4 all-gather.16
  277.3 151.1 all-gather.22
  430.3 50.9 all-gather.18
  483.1 52.5 all-gather.20
  1081.5 323.6 reduce-scatter.10
  1407.5 323.8 reduce-scatter.8
  1735.0 34.3 reduce-scatter.18
  1773.0 35.1 reduce-scatter.16
  1811.8 35.1 reduce-scatter.14
  1850.7 35.2 reduce-scatter.12
  1889.4 86.3 reduce-scatter.20
  1979.6 86.3 reduce-scatter.22
where the time goes:
time: 2090 us; the launch traced here: 2070 us
  waiting for transfers between devices  1090 us (52%)
  matrix products  473 us (23%)
  local copies, waits for them, and re-layouts  297 us (14%)
  other arithmetic  95.4 us (5%)
  loops' own time  51.5 us (2%)
  blocking collectives  49.4 us (2%)
    reduce_scatter x1, waiting for transfers between devices, per_device(): lax.psum_scatter(jnp.dot(attended_low, full_out, preferred_element_type=j...  321 us
    dynamic_update_slice x20, local copies, waits for them, and re-layouts, per_device(): lax.map(backward_sequence, jnp.arange(seq_count))  181 us
    reduce_scatter x1, waiting for transfers between devices, per_device(): lax.psum_scatter(jnp.einsum('rk,dk->rd', query_grad, back_query, preferre...  158 us
    all_gather x1, waiting for transfers between devices, per_device(): group_rows = lax.all_gather(normed, 'tensor', axis=0, tiled=True)  153 us
    all_gather x1, waiting for transfers between devices, per_device(): upstream = lax.all_gather(grad_out, 'tensor', axis=0, tiled=True)  149 us
    reduce_scatter x1, waiting for transfers between devices, per_device(): lax.psum_scatter(down_wgrad, 'dp', scatter_dimension=1, tiled=True)  90.2 us
    reduce_scatter x1, waiting for transfers between devices, per_device(): lax.psum_scatter(up_wgrad, 'dp', scatter_dimension=0, tiled=True)  89.9 us
    dot_general x4, matrix products, project(): jnp.dot(group_rows, weight_part, preferred_element_type=jnp.float32)  60.7 us
  transfers between devices with their start and end apart: 16, of which 10 were waited for; matrix products, arithmetic and copies ran while one was open for 37% of the time, Pallas kernels for 0%

commit v1 on v0

v1 whole, which is shorter than its diff:
```python
import functools

import jax
import jax.numpy as jnp
from jax import lax
from jax.experimental import pallas as pl
from jax.experimental.pallas import tpu as pltpu
from jax.sharding import PartitionSpec as P

HEAD_DIM = 64
ROT = 32
SPAN = 256
EPS = 1e-05
F32 = jnp.float32
BF16 = jnp.bfloat16
VMEM_BYTES = 60 * 2**20


def nn(a, b):
    return jnp.dot(a, b, preferred_element_type=F32)


def nt(a, b):
    return lax.dot_general(a, b, (((1,), (1,)), ((), ())), preferred_element_type=F32)


def tn(a, b):
    return lax.dot_general(a, b, (((0,), (0,)), ((), ())), preferred_element_type=F32)


def params(semantics):
    return pltpu.CompilerParams(dimension_semantics=semantics, vmem_limit_bytes=VMEM_BYTES)


def cost(flops, bytes_accessed, transcendentals=0):
    return pl.CostEstimate(
        flops=int(flops), bytes_accessed=int(bytes_accessed), transcendentals=int(transcendentals)
    )


def once(shape, index_map):
    return pl.BlockSpec(shape, index_map, pipeline_mode=pl.Buffered(1))


def rotary_tables(length):
    halves = ROT // 2
    exponent = jnp.arange(halves, dtype=F32) * (2.0 / ROT)
    frequency = jnp.power(10000.0, -exponent)
    angles = jnp.arange(length, dtype=F32)[:, None] * frequency[None, :]
    cos, sin = jnp.cos(angles), jnp.sin(angles)
    zero = jnp.zeros((length, halves), F32)
    rest = HEAD_DIM - ROT
    head = lambda a, b, fill: jnp.concatenate([a, b, jnp.full((length, rest), fill, F32)], axis=1)
    return tuple(
        jnp.concatenate([t, t], axis=1)
        for t in (head(cos, cos, 1.0), head(-sin, zero, 0.0), head(zero, sin, 0.0))
    )


def rotated(values, cos, low, high):
    halves = ROT // 2
    pieces = []
    for start in range(0, values.shape[1], 128):
        u = values[:, start : start + 128]
        pieces.append(
            u * cos + pltpu.roll(u, 128 - halves, 1) * low + pltpu.roll(u, halves, 1) * high
        )
    return pieces[0] if len(pieces) == 1 else jnp.concatenate(pieces, axis=1)


GELU_A = 0.7978845608028654
GELU_B = 0.044715


def gelu(v):
    return 0.5 * v * (1.0 + jnp.tanh(GELU_A * (v + GELU_B * (v * v * v))))


def gelu_slope(v):
    square = v * v
    t = jnp.tanh(GELU_A * (v + GELU_B * (v * square)))
    return 0.5 * (1.0 + t) + 0.5 * v * (1.0 - t * t) * (GELU_A * (1.0 + 3.0 * GELU_B * square))


def project_kernel(width, x, w, bias, cos, low, high, q, k, v, active, hidden):
    rows = x[...]
    tables = (cos[...], low[...], high[...])
    q[...] = (
        rotated(nn(rows, w[:, :width]) + bias[:, :width], *tables).astype(BF16)
        * jnp.asarray(HEAD_DIM**-0.5, BF16)
    )
    k[...] = rotated(
        nn(rows, w[:, width : 2 * width]) + bias[:, width : 2 * width], *tables
    ).astype(BF16)
    v[...] = (nn(rows, w[:, 2 * width : 3 * width]) + bias[:, 2 * width : 3 * width]).astype(BF16)
    units = hidden.shape[1]
    step = min(256, units)
    for start in range(0, units, step):
        at = slice(3 * width + start, 3 * width + start + step)
        h = nn(rows, w[:, at]) + bias[:, at]
        hidden[:, start : start + step] = h
        active[:, start : start + step] = gelu(h).astype(BF16)


def project(x, w, bias, tables, width, units, length, tile=512):
    rows, depth = x.shape
    per = length // tile
    row = lambda n: pl.BlockSpec((tile, n), lambda i: (i, 0))
    table = pl.BlockSpec((tile, 128), lambda i: (i % per, 0))
    total = 3 * width + units
    return pl.pallas_call(
        functools.partial(project_kernel, width),
        grid=(rows // tile,),
        in_specs=[
            row(depth),
            once((depth, total), lambda i: (0, 0)),
            once((1, total), lambda i: (0, 0)),
            table,
            table,
            table,
        ],
        out_specs=[row(width), row(width), row(width), row(units), row(units)],
        out_shape=[
            jax.ShapeDtypeStruct((rows, width), BF16),
            jax.ShapeDtypeStruct((rows, width), BF16),
            jax.ShapeDtypeStruct((rows, width), BF16),
            jax.ShapeDtypeStruct((rows, units), BF16),
            jax.ShapeDtypeStruct((rows, units), F32),
        ],
        compiler_params=params(("arbitrary",)),
        cost_estimate=cost(2 * rows * depth * total, 2 * depth * (rows + total) + rows * units * 6),
        name="project",
    )(x, w, bias, *tables)


def mix_kernel(attended, active, w, out):
    parts, inner, columns = w.shape
    width = attended.shape[1]
    for d in range(parts):
        out[:, d * columns : (d + 1) * columns] = (
            nn(attended[...], w[d, :width, :]) + nn(active[...], w[d, width:, :])
        ).astype(out.dtype)


def mix(attended, active, w, tile=512):
    rows, width = attended.shape
    units = active.shape[1]
    parts, inner, columns = w.shape
    row = lambda n: pl.BlockSpec((tile, n), lambda i: (i, 0))
    return pl.pallas_call(
        mix_kernel,
        grid=(rows // tile,),
        in_specs=[row(width), row(units), once(w.shape, lambda i: (0, 0, 0))],
        out_specs=row(parts * columns),
        out_shape=jax.ShapeDtypeStruct((rows, parts * columns), BF16),
        compiler_params=params(("arbitrary",)),
        cost_estimate=cost(2 * rows * inner * parts * columns, 2 * inner * (rows + parts * columns)),
        name="mix",
    )(attended, active, w)


def unmix_kernel(g, w, hidden, attended_grad, hidden_grad, sums):
    parts, inner, columns = w.shape
    width = attended_grad.shape[1]
    units = hidden.shape[1]

    @pl.when(pl.program_id(0) == 0)
    def _():
        sums[...] = jnp.zeros_like(sums)

    def back(lo, hi):
        total = nt(g[:, :columns], w[0, lo:hi, :])
        for d in range(1, parts):
            total = total + nt(g[:, d * columns : (d + 1) * columns], w[d, lo:hi, :])
        return total

    attended_grad[...] = back(0, width).astype(BF16)
    step = min(256, units)
    for start in range(0, units, step):
        at = slice(start, start + step)
        low = (back(width + start, width + start + step) * gelu_slope(hidden[:, at])).astype(BF16)
        hidden_grad[:, at] = low
        sums[:, at] += jnp.sum(low.astype(F32), axis=0, keepdims=True)


def unmix(g, w, hidden, width, tile=512):
    rows, depth = g.shape
    units = hidden.shape[1]
    parts, inner, columns = w.shape
    row = lambda n: pl.BlockSpec((tile, n), lambda i: (i, 0))
    return pl.pallas_call(
        unmix_kernel,
        grid=(rows // tile,),
        in_specs=[row(depth), once(w.shape, lambda i: (0, 0, 0)), row(units)],
        out_specs=[row(width), row(units), pl.BlockSpec((1, units), lambda i: (0, 0))],
        out_shape=[
            jax.ShapeDtypeStruct((rows, width), BF16),
            jax.ShapeDtypeStruct((rows, units), BF16),
            jax.ShapeDtypeStruct((1, units), F32),
        ],
        compiler_params=params(("arbitrary",)),
        cost_estimate=cost(2 * rows * inner * depth, 2 * depth * (rows + inner) + rows * units * 6),
        name="unmix",
    )(g, w, hidden)


def unproject_kernel(qkv_grad, hidden_grad, w, out):
    three = qkv_grad.shape[1]
    depth = w.shape[0]
    step = min(512, depth)
    for start in range(0, depth, step):
        out[:, start : start + step] = (
            nt(qkv_grad[...], w[start : start + step, :three])
            + nt(hidden_grad[...], w[start : start + step, three:])
        ).astype(out.dtype)


def unproject(qkv_grad, hidden_grad, w, tile=512):
    rows, three = qkv_grad.shape
    units = hidden_grad.shape[1]
    depth, total = w.shape
    row = lambda n: pl.BlockSpec((tile, n), lambda i: (i, 0))
    return pl.pallas_call(
        unproject_kernel,
        grid=(rows // tile,),
        in_specs=[row(three), row(units), once(w.shape, lambda i: (0, 0))],
        out_specs=row(depth),
        out_shape=jax.ShapeDtypeStruct((rows, depth), BF16),
        compiler_params=params(("arbitrary",)),
        cost_estimate=cost(2 * rows * total * depth, 2 * depth * (rows + total)),
        name="unproject",
    )(qkv_grad, hidden_grad, w)


def outer_kernel(a, b, out):
    out[...] = tn(a[...], b[...]).astype(out.dtype)


def outer_rows(x, d, tile=512):
    rows, depth = x.shape
    n = d.shape[1]
    tile = min(tile, depth)
    return pl.pallas_call(
        outer_kernel,
        grid=(depth // tile,),
        in_specs=[pl.BlockSpec((rows, tile), lambda i: (0, i)), once((rows, n), lambda i: (0, 0))],
        out_specs=pl.BlockSpec((tile, n), lambda i: (i, 0)),
        out_shape=jax.ShapeDtypeStruct((depth, n), BF16),
        compiler_params=params(("arbitrary",)),
        cost_estimate=cost(2 * rows * depth * n, 2 * (rows * (depth + n) + depth * n)),
        name="outer_rows",
    )(x, d)


def outer_columns_kernel(a, b, g, out):
    width = a.shape[1]
    out[0, :width, :] = tn(a[...], g[...]).astype(out.dtype)
    out[0, width:, :] = tn(b[...], g[...]).astype(out.dtype)


def outer_columns(a, b, g, parts):
    rows, depth = g.shape
    width, units = a.shape[1], b.shape[1]
    tile = depth // parts
    return pl.pallas_call(
        outer_columns_kernel,
        grid=(parts,),
        in_specs=[
            once((rows, width), lambda i: (0, 0)),
            once((rows, units), lambda i: (0, 0)),
            pl.BlockSpec((rows, tile), lambda i: (0, i)),
        ],
        out_specs=pl.BlockSpec((1, width + units, tile), lambda i: (i, 0, 0)),
        out_shape=jax.ShapeDtypeStruct((parts, width + units, tile), BF16),
        compiler_params=params(("arbitrary",)),
        cost_estimate=cost(
            2 * rows * depth * (width + units), 2 * (rows * (depth + width + units) + depth * (width + units))
        ),
        name="outer_columns",
    )(a, b, g)


def head_lanes(width, head):
    return lax.broadcasted_iota(jnp.int32, (1, width), 1) // HEAD_DIM == head


def attend_kernel(q, k, v, column_ids, row_ids, out, log_sums):
    length, width = q.shape
    heads = width // HEAD_DIM
    tile = min(SPAN, length)
    lanes = lax.broadcasted_iota(jnp.int32, (1, 128), 1)
    for begin in range(0, length, tile):
        end = min(length, begin + tile + SPAN)
        q_ids = column_ids[begin : begin + tile, :]
        blocked = row_ids[:, begin:end] > q_ids
        rows = q[begin : begin + tile, :]

        def one_head(head, carry):
            total, sums = carry
            mine = head_lanes(width, head)
            scores = nt(jnp.where(mine, rows, jnp.zeros_like(rows)), k[:end, :])
            tail = jnp.where(blocked, -1e9, scores[:, begin:])
            scores = jnp.concatenate([scores[:, :begin], tail], axis=1) if begin else tail
            highest = jnp.max(scores, axis=1, keepdims=True)
            powers = jnp.exp(scores - highest)
            amount = jnp.sum(powers, axis=1, keepdims=True)
            low = (powers * (1.0 / amount)).astype(BF16)
            total = jnp.where(mine, nn(low, v[:end, :]), total)
            sums = jnp.where(lanes == head, highest + jnp.log(amount), sums)
            return total, sums

        total, sums = jnp.zeros((tile, width), F32), jnp.zeros((tile, 128), F32)
        for head in range(heads):
            total, sums = one_head(head, (total, sums))
        out[begin : begin + tile, :] = total.astype(BF16)
        log_sums[:, begin : begin + tile] = sums.T[:8, :]


def attend(q, k, v, column_ids, row_ids):
    rows, width = q.shape
    seqs, _, length = row_ids.shape
    heads = width // HEAD_DIM
    seq = pl.BlockSpec((length, width), lambda s: (s, 0))
    return pl.pallas_call(
        attend_kernel,
        grid=(seqs,),
        in_specs=[
            seq,
            seq,
            seq,
            pl.BlockSpec((length, 1), lambda s: (s, 0)),
            pl.BlockSpec((None, 1, length), lambda s: (s, 0, 0)),
        ],
        out_specs=[seq, pl.BlockSpec((8, length), lambda s: (0, s))],
        out_shape=[
            jax.ShapeDtypeStruct((rows, width), BF16),
            jax.ShapeDtypeStruct((8, rows), F32),
        ],
        compiler_params=params(("arbitrary",)),
        cost_estimate=cost(
            8 * seqs * heads * length * length * 256 * 0.8, 8 * rows * width, seqs * heads * length**2
        ),
        name="attend",
    )(q, k, v, column_ids, row_ids)


def unattend_kernel(
    q, k, v, g, log_sums, column_ids, row_ids, cos, low, high, out, sums, key_total, value_total
):
    length, width = q.shape
    heads = width // HEAD_DIM
    tile = min(SPAN, length)
    tables = (cos[...], -low[...], -high[...])

    @pl.when(pl.program_id(0) == 0)
    def _():
        sums[...] = jnp.zeros_like(sums)

    key_total[...] = jnp.zeros_like(key_total)
    value_total[...] = jnp.zeros_like(value_total)
    for begin in range(0, length, tile):
        end = min(length, begin + tile + SPAN)
        at = slice(begin, begin + tile)
        blocked = column_ids[begin:end, :] > row_ids[:, at]
        q_rows, g_rows = q[at, :], g[at, :]
        query_total = jnp.zeros((tile, width), F32)
        for head in range(heads):
            mine = head_lanes(width, head)
            q_head = jnp.where(mine, q_rows, jnp.zeros_like(q_rows))
            g_head = jnp.where(mine, g_rows, jnp.zeros_like(g_rows))
            scores = nt(k[:end, :], q_head)
            tail = jnp.where(blocked, -1e9, scores[begin:, :])
            scores = jnp.concatenate([scores[:begin, :], tail], axis=0) if begin else tail
            probs = jnp.exp(scores - log_sums[head : head + 1, at])
            value_total[:end, :] += nn(probs.astype(BF16), g_head)
            prob_grad = nt(v[:end, :], g_head)
            inner = jnp.sum(prob_grad * probs, axis=0, keepdims=True)
            score_grad = (probs * (prob_grad - inner)).astype(BF16)
            key_total[:end, :] += nn(score_grad, q_head)
            query_total = jnp.where(mine, tn(score_grad, k[:end, :]), query_total)
        turned = rotated(query_total * HEAD_DIM**-0.5, *(t[at, :] for t in tables)).astype(BF16)
        out[at, :width] = turned
        sums[:, :width] += jnp.sum(turned.astype(F32), axis=0, keepdims=True)
    turned = rotated(key_total[...], *tables).astype(BF16)
    out[:, width : 2 * width] = turned
    sums[:, width : 2 * width] += jnp.sum(turned.astype(F32), axis=0, keepdims=True)
    turned = value_total[...].astype(BF16)
    out[:, 2 * width :] = turned
    sums[:, 2 * width :] += jnp.sum(turned.astype(F32), axis=0, keepdims=True)


def unattend(q, k, v, g, log_sums, column_ids, row_ids, tables):
    rows, width = q.shape
    seqs, _, length = row_ids.shape
    heads = width // HEAD_DIM
    seq = pl.BlockSpec((length, width), lambda s: (s, 0))
    table = once((length, 128), lambda s: (0, 0))
    return pl.pallas_call(
        unattend_kernel,
        grid=(seqs,),
        in_specs=[
            seq,
            seq,
            seq,
            seq,
            pl.BlockSpec((8, length), lambda s: (0, s)),
            pl.BlockSpec((length, 1), lambda s: (s, 0)),
            pl.BlockSpec((None, 1, length), lambda s: (s, 0, 0)),
            table,
            table,
            table,
        ],
        out_specs=[
            pl.BlockSpec((length, 3 * width), lambda s: (s, 0)),
            pl.BlockSpec((1, 3 * width), lambda s: (0, 0)),
        ],
        out_shape=[
            jax.ShapeDtypeStruct((rows, 3 * width), BF16),
            jax.ShapeDtypeStruct((1, 3 * width), F32),
        ],
        scratch_shapes=[pltpu.VMEM((length, width), F32), pltpu.VMEM((length, width), F32)],
        compiler_params=params(("arbitrary",)),
        cost_estimate=cost(
            20 * seqs * heads * length * length * 256 * 0.8,
            14 * rows * width,
            seqs * heads * length**2,
        ),
        name="unattend",
    )(q, k, v, g, log_sums, column_ids, row_ids, *tables)


def per_device(
    inputs,
    block_ids,
    norm_gain,
    norm_bias,
    query_weight,
    query_bias,
    key_weight,
    key_bias,
    value_weight,
    value_bias,
    out_weight,
    out_bias,
    up_weight,
    up_bias,
    down_weight,
    down_bias,
    grad_out,
):
    seqs, length = block_ids.shape
    width = query_weight.shape[1]
    units = up_weight.shape[1]
    groups = lax.axis_size("dp")
    gain, shift = norm_gain.astype(F32), norm_bias.astype(F32)

    x = inputs.astype(F32)
    center = jnp.mean(x, axis=-1, keepdims=True)
    centered = x - center
    scale = lax.rsqrt(jnp.mean(centered * centered, axis=-1, keepdims=True) + EPS)
    normed = (centered * scale * gain + shift).astype(BF16)

    first = jnp.concatenate([query_weight, key_weight, value_weight, up_weight], axis=1)
    second = jnp.concatenate([out_weight, down_weight], axis=0)
    first_full = lax.all_gather(first, "dp", axis=0, tiled=True)
    rows = lax.all_gather(normed, "tensor", axis=0, tiled=True)
    second_full = lax.all_gather(second, "dp", axis=0)
    upstream = lax.all_gather(grad_out, "tensor", axis=0, tiled=True)
    bias = jnp.concatenate([query_bias, key_bias, value_bias, up_bias]).astype(F32)[None, :]
    tables = rotary_tables(length)
    column_ids = block_ids.reshape(seqs * length, 1)
    row_ids = block_ids.reshape(seqs, 1, length)

    q, k, v, active, hidden = project(rows, first_full, bias, tables, width, units, length)
    attended, log_sums = attend(q, k, v, column_ids, row_ids)
    partial = mix(attended, active, second_full)
    branch = lax.psum_scatter(partial, "tensor", scatter_dimension=0, tiled=True)
    output = (
        x + branch.astype(F32) + out_bias.astype(F32) + down_bias.astype(F32)
    ).astype(BF16)

    attended_grad, hidden_grad, up_sum = unmix(upstream, second_full, hidden, width)
    second_grad = outer_columns(attended, active, upstream, groups)
    qkv_grad, qkv_sum = unattend(
        q, k, v, attended_grad, log_sums, column_ids, row_ids, tables
    )
    normed_part = unproject(qkv_grad, hidden_grad, first_full)
    normed_grad = lax.psum_scatter(
        normed_part, "tensor", scatter_dimension=0, tiled=True
    ).astype(F32)
    up_grad = outer_rows(rows, hidden_grad)
    first_grad = outer_rows(rows, qkv_grad)

    second_grad = lax.psum_scatter(second_grad, "dp", scatter_dimension=0).astype(F32)
    up_grad = lax.psum_scatter(up_grad, "dp", scatter_dimension=0, tiled=True).astype(F32)
    first_grad = lax.psum_scatter(first_grad, "dp", scatter_dimension=0, tiled=True).astype(F32)

    hat = centered * scale
    e = normed_grad * gain
    input_grad = (
        grad_out.astype(F32)
        + (
            e
            - jnp.mean(e, axis=-1, keepdims=True)
            - hat * jnp.mean(e * hat, axis=-1, keepdims=True)
        )
        * scale
    ).astype(BF16)
    gain_grad, shift_grad, outer_bias_grad = lax.psum(
        (
            jnp.sum(normed_grad * hat, axis=0),
            jnp.sum(normed_grad, axis=0),
            jnp.sum(grad_out, axis=0, dtype=F32),
        ),
        ("dp", "tensor"),
    )
    qkv_sum, up_sum = lax.psum((qkv_sum[0], up_sum[0]), "dp")
    return (
        output,
        input_grad,
        gain_grad,
        shift_grad,
        first_grad[:, :width],
        qkv_sum[:width],
        first_grad[:, width : 2 * width],
        qkv_sum[width : 2 * width],
        first_grad[:, 2 * width :],
        qkv_sum[2 * width :],
        second_grad[:width],
        outer_bias_grad,
        up_grad,
        up_sum,
        second_grad[width:],
        outer_bias_grad,
    )


def solution(mesh):
    tokens = P(("dp", "tensor"), None)
    down = P("dp", "tensor")
    across = P("tensor", "dp")
    part = P("tensor")
    return jax.shard_map(
        per_device,
        mesh=mesh,
        in_specs=(
            tokens,
            P("dp", None),
            P(),
            P(),
            down,
            part,
            down,
            part,
            down,
            part,
            across,
            P(),
            down,
            part,
            across,
            P(),
            tokens,
        ),
        out_specs=(
            tokens,
            tokens,
            P(),
            P(),
            down,
            part,
            down,
            part,
            down,
            part,
            across,
            P(),
            down,
            part,
            across,
            P(),
        ),
        check_vma=False,
    )
```

time: 2090 us -> 1140 us (0.55)
  matrix products: 473 us -> 0 us
  waiting for transfers between devices: 1090 us -> 727 us
  Pallas kernels: 0 us -> 303 us
  local copies, waits for them, and re-layouts: 297 us -> 15.3 us
  other arithmetic: 95.4 us -> 24.9 us
  loops' own time: 51.5 us -> 0 us
    dot_general x74 -> x0, matrix products: 473 us -> none  [the longest x4 60.7 us: project(): jnp.dot(group_rows, weight_part, preferred_element_type=jnp.float32)]
    reduce_scatter x8 -> x4, waiting for transfers between devices: 768 us -> 332 us  [the longest x1 167 us: per_device(): lax.psum_scatter(normed_part, 'tensor', scatter_dimension=0, tiled=True)]
    pallas_call x0 -> x9, Pallas kernels: none -> 303 us  [the longest x1 62.1 us: unattend(): pl.pallas_call(unattend_kernel, grid=(seqs,), in_specs=[seq, seq, seq, se...]
    dynamic_update_slice x20 -> x0, local copies, waits for them, and re-layouts: 181 us -> none  [per_device(): lax.map(backward_sequence, jnp.arange(seq_count))]
    another operation x6 -> x0, loops' own time: 51.5 us -> none  [the longest x4 21.5 us: backward_sequence(): lax.scan(backward_block, (zero_total, zero_total), jnp.arange(per_sequence))]
    all_gather x7 -> x3, waiting for transfers between devices: 170 us -> 218 us  [the longest x1 153 us: per_device(): rows = lax.all_gather(normed, 'tensor', axis=0, tiled=True)]
    while x80 -> x0, local copies, waits for them, and re-layouts: 34.9 us -> none  [the longest x3 10.9 us: per_device(): lax.map(forward_block, jnp.arange(seq_count * per_sequence))]
    reduce_sum x16 -> x4, other arithmetic: 43.8 us -> 11.6 us  [the longest x1 7.08 us: per_device(): jnp.sum(grad_out, axis=0, dtype=F32)]
  transfers between devices with their start and end apart: 16 -> 9, of which waited for: 10 -> 6; matrix products, arithmetic and copies ran while one was open for 37% -> 2% of each run, Pallas kernels for 0% -> 16%
where the time goes in v1:
time: 1140 us; the launch traced here: 1130 us
  waiting for transfers between devices  727 us (64%)
  Pallas kernels  303 us (27%)
  blocking collectives  49 us (4%)
  other arithmetic  24.9 us (2%)
  local copies, waits for them, and re-layouts  15.3 us (1%)
  between operations  14.4 us (1%)
    reduce_scatter x1, waiting for transfers between devices, per_device(): lax.psum_scatter(normed_part, 'tensor', scatter_dimension=0, tiled=True)  167 us
    reduce_scatter x1, waiting for transfers between devices, per_device(): lax.psum_scatter(partial, 'tensor', scatter_dimension=0, tiled=True)  166 us
    all_gather x1, waiting for transfers between devices, per_device(): rows = lax.all_gather(normed, 'tensor', axis=0, tiled=True)  153 us
    all_gather x1, waiting for transfers between devices, per_device(): upstream = lax.all_gather(grad_out, 'tensor', axis=0, tiled=True)  147 us
    all_gather x1, waiting for transfers between devices, per_device(): first_full = lax.all_gather(first, 'dp', axis=0, tiled=True)  65.2 us
    pallas_call x1, Pallas kernels, unattend(): pl.pallas_call(unattend_kernel, grid=(seqs,), in_specs=[seq, seq, seq, se...  62.1 us
    pallas_call x2, Pallas kernels, outer_rows(): pl.pallas_call(outer_kernel, grid=(depth // tile,), in_specs=[pl.BlockSpe...  42.7 us
    pallas_call x1, Pallas kernels, project(): pl.pallas_call(functools.partial(project_kernel, width), grid=(rows // ti...  41 us
  transfers between devices with their start and end apart: 9, of which 6 were waited for; matrix products, arithmetic and copies ran while one was open for 2% of the time, Pallas kernels for 16%

profile of v1, /device:TPU:0, one launch (start us, length us, event | category | flops | bytes accessed | tf_op | source)
XLA Modules:
  0.0 1133.1 jit_solution(9475057469447925002)
XLA Ops:
  7.3 2.9 pad_maximum_fusion
  12.0 2.2 fusion.8
  22.5 2.0 copy.38
  26.9 65.2 %all-gather.8.cloned.1.call-done.w = bf16[2048,1792]{1,0:T(8,128)(2,1)} async-done(((bf16[512,1792]{1,0:T(8,128)(2,1)}), bf16[2048,1792]{1,0:T(8,128)(2,1)}) %all-gather.8.cloned.1.call-update) | async-done | bytes 7340048 | tf_op jit(solution)/shard_map/all_gather | solution.py:465
  92.1 153.3 %all-gather.6.cloned.1.call-done.x.a = bf16[4096,2048]{1,0:T(8,128)(2,1)} async-done(((bf16[512,2048]{1,0:T(8,128)(2,1)}), bf16[4096,2048]{1,0:T(8,128)(2,1)}) %all-gather.6.cloned.1.call-update) | async-done | bytes 16777232 | tf_op jit(solution)/shard_map/all_gather | solution.py:466
  245.4 41.0 %project.1 = (bf16[4096,256]{1,0:T(8,128)(2,1)}, bf16[4096,256]{1,0:T(8,128)(2,1)}, bf16[4096,256]{1,0:T(8,128)(2,1)}, bf16[4096,1024]{1,0:T(8,128)(2,1)}, f32[4096,1024]{1,0:T(8,128)}) custom-call(bf16[4096,2048]{1,0:T(8,128)(2,1)} %all-gather.6.cloned.1.call-done.x.a, bf16[2048,1792]{1,0:T(8,128)(2,1)} %all-gather.8.cloned.1.call-done.w, ...), custom_call_target="tpu_custom_call" | custom-call | flops 30064771072 | bytes 49283072 | tf_op jit(solution)/shard_map/project/pallas_call | solution.py:111
  286.4 26.4 %attend.1 = (bf16[4096,256]{1,0:T(8,128)(2,1)}, f32[8,4096]{1,0:T(8,128)}) custom-call(bf16[4096,256]{1,0:T(8,128)(2,1)} %get-tuple-element.28.q, bf16[4096,256]{1,0:T(8,128)(2,1)} %get-tuple-element.29.k, bf16[4096,256]{1,0:T(8,128)(2,1)} %get-tuple-element.30.v, s32[4096,1]{1,0:T(8,128)} %bitcast.11, s32[4,1,1024]{2,1,0:T(1,128)} %reshape.127.row_ids), custom_call_target="tpu_custom_call" | custom-call | flops 27487791104 | bytes 8388608 | tf_op jit(solution)/shard_map/attend/pallas_call | solution.py:324
  312.8 147.3 %all-gather.10.cloned.1.call-done.g = bf16[4096,2048]{1,0:T(8,128)(2,1)} async-done(((bf16[512,2048]{1,0:T(8,128)(2,1)}), bf16[4096,2048]{1,0:T(8,128)(2,1)}) %all-gather.10.cloned.1.call-update) | async-done | bytes 16777232 | tf_op jit(solution)/shard_map/all_gather | solution.py:468
  460.1 36.7 %unmix.1 = (bf16[4096,256]{1,0:T(8,128)(2,1)}, bf16[4096,1024]{1,0:T(8,128)(2,1)}, f32[1,1024]{1,0:T(1,128)}) custom-call(bf16[4096,2048]{1,0:T(8,128)(2,1)} %all-gather.10.cloned.1.call-done.g, bf16[4,1280,512]{2,1,0:T(8,128)(2,1)} %bitcast.16, f32[4096,1024]{1,0:T(8,128)} %get-tuple-element.33.hidden), custom_call_target="tpu_custom_call" | custom-call | flops 21474836480 | bytes 47185920 | tf_op jit(solution)/shard_map/unmix/pallas_call | solution.py:191
  496.8 62.1 %unattend.1 = (bf16[4096,768]{1,0:T(8,128)(2,1)}, f32[1,768]{1,0:T(1,128)}) custom-call(bf16[4096,256]{1,0:T(8,128)(2,1)} %get-tuple-element.28.q, bf16[4096,256]{1,0:T(8,128)(2,1)} %get-tuple-element.29.k, bf16[4096,256]{1,0:T(8,128)(2,1)} %get-tuple-element.30.v, bf16[4096,256]{1,0:T(8,128)(2,1)} %get-tuple-element.34.g, ...), custom_call_target="tpu_custom_call" | custom-call | flops 68719476736 | bytes 14680064 | tf_op jit(solution)/shard_map/unattend/pallas_call | solution.py:398
  558.9 18.9 %outer_rows.2 = bf16[2048,768]{1,0:T(8,128)(2,1)} custom-call(bf16[4096,2048]{1,0:T(8,128)(2,1)} %all-gather.6.cloned.1.call-done.x.a, bf16[4096,768]{1,0:T(8,128)(2,1)} %get-tuple-element.36.qkv_grad.b), custom_call_target="tpu_custom_call" | custom-call | flops 12884901888 | bytes 26214400 | tf_op jit(solution)/shard_map/outer_rows/pallas_call | solution.py:243
  577.8 23.8 %outer_rows.3 = bf16[2048,1024]{1,0:T(8,128)(2,1)} custom-call(bf16[4096,2048]{1,0:T(8,128)(2,1)} %all-gather.6.cloned.1.call-done.x.a, bf16[4096,1024]{1,0:T(8,128)(2,1)} %get-tuple-element.37.hidden_grad.b), custom_call_target="tpu_custom_call" | custom-call | flops 17179869184 | bytes 29360128 | tf_op jit(solution)/shard_map/outer_rows/pallas_call | solution.py:243
  601.7 28.9 %outer_columns.1 = bf16[4,1280,512]{2,1,0:T(8,128)(2,1)} custom-call(bf16[4096,256]{1,0:T(8,128)(2,1)} %get-tuple-element.31.attended.a, bf16[4096,1024]{1,0:T(8,128)(2,1)} %get-tuple-element.32.active.b, bf16[4096,2048]{1,0:T(8,128)(2,1)} %all-gather.10.cloned.1.call-done.g), custom_call_target="tpu_custom_call" | custom-call | flops 21474836480 | bytes 32505856 | tf_op jit(solution)/shard_map/outer_columns/pallas_call | solution.py:265
  630.6 37.5 %unproject.1 = bf16[4096,2048]{1,0:T(8,128)(2,1)} custom-call(bf16[4096,768]{1,0:T(8,128)(2,1)} %get-tuple-element.36.qkv_grad.b, bf16[4096,1024]{1,0:T(8,128)(2,1)} %get-tuple-element.37.hidden_grad.b, bf16[2048,1792]{1,0:T(8,128)(2,1)} %all-gather.8.cloned.1.call-done.w), custom_call_target="tpu_custom_call" | custom-call | flops 30064771072 | bytes 24117248 | tf_op jit(solution)/shard_map/unproject/pallas_call | solution.py:223
  668.2 27.4 %mix.1 = bf16[4096,2048]{1,0:T(8,128)(2,1)} custom-call(bf16[4096,256]{1,0:T(8,128)(2,1)} %get-tuple-element.31.attended.a, bf16[4096,1024]{1,0:T(8,128)(2,1)} %get-tuple-element.32.active.b, bf16[4,1280,512]{2,1,0:T(8,128)(2,1)} %bitcast.17), custom_call_target="tpu_custom_call" | custom-call | flops 21474836480 | bytes 15728640 | tf_op jit(solution)/shard_map/mix/pallas_call | solution.py:150
  696.3 11.0 all-reduce.2
  707.9 2.3 fusion.21
  710.2 2.8 convert_element_type.68
  713.0 27.7 %reduce-scatter.16.cloned.1.call-done = bf16[1,1280,512]{2,1,0:T(8,128)(2,1)} async-done(((bf16[4,1280,512]{2,1,0:T(8,128)(2,1)}), bf16[1,1280,512]{2,1,0:T(8,128)(2,1)}) %reduce-scatter.16.cloned.1.call-update) | async-done | bytes 1310736
  744.8 166.7 %reduce-scatter.10.cloned.1.call-done = bf16[512,2048]{1,0:T(8,128)(2,1)} async-done(((bf16[4096,2048]{1,0:T(8,128)(2,1)}), bf16[512,2048]{1,0:T(8,128)(2,1)}) %reduce-scatter.10.cloned.1.call-update) | async-done | bytes 2097168 | tf_op jit(solution)/shard_map/reduce_scatter | solution.py:488
  911.5 3.5 fusion.17
  915.0 165.6 %reduce-scatter.8.cloned.1.call-done = bf16[512,2048]{1,0:T(8,128)(2,1)} async-done(((bf16[4096,2048]{1,0:T(8,128)(2,1)}), bf16[512,2048]{1,0:T(8,128)(2,1)}) %reduce-scatter.8.cloned.1.call-update) | async-done | bytes 2097168 | tf_op jit(solution)/shard_map/reduce_scatter | solution.py:477
  1080.6 7.1 convert_reduce_fusion.2
  1087.7 38.0 %all-reduce.1 = (f32[2048]{0:T(1024)}, f32[2048]{0:T(1024)}, f32[2048]{0:T(1024)S(1)}) all-reduce(f32[2048]{0:T(1024)S(1)} %get-tuple-element.40, f32[2048]{0:T(1024)S(1)} %get-tuple-element.43, f32[2048]{0:T(1024)S(1)} %get-tuple-element.49), channel_id=1, replica_groups=mesh['dp'=4,'tensor'=8] {'dp','tensor'}, use_global_device_ids=true, to_apply=%region_7.0 | all-reduce | flops 6144 | bytes 49152 | tf_op jit(solution)/shard_map/psum | solution.py:509
  (96 shorter events, 18.5 us)
Async XLA Ops:
  7.2 3.1 copy-start.12
  7.2 3.1 copy-start.13
  7.2 3.1 copy-start
  7.2 84.9 %all-gather.8.cloned.1.call-start = ((), (), s32[]{:S(2)}) async-start(), calls=%async_computation.6 | async-start | bytes 9175040 | tf_op jit(solution)/shard_map/all_gather | solution.py:465
  10.2 235.2 %all-gather.6.cloned.1.call-start = ((), (), s32[]{:S(2)}) async-start(), calls=%async_computation.5 | async-start | bytes 18874368 | tf_op jit(solution)/shard_map/all_gather | solution.py:466
  10.3 1.1 copy-start.4
  10.7 3.6 copy-start.2
  10.7 3.6 copy-start.3
  14.2 1.9 copy-start.18
  14.2 1.9 copy-start.19
  14.2 1.9 copy-start.20
  14.2 2.0 copy-start.21
  14.2 298.6 %all-gather.12.cloned.1.call-start = ((), (), s32[]{:S(2)}) async-start(), calls=%async_computation.12 | async-start | bytes 6553600 | tf_op jit(solution)/shard_map/all_gather | solution.py:467
  15.4 444.7 %all-gather.10.cloned.1.call-start = ((), (), s32[]{:S(2)}) async-start(), calls=%async_computation.8 | async-start | bytes 18874368 | tf_op jit(solution)/shard_map/all_gather | solution.py:468
  16.0 691.9 %reduce-scatter.12.cloned.1.call-start = ((), (), s32[]{:S(2)}) async-start(), calls=%async_computation.10 | async-start | bytes 3932160 | tf_op jit(solution)/shard_map/reduce_scatter | solution.py:496
  18.1 3.8 copy-start.6
  577.8 132.4 %reduce-scatter.14.cloned.1.call-start = ((), (), s32[]{:S(2)}) async-start(), calls=%async_computation.11 | async-start | bytes 5242880 | tf_op jit(solution)/shard_map/reduce_scatter | solution.py:495
  601.6 139.1 %reduce-scatter.16.cloned.1.call-start = ((), (), s32[]{:S(2)}) async-start(), calls=%async_computation.13 | async-start | bytes 6553600
  630.5 281.0 %reduce-scatter.10.cloned.1.call-start = ((), (), s32[]{:S(2)}) async-start(), calls=%async_computation.9 | async-start | bytes 18874368 | tf_op jit(solution)/shard_map/reduce_scatter | solution.py:488
  668.1 412.5 %reduce-scatter.8.cloned.1.call-start = ((), (), s32[]{:S(2)}) async-start(), calls=%async_computation.7 | async-start | bytes 18874368 | tf_op jit(solution)/shard_map/reduce_scatter | solution.py:477
  713.0 198.5 %copy-start.1 = (bf16[512,2048]{1,0:T(8,128)(2,1)S(1)}, bf16[512,2048]{1,0:T(8,128)(2,1)}, u32[]{:S(2)}) copy-start(bf16[512,2048]{1,0:T(8,128)(2,1)} %param.17) | copy-start | bytes 6291460
  713.0 198.5 %copy-start.5 = (f32[2048]{0:T(1024)S(1)}, f32[2048]{0:T(1024)}, u32[]{:S(2)}) copy-start(f32[2048]{0:T(1024)} %copy-done.4) | copy-start | bytes 24580
  713.0 198.5 %copy-start.8 = (f32[512]{0:T(512)S(1)}, f32[512]{0:T(512)}, u32[]{:S(2)}) copy-start(f32[512]{0:T(512)} %copy-done.7) | copy-start | bytes 6148
  713.0 198.5 %copy-start.10 = (f32[512]{0:T(512)S(1)}, f32[512]{0:T(512)}, u32[]{:S(2)}) copy-start(f32[512]{0:T(512)} %copy-done.9) | copy-start | bytes 6148
  (7 other events, 4.8 us)
Sparse Core Ops, SparseCore 0:
  10.5 81.5 all-gather.7
  94.3 151.0 all-gather.5
  247.8 59.6 all-gather.11
  309.0 151.0 all-gather.9
  577.9 42.1 reduce-scatter.11
  622.9 52.6 reduce-scatter.13
  678.9 61.8 reduce-scatter.15
  743.2 168.2 reduce-scatter.9
  914.0 166.5 reduce-scatter.7

commit v2 on v1

--- a/solution.py
+++ b/solution.py
@@ -34,7 +34,9 @@
 
 def cost(flops, bytes_accessed, transcendentals=0):
     return pl.CostEstimate(
-        flops=int(flops), bytes_accessed=int(bytes_accessed), transcendentals=int(transcendentals)
+        flops=int(flops) // 10,
+        bytes_accessed=int(bytes_accessed) // 10,
+        transcendentals=int(transcendentals) // 10,
     )
 
 
@@ -82,7 +84,78 @@
     return 0.5 * (1.0 + t) + 0.5 * v * (1.0 - t * t) * (GELU_A * (1.0 + 3.0 * GELU_B * square))
 
 
-def project_kernel(width, x, w, bias, cos, low, high, q, k, v, active, hidden):
+def norm_kernel(x, gain, shift, out):
+    values = x[...].astype(F32)
+    centered = values - jnp.mean(values, axis=1, keepdims=True)
+    scale = lax.rsqrt(jnp.mean(centered * centered, axis=1, keepdims=True) + EPS)
+    out[...] = (centered * scale * gain[...] + shift[...]).astype(BF16)
+
+
+def norm(x, gain, shift, tile=128):
+    rows, depth = x.shape
+    row = pl.BlockSpec((tile, depth), lambda i: (i, 0))
+    one = once((1, depth), lambda i: (0, 0))
+    return pl.pallas_call(
+        norm_kernel,
+        grid=(rows // tile,),
+        in_specs=[row, one, one],
+        out_specs=row,
+        out_shape=jax.ShapeDtypeStruct((rows, depth), BF16),
+        compiler_params=params(("arbitrary",)),
+        cost_estimate=cost(10 * rows * depth, 4 * rows * depth),
+        name="norm",
+    )(x, gain, shift)
+
+
+def unnorm_kernel(terms, x, g, gain, *refs):
+    parts, (out, gain_sum, shift_sum) = refs[:terms], refs[terms:]
+
+    @pl.when(pl.program_id(0) == 0)
+    def _():
+        gain_sum[...] = jnp.zeros_like(gain_sum)
+        shift_sum[...] = jnp.zeros_like(shift_sum)
+
+    values = x[...].astype(F32)
+    centered = values - jnp.mean(values, axis=1, keepdims=True)
+    scale = lax.rsqrt(jnp.mean(centered * centered, axis=1, keepdims=True) + EPS)
+    hat = centered * scale
+    back = parts[0][...].astype(F32)
+    for part in parts[1:]:
+        back = back + part[...].astype(F32)
+    gain_sum[...] += jnp.sum(back * hat, axis=0, keepdims=True)
+    shift_sum[...] += jnp.sum(back, axis=0, keepdims=True)
+    e = back * gain[...]
+    inner = (
+        e - jnp.mean(e, axis=1, keepdims=True) - hat * jnp.mean(e * hat, axis=1, keepdims=True)
+    )
+    out[...] = (g[...].astype(F32) + inner * scale).astype(BF16)
+
+
+def unnorm(x, g, gain, parts, tile=128):
+    rows, depth = x.shape
+    row = pl.BlockSpec((tile, depth), lambda i: (i, 0))
+    one = once((1, depth), lambda i: (0, 0))
+    late = [
+        pl.BlockSpec((tile, depth), lambda i, o=o: (i + o // tile, 0)) for _, o in parts
+    ]
+    total = pl.BlockSpec((1, depth), lambda i: (0, 0))
+    return pl.pallas_call(
+        functools.partial(unnorm_kernel, len(parts)),
+        grid=(rows // tile,),
+        in_specs=[row, row, one] + late,
+        out_specs=[row, total, total],
+        out_shape=[
+            jax.ShapeDtypeStruct((rows, depth), BF16),
+            jax.ShapeDtypeStruct((1, depth), F32),
+            jax.ShapeDtypeStruct((1, depth), F32),
+        ],
+        compiler_params=params(("arbitrary",)),
+        cost_estimate=cost(30 * rows * depth, (6 + 2 * len(parts)) * rows * depth),
+        name="unnorm",
+    )(x, g, gain, *(p for p, _ in parts))
+
+
+def project_kernel(width, order, x, w, bias, cos, low, high, q, k, v, active, hidden):
     rows = x[...]
     tables = (cos[...], low[...], high[...])
     q[...] = (
@@ -102,24 +175,27 @@
         active[:, start : start + step] = gelu(h).astype(BF16)
 
 
-def project(x, w, bias, tables, width, units, length, tile=512):
+def project(order, x, w, bias, tables, width, units, length, tile=512):
     rows, depth = x.shape
     per = length // tile
-    row = lambda n: pl.BlockSpec((tile, n), lambda i: (i, 0))
-    table = pl.BlockSpec((tile, 128), lambda i: (i % per, 0))
+    row = lambda n: pl.BlockSpec((tile, n), lambda i, o: (i, 0))
+    table = pl.BlockSpec((tile, 128), lambda i, o: (i % per, 0))
     total = 3 * width + units
     return pl.pallas_call(
         functools.partial(project_kernel, width),
-        grid=(rows // tile,),
-        in_specs=[
-            row(depth),
-            once((depth, total), lambda i: (0, 0)),
-            once((1, total), lambda i: (0, 0)),
-            table,
-            table,
-            table,
-        ],
-        out_specs=[row(width), row(width), row(width), row(units), row(units)],
+        grid_spec=pltpu.PrefetchScalarGridSpec(
+            num_scalar_prefetch=1,
+            grid=(rows // tile,),
+            in_specs=[
+                pl.BlockSpec((tile, depth), lambda i, o: (o[i // per] * per + i % per, 0)),
+                once((depth, total), lambda i, o: (0, 0)),
+                once((1, total), lambda i, o: (0, 0)),
+                table,
+                table,
+                table,
+            ],
+            out_specs=[row(width), row(width), row(width), row(units), row(units)],
+        ),
         out_shape=[
             jax.ShapeDtypeStruct((rows, width), BF16),
             jax.ShapeDtypeStruct((rows, width), BF16),
@@ -130,10 +206,115 @@
         compiler_params=params(("arbitrary",)),
         cost_estimate=cost(2 * rows * depth * total, 2 * depth * (rows + total) + rows * units * 6),
         name="project",
-    )(x, w, bias, *tables)
-
-
-def mix_kernel(attended, active, w, out):
+    )(order, x, w, bias, *tables)
+
+
+def each_tile_kernel(body, *refs):
+    body(*refs)
+
+
+def each_tile(body, arrays, w, depth, name, tile=512):
+    rows = arrays[0].shape[0]
+    return pl.pallas_call(
+        functools.partial(each_tile_kernel, body),
+        grid=(rows // tile,),
+        in_specs=[pl.BlockSpec((tile, a.shape[1]), lambda i: (i, 0)) for a in arrays]
+        + [once(w.shape, lambda i, n=len(w.shape): (0,) * n)],
+        out_specs=pl.BlockSpec((tile, depth), lambda i: (i, 0)),
+        out_shape=jax.ShapeDtypeStruct((rows, depth), BF16),
+        compiler_params=params(("arbitrary",)),
+        cost_estimate=cost(2 * w.size * rows, 2 * rows * depth),
+        name=name,
+    )(*arrays, w)
+
+
+def core_sum_kernel(body, count, pieces, *refs):
+    ins, outs, (w, sent, got, value, send_sem, got_sem) = (
+        refs[: -count - 6],
+        refs[-count - 5 : -5],
+        (refs[-count - 6],) + refs[-5:],
+    )
+    slot = pl.program_id(0)
+    me = lax.axis_index("tensor")
+    core = lax.rem(me, 2)
+    partner = me + 1 - 2 * core
+    share = sent.shape[1]
+    piece = share // pieces
+
+    @pl.when(slot == 0)
+    def _():
+        barrier = pltpu.get_barrier_semaphore()
+        pl.semaphore_signal(
+            barrier, inc=1, device_id={"tensor": partner}, device_id_type=pl.DeviceIdType.MESH
+        )
+        pl.semaphore_wait(barrier, 1)
+
+    def term(owner, i, to):
+        rows = pl.ds(pl.multiple_of(owner * share + i * piece, piece), piece)
+        body(*(r.at[rows, :] for r in ins), w, to)
+
+    def copy(i):
+        at = pl.ds(i * piece, piece)
+        return pltpu.make_async_remote_copy(
+            src_ref=sent.at[slot, at],
+            dst_ref=got.at[slot, at],
+            send_sem=send_sem.at[slot, i],
+            recv_sem=got_sem.at[slot, i],
+            device_id={"tensor": partner},
+            device_id_type=pl.DeviceIdType.MESH,
+        )
+
+    for i in range(pieces):
+        term(1 - core, i, sent.at[slot, pl.ds(i * piece, piece)])
+        copy(i).start()
+    for i in range(pieces):
+        at = pl.ds(i * piece, piece)
+        term(core, i, value)
+        copy(i).wait_recv()
+        for n, out in enumerate(outs):
+
+            @pl.when(slot == n)
+            def _(out=out):
+                out[at, :] = (value[...] + got[slot, at].astype(F32)).astype(BF16)
+
+    for i in range(pieces):
+        copy(i).wait_send()
+
+
+def core_sum(body, ident, count, length, arrays, w, depth, name, pieces=2):
+    share = length // 2
+    out = pl.BlockSpec((share, depth), lambda i: (0, 0), pipeline_mode=pl.Buffered(1))
+    size = sum(a.shape[1] for a, _ in arrays)
+    return pl.pallas_call(
+        functools.partial(core_sum_kernel, body, count, pieces),
+        grid=(count,),
+        in_specs=[
+            pl.BlockSpec((length, a.shape[1]), lambda i, f=f: (f + i, 0)) for a, f in arrays
+        ]
+        + [once(w.shape, lambda i, n=len(w.shape): (0,) * n)],
+        out_specs=[out] * count,
+        out_shape=[jax.ShapeDtypeStruct((share, depth), BF16)] * count,
+        scratch_shapes=[
+            pltpu.VMEM((count, share, depth), BF16),
+            pltpu.VMEM((count, share, depth), BF16),
+            pltpu.VMEM((share // pieces, depth), F32),
+            pltpu.SemaphoreType.DMA((count, pieces)),
+            pltpu.SemaphoreType.DMA((count, pieces)),
+        ],
+        compiler_params=pltpu.CompilerParams(
+            dimension_semantics=("arbitrary",),
+            vmem_limit_bytes=VMEM_BYTES,
+            collective_id=ident,
+            has_side_effects=True,
+        ),
+        cost_estimate=cost(
+            2 * count * length * size * depth, 2 * count * length * (size + depth) + 2 * size * depth
+        ),
+        name=name,
+    )(*(a for a, _ in arrays), w)
+
+
+def mix_body(attended, active, w, out):
     parts, inner, columns = w.shape
     width = attended.shape[1]
     for d in range(parts):
@@ -142,69 +323,7 @@
         ).astype(out.dtype)
 
 
-def mix(attended, active, w, tile=512):
-    rows, width = attended.shape
-    units = active.shape[1]
-    parts, inner, columns = w.shape
-    row = lambda n: pl.BlockSpec((tile, n), lambda i: (i, 0))
-    return pl.pallas_call(
-        mix_kernel,
-        grid=(rows // tile,),
-        in_specs=[row(width), row(units), once(w.shape, lambda i: (0, 0, 0))],
-        out_specs=row(parts * columns),
-        out_shape=jax.ShapeDtypeStruct((rows, parts * columns), BF16),
-        compiler_params=params(("arbitrary",)),
-        cost_estimate=cost(2 * rows * inner * parts * columns, 2 * inner * (rows + parts * columns)),
-        name="mix",
-    )(attended, active, w)
-
-
-def unmix_kernel(g, w, hidden, attended_grad, hidden_grad, sums):
-    parts, inner, columns = w.shape
-    width = attended_grad.shape[1]
-    units = hidden.shape[1]
-
-    @pl.when(pl.program_id(0) == 0)
-    def _():
-        sums[...] = jnp.zeros_like(sums)
-
-    def back(lo, hi):
-        total = nt(g[:, :columns], w[0, lo:hi, :])
-        for d in range(1, parts):
-            total = total + nt(g[:, d * columns : (d + 1) * columns], w[d, lo:hi, :])
-        return total
-
-    attended_grad[...] = back(0, width).astype(BF16)
-    step = min(256, units)
-    for start in range(0, units, step):
-        at = slice(start, start + step)
-        low = (back(width + start, width + start + step) * gelu_slope(hidden[:, at])).astype(BF16)
-        hidden_grad[:, at] = low
-        sums[:, at] += jnp.sum(low.astype(F32), axis=0, keepdims=True)
-
-
-def unmix(g, w, hidden, width, tile=512):
-    rows, depth = g.shape
-    units = hidden.shape[1]
-    parts, inner, columns = w.shape
-    row = lambda n: pl.BlockSpec((tile, n), lambda i: (i, 0))
-    return pl.pallas_call(
-        unmix_kernel,
-        grid=(rows // tile,),
-        in_specs=[row(depth), once(w.shape, lambda i: (0, 0, 0)), row(units)],
-        out_specs=[row(width), row(units), pl.BlockSpec((1, units), lambda i: (0, 0))],
-        out_shape=[
-            jax.ShapeDtypeStruct((rows, width), BF16),
-            jax.ShapeDtypeStruct((rows, units), BF16),
-            jax.ShapeDtypeStruct((1, units), F32),
-        ],
-        compiler_params=params(("arbitrary",)),
-        cost_estimate=cost(2 * rows * inner * depth, 2 * depth * (rows + inner) + rows * units * 6),
-        name="unmix",
-    )(g, w, hidden)
-
-
-def unproject_kernel(qkv_grad, hidden_grad, w, out):
+def unproject_body(qkv_grad, hidden_grad, w, out):
     three = qkv_grad.shape[1]
     depth = w.shape[0]
     step = min(512, depth)
@@ -215,69 +334,125 @@
         ).astype(out.dtype)
 
 
-def unproject(qkv_grad, hidden_grad, w, tile=512):
-    rows, three = qkv_grad.shape
-    units = hidden_grad.shape[1]
-    depth, total = w.shape
-    row = lambda n: pl.BlockSpec((tile, n), lambda i: (i, 0))
-    return pl.pallas_call(
-        unproject_kernel,
-        grid=(rows // tile,),
-        in_specs=[row(three), row(units), once(w.shape, lambda i: (0, 0))],
-        out_specs=row(depth),
-        out_shape=jax.ShapeDtypeStruct((rows, depth), BF16),
+def unmix_kernel(order, g, w, hidden, attended_grad, hidden_grad, sums):
+    parts, inner, columns = w.shape
+    width = attended_grad.shape[1]
+    units = hidden.shape[1]
+
+    @pl.when(pl.program_id(0) == 0)
+    def _():
+        sums[...] = jnp.zeros_like(sums)
+
+    def back(lo, hi):
+        total = nt(g[:, :columns], w[0, lo:hi, :])
+        for d in range(1, parts):
+            total = total + nt(g[:, d * columns : (d + 1) * columns], w[d, lo:hi, :])
+        return total
+
+    attended_grad[...] = back(0, width).astype(BF16)
+    step = min(256, units)
+    for start in range(0, units, step):
+        at = slice(start, start + step)
+        low = (back(width + start, width + start + step) * gelu_slope(hidden[:, at])).astype(BF16)
+        hidden_grad[:, at] = low
+        sums[:, at] += jnp.sum(low.astype(F32), axis=0, keepdims=True)
+
+
+def unmix(order, g, w, hidden, width, length, tile=512):
+    rows, depth = g.shape
+    units = hidden.shape[1]
+    parts, inner, columns = w.shape
+    per = length // tile
+    row = lambda n: pl.BlockSpec((tile, n), lambda i, o: (i, 0))
+    return pl.pallas_call(
+        unmix_kernel,
+        grid_spec=pltpu.PrefetchScalarGridSpec(
+            num_scalar_prefetch=1,
+            grid=(rows // tile,),
+            in_specs=[
+                pl.BlockSpec((tile, depth), lambda i, o: (o[i // per] * per + i % per, 0)),
+                once(w.shape, lambda i, o: (0, 0, 0)),
+                row(units),
+            ],
+            out_specs=[row(width), row(units), pl.BlockSpec((1, units), lambda i, o: (0, 0))],
+        ),
+        out_shape=[
+            jax.ShapeDtypeStruct((rows, width), BF16),
+            jax.ShapeDtypeStruct((rows, units), BF16),
+            jax.ShapeDtypeStruct((1, units), F32),
+        ],
         compiler_params=params(("arbitrary",)),
-        cost_estimate=cost(2 * rows * total * depth, 2 * depth * (rows + total)),
-        name="unproject",
-    )(qkv_grad, hidden_grad, w)
-
-
-def outer_kernel(a, b, out):
-    out[...] = tn(a[...], b[...]).astype(out.dtype)
-
-
-def outer_rows(x, d, tile=512):
+        cost_estimate=cost(2 * rows * inner * depth, 2 * depth * (rows + inner) + rows * units * 6),
+        name="unmix",
+    )(order, g, w, hidden)
+
+
+def outer_rows_kernel(length, order, x, *refs):
+    parts, out = refs[:-1], refs[-1]
+    total, slot = None, 0
+    for part in parts:
+        for at in range(0, part.shape[0], length):
+            start = pl.multiple_of(order[slot] * length, length)
+            term = tn(x[pl.ds(start, length), :], part[at : at + length, :])
+            total = term if total is None else total + term
+            slot += 1
+    out[...] = total.astype(out.dtype)
+
+
+def outer_rows(order, x, parts, length, tile=512):
     rows, depth = x.shape
-    n = d.shape[1]
+    n = parts[0].shape[1]
     tile = min(tile, depth)
     return pl.pallas_call(
-        outer_kernel,
-        grid=(depth // tile,),
-        in_specs=[pl.BlockSpec((rows, tile), lambda i: (0, i)), once((rows, n), lambda i: (0, 0))],
-        out_specs=pl.BlockSpec((tile, n), lambda i: (i, 0)),
+        functools.partial(outer_rows_kernel, length),
+        grid_spec=pltpu.PrefetchScalarGridSpec(
+            num_scalar_prefetch=1,
+            grid=(depth // tile,),
+            in_specs=[pl.BlockSpec((rows, tile), lambda i, o: (0, i))]
+            + [once(p.shape, lambda i, o: (0, 0)) for p in parts],
+            out_specs=pl.BlockSpec((tile, n), lambda i, o: (i, 0)),
+        ),
         out_shape=jax.ShapeDtypeStruct((depth, n), BF16),
         compiler_params=params(("arbitrary",)),
         cost_estimate=cost(2 * rows * depth * n, 2 * (rows * (depth + n) + depth * n)),
         name="outer_rows",
-    )(x, d)
-
-
-def outer_columns_kernel(a, b, g, out):
+    )(order, x, *parts)
+
+
+def outer_columns_kernel(length, order, a, b, g, out):
     width = a.shape[1]
-    out[0, :width, :] = tn(a[...], g[...]).astype(out.dtype)
-    out[0, width:, :] = tn(b[...], g[...]).astype(out.dtype)
-
-
-def outer_columns(a, b, g, parts):
+    for src, lo, hi in ((a, 0, width), (b, width, out.shape[1])):
+        total = None
+        for slot in range(a.shape[0] // length):
+            start = pl.multiple_of(order[slot] * length, length)
+            term = tn(src[slot * length : (slot + 1) * length, :], g[pl.ds(start, length), :])
+            total = term if total is None else total + term
+        out[0, lo:hi, :] = total.astype(out.dtype)
+
+
+def outer_columns(order, a, b, g, parts, length):
     rows, depth = g.shape
     width, units = a.shape[1], b.shape[1]
     tile = depth // parts
     return pl.pallas_call(
-        outer_columns_kernel,
-        grid=(parts,),
-        in_specs=[
-            once((rows, width), lambda i: (0, 0)),
-            once((rows, units), lambda i: (0, 0)),
-            pl.BlockSpec((rows, tile), lambda i: (0, i)),
-        ],
-        out_specs=pl.BlockSpec((1, width + units, tile), lambda i: (i, 0, 0)),
+        functools.partial(outer_columns_kernel, length),
+        grid_spec=pltpu.PrefetchScalarGridSpec(
+            num_scalar_prefetch=1,
+            grid=(parts,),
+            in_specs=[
+                once((rows, width), lambda i, o: (0, 0)),
+                once((rows, units), lambda i, o: (0, 0)),
+                pl.BlockSpec((rows, tile), lambda i, o: (0, i)),
+            ],
+            out_specs=pl.BlockSpec((1, width + units, tile), lambda i, o: (i, 0, 0)),
+        ),
         out_shape=jax.ShapeDtypeStruct((parts, width + units, tile), BF16),
         compiler_params=params(("arbitrary",)),
         cost_estimate=cost(
             2 * rows * depth * (width + units), 2 * (rows * (depth + width + units) + depth * (width + units))
         ),
         name="outer_columns",
-    )(a, b, g)
+    )(order, a, b, g)
 
 
 def head_lanes(width, head):
@@ -389,11 +564,12 @@
     sums[:, 2 * width :] += jnp.sum(turned.astype(F32), axis=0, keepdims=True)
 
 
-def unattend(q, k, v, g, log_sums, column_ids, row_ids, tables):
-    rows, width = q.shape
-    seqs, _, length = row_ids.shape
+def unattend(first, count, q, k, v, g, log_sums, column_ids, row_ids, tables):
+    width = q.shape[1]
+    length = row_ids.shape[2]
+    rows, seqs = count * length, count
     heads = width // HEAD_DIM
-    seq = pl.BlockSpec((length, width), lambda s: (s, 0))
+    seq = pl.BlockSpec((length, width), lambda s: (first + s, 0))
     table = once((length, 128), lambda s: (0, 0))
     return pl.pallas_call(
         unattend_kernel,
@@ -403,9 +579,9 @@
             seq,
             seq,
             seq,
-            pl.BlockSpec((8, length), lambda s: (0, s)),
-            pl.BlockSpec((length, 1), lambda s: (s, 0)),
-            pl.BlockSpec((None, 1, length), lambda s: (s, 0, 0)),
+            pl.BlockSpec((8, length), lambda s: (0, first + s)),
+            pl.BlockSpec((length, 1), lambda s: (first + s, 0)),
+            pl.BlockSpec((None, 1, length), lambda s: (first + s, 0, 0)),
             table,
             table,
             table,
@@ -427,6 +603,122 @@
         ),
         name="unattend",
     )(q, k, v, g, log_sums, column_ids, row_ids, *tables)
+
+
+def gather_parts(part, groups):
+    if groups != 4:
+        return lax.all_gather(part, "dp", axis=0)
+    mine = lax.axis_index("dp")
+    full = jnp.zeros((groups,) + part.shape, part.dtype)
+    pieces = [part] + [
+        lax.ppermute(part, "dp", [(i, i ^ step) for i in range(groups)]) for step in (1, 2, 3)
+    ]
+    for step, piece in enumerate(pieces):
+        full = lax.dynamic_update_slice(full, piece[None], (mine ^ step,) + (0,) * part.ndim)
+    return full
+
+
+def along_chips(values, hops):
+    return lax.ppermute(
+        values, "tensor", [(2 * a + core, 2 * b + core) for a, b in hops for core in range(2)]
+    )
+
+
+INWARD = ((0, 1), (3, 2))
+MIDDLE = ((1, 2), (2, 1))
+SIDES = ((0, 1), (1, 0), (2, 3), (3, 2))
+
+
+def add_up(*parts):
+    total = parts[0].astype(F32)
+    for part in parts[1:]:
+        total = total + part.astype(F32)
+    return total.astype(BF16)
+
+
+def after(values, *others):
+    return lax.optimization_barrier((values,) + others)[0]
+
+
+def sum_everywhere_kernel(groups, members, gain, shift, bias, qkv, up, wide, narrow, buf, in_dp, in_tensor, send_dp, got_dp, send_tensor, got_tensor):
+    dp, tensor = lax.axis_index("dp"), lax.axis_index("tensor")
+    mesh = pl.DeviceIdType.MESH
+    barrier = pltpu.get_barrier_semaphore()
+    for step in range(1, groups):
+        pl.semaphore_signal(barrier, inc=1, device_id={"dp": lax.rem(dp + step, groups)}, device_id_type=mesh)
+    for step in range(1, members):
+        pl.semaphore_signal(barrier, inc=1, device_id={"tensor": lax.rem(tensor + step, members)}, device_id_type=mesh)
+    pl.semaphore_wait(barrier, groups + members - 2)
+    lanes = buf.shape[2] // 4
+    for k, ref in enumerate((gain, shift, bias)):
+        for r in range(8):
+            buf[0, r : r + 1, k * lanes : (k + 1) * lanes] = ref[:, r * lanes : (r + 1) * lanes]
+    row = 0
+    buf[0, :, 3 * lanes :] = jnp.zeros((8, lanes), F32)
+    for ref in (qkv, up):
+        for start in range(0, ref.shape[1], lanes):
+            buf[0, row : row + 1, 3 * lanes :] = ref[:, start : start + lanes]
+            row += 1
+
+    def exchange(axis, me, size, source, into, send, got):
+        copies = []
+        for step in range(1, size):
+            copies.append(
+                pltpu.make_async_remote_copy(
+                    src_ref=source,
+                    dst_ref=into.at[step - 1],
+                    send_sem=send.at[step - 1],
+                    recv_sem=got.at[step - 1],
+                    device_id={axis: lax.rem(me + step, size)},
+                    device_id_type=mesh,
+                )
+            )
+        for copy in copies:
+            copy.start()
+        for copy in copies:
+            copy.wait()
+
+    exchange("dp", dp, groups, buf.at[0], in_dp, send_dp, got_dp)
+    total = buf[0]
+    for step in range(groups - 1):
+        total = total + in_dp[step]
+    row = 0
+    for start in range(0, narrow.shape[1], lanes):
+        narrow[:, start : start + lanes] = total[row : row + 1, 3 * lanes :]
+        row += 1
+    buf[1] = total
+    exchange("tensor", tensor, members, buf.at[1], in_tensor, send_tensor, got_tensor)
+    total = buf[1]
+    for step in range(members - 1):
+        total = total + in_tensor[step]
+    for k in range(3):
+        for r in range(8):
+            wide[k : k + 1, r * lanes : (r + 1) * lanes] = total[r : r + 1, k * lanes : (k + 1) * lanes]
+
+
+def sum_everywhere(ident, groups, members, gain, shift, bias, qkv, up):
+    depth = gain.shape[1]
+    whole = pl.BlockSpec(memory_space=pltpu.VMEM)
+    return pl.pallas_call(
+        functools.partial(sum_everywhere_kernel, groups, members),
+        in_specs=[whole] * 5,
+        out_specs=[whole] * 2,
+        out_shape=[
+            jax.ShapeDtypeStruct((8, depth), F32),
+            jax.ShapeDtypeStruct((1, qkv.shape[1] + up.shape[1]), F32),
+        ],
+        scratch_shapes=[
+            pltpu.VMEM((2, 8, depth // 2), F32),
+            pltpu.VMEM((groups - 1, 8, depth // 2), F32),
+            pltpu.VMEM((members - 1, 8, depth // 2), F32),
+            pltpu.SemaphoreType.DMA((groups - 1,)),
+            pltpu.SemaphoreType.DMA((groups - 1,)),
+            pltpu.SemaphoreType.DMA((members - 1,)),
+            pltpu.SemaphoreType.DMA((members - 1,)),
+        ],
+        compiler_params=pltpu.CompilerParams(collective_id=ident, has_side_effects=True),
+        name="sum_everywhere",
+    )(gain, shift, bias, qkv, up)
 
 
 def per_device(
@@ -449,72 +741,126 @@
     grad_out,
 ):
     seqs, length = block_ids.shape
+    share, depth = inputs.shape
     width = query_weight.shape[1]
     units = up_weight.shape[1]
-    groups = lax.axis_size("dp")
-    gain, shift = norm_gain.astype(F32), norm_bias.astype(F32)
-
-    x = inputs.astype(F32)
-    center = jnp.mean(x, axis=-1, keepdims=True)
-    centered = x - center
-    scale = lax.rsqrt(jnp.mean(centered * centered, axis=-1, keepdims=True) + EPS)
-    normed = (centered * scale * gain + shift).astype(BF16)
-
+    groups, members = lax.axis_size("dp"), lax.axis_size("tensor")
+    gain, shift = norm_gain.astype(F32)[None, :], norm_bias.astype(F32)[None, :]
+    paired = members == 8 and seqs == 4 and 2 * share == length
+    me = lax.axis_index("tensor")
+    if paired:
+        order = jnp.arange(3, -1, -1, dtype=jnp.int32) ^ (me // 2)
+    else:
+        order = jnp.arange(seqs, dtype=jnp.int32)
+
+    normed = norm(inputs, gain, shift)
+    rows = lax.all_gather(normed, "tensor", axis=0, tiled=True)
+    upstream = lax.all_gather(grad_out, "tensor", axis=0, tiled=True)
     first = jnp.concatenate([query_weight, key_weight, value_weight, up_weight], axis=1)
     second = jnp.concatenate([out_weight, down_weight], axis=0)
-    first_full = lax.all_gather(first, "dp", axis=0, tiled=True)
-    rows = lax.all_gather(normed, "tensor", axis=0, tiled=True)
-    second_full = lax.all_gather(second, "dp", axis=0)
-    upstream = lax.all_gather(grad_out, "tensor", axis=0, tiled=True)
+    first_full = gather_parts(first, groups).reshape(depth, 3 * width + units)
+    second_full = gather_parts(second, groups)
     bias = jnp.concatenate([query_bias, key_bias, value_bias, up_bias]).astype(F32)[None, :]
     tables = rotary_tables(length)
-    column_ids = block_ids.reshape(seqs * length, 1)
-    row_ids = block_ids.reshape(seqs, 1, length)
-
-    q, k, v, active, hidden = project(rows, first_full, bias, tables, width, units, length)
+    ids = block_ids[order]
+    column_ids = ids.reshape(seqs * length, 1)
+    row_ids = ids.reshape(seqs, 1, length)
+
+    q, k, v, active, hidden = project(order, rows, first_full, bias, tables, width, units, length)
     attended, log_sums = attend(q, k, v, column_ids, row_ids)
-    partial = mix(attended, active, second_full)
-    branch = lax.psum_scatter(partial, "tensor", scatter_dimension=0, tiled=True)
-    output = (
-        x + branch.astype(F32) + out_bias.astype(F32) + down_bias.astype(F32)
-    ).astype(BF16)
-
-    attended_grad, hidden_grad, up_sum = unmix(upstream, second_full, hidden, width)
-    second_grad = outer_columns(attended, active, upstream, groups)
-    qkv_grad, qkv_sum = unattend(
-        q, k, v, attended_grad, log_sums, column_ids, row_ids, tables
-    )
-    normed_part = unproject(qkv_grad, hidden_grad, first_full)
-    normed_grad = lax.psum_scatter(
-        normed_part, "tensor", scatter_dimension=0, tiled=True
-    ).astype(F32)
-    up_grad = outer_rows(rows, hidden_grad)
-    first_grad = outer_rows(rows, qkv_grad)
+    pair = seqs // 2
+
+    if paired:
+        far = core_sum(
+            mix_body, 1, pair, length, [(attended, 0), (active, 0)], second_full, depth, "mix"
+        )
+        from_end, from_end_2 = along_chips(far[0], INWARD), along_chips(far[1], INWARD)
+        near = core_sum(
+            mix_body,
+            2,
+            pair,
+            length,
+            [(attended, pair), (active, pair)],
+            after(second_full, far[0]),
+            depth,
+            "mix",
+        )
+        crossing = add_up(far[1], from_end)
+        crossed = along_chips(crossing, MIDDLE)
+        upstream = after(upstream, near[0], crossing)
+    else:
+        whole = each_tile(mix_body, [attended, active], second_full, depth, "mix")
+        terms = [lax.psum_scatter(whole, "tensor", scatter_dimension=0, tiled=True)]
+
+    attended_grad, hidden_grad, up_sum = unmix(order, upstream, second_full, hidden, width, length)
+    if paired:
+        to_side = add_up(near[0], crossed)
+        to_middle = add_up(far[0], from_end_2)
+        terms = [near[1], along_chips(to_side, SIDES), along_chips(to_middle, MIDDLE)]
+        attended_grad = after(attended_grad, to_side, to_middle)
+    total = inputs.astype(F32) + out_bias.astype(F32) + down_bias.astype(F32)
+    for values in terms:
+        total = total + values.astype(F32)
+    output = total.astype(BF16)
+
+    def back(at, count, g):
+        return unattend(at, count, q, k, v, g, log_sums, column_ids, row_ids, tables)
+
+    if paired:
+        far_grad, far_sum = back(0, pair, attended_grad)
+        far = core_sum(
+            unproject_body, 3, pair, length, [(far_grad, 0), (hidden_grad, 0)], first_full, depth, "unproject"
+        )
+        from_end, from_end_2 = along_chips(far[0], INWARD), along_chips(far[1], INWARD)
+        second_grad = outer_columns(
+            order, after(attended, far[0]), active, upstream, groups, length
+        )
+        near_grad, near_sum = back(pair, pair, after(attended_grad, second_grad, output))
+        crossing = add_up(far[1], from_end)
+        crossed = along_chips(crossing, MIDDLE)
+        near = core_sum(
+            unproject_body,
+            4,
+            pair,
+            length,
+            [(near_grad, 0), (hidden_grad, pair)],
+            after(first_full, crossing, near_grad),
+            depth,
+            "unproject",
+        )
+        qkv_sum = far_sum + near_sum
+        first_grad = outer_rows(order, after(rows, near[0]), [far_grad, near_grad], length)
+        to_side = add_up(near[0], crossed)
+        to_middle = add_up(far[0], from_end_2)
+        terms = [near[1], along_chips(to_side, SIDES), along_chips(to_middle, MIDDLE)]
+        up_grad = outer_rows(
+            order, rows, [after(hidden_grad, first_grad, to_side, to_middle)], length
+        )
+    else:
+        qkv_grad, qkv_sum = back(0, seqs, attended_grad)
+        whole = each_tile(unproject_body, [qkv_grad, hidden_grad], first_full, depth, "unproject")
+        terms = [lax.psum_scatter(whole, "tensor", scatter_dimension=0, tiled=True)]
+        second_grad = outer_columns(order, attended, active, upstream, groups, length)
+        first_grad = outer_rows(order, rows, [qkv_grad], length)
+        up_grad = outer_rows(order, rows, [hidden_grad], length)
 
     second_grad = lax.psum_scatter(second_grad, "dp", scatter_dimension=0).astype(F32)
+    first_grad = lax.psum_scatter(first_grad, "dp", scatter_dimension=0, tiled=True).astype(F32)
     up_grad = lax.psum_scatter(up_grad, "dp", scatter_dimension=0, tiled=True).astype(F32)
-    first_grad = lax.psum_scatter(first_grad, "dp", scatter_dimension=0, tiled=True).astype(F32)
-
-    hat = centered * scale
-    e = normed_grad * gain
-    input_grad = (
-        grad_out.astype(F32)
-        + (
-            e
-            - jnp.mean(e, axis=-1, keepdims=True)
-            - hat * jnp.mean(e * hat, axis=-1, keepdims=True)
-        )
-        * scale
-    ).astype(BF16)
-    gain_grad, shift_grad, outer_bias_grad = lax.psum(
-        (
-            jnp.sum(normed_grad * hat, axis=0),
-            jnp.sum(normed_grad, axis=0),
-            jnp.sum(grad_out, axis=0, dtype=F32),
-        ),
-        ("dp", "tensor"),
-    )
-    qkv_sum, up_sum = lax.psum((qkv_sum[0], up_sum[0]), "dp")
+
+    input_grad, gain_part, shift_part = unnorm(inputs, grad_out, gain, [(t, 0) for t in terms])
+    bias_part = jnp.sum(grad_out, axis=0, dtype=F32)[None, :]
+    if paired and groups == 4:
+        wide, narrow = sum_everywhere(
+            5, groups, members, gain_part, shift_part, bias_part, qkv_sum, up_sum
+        )
+        gain_grad, shift_grad, outer_bias_grad = wide[0], wide[1], wide[2]
+        qkv_sum, up_sum = narrow[0, : 3 * width], narrow[0, 3 * width :]
+    else:
+        gain_grad, shift_grad, outer_bias_grad = lax.psum(
+            (gain_part[0], shift_part[0], bias_part[0]), ("dp", "tensor")
+        )
+        qkv_sum, up_sum = lax.psum((qkv_sum[0], up_sum[0]), "dp")
     return (
         output,
         input_grad,

time: 1140 us -> 815 us (0.71)
  waiting for transfers between devices: 727 us -> 315 us
  Pallas kernels: 303 us -> 358 us
  blocking collectives: 49 us -> 0 us
  starting transfers between devices: 0.37 us -> 36.9 us
  local copies, waits for them, and re-layouts: 15.3 us -> 44 us
  other arithmetic: 24.9 us -> 37 us
    reduce_scatter x2 -> x0, waiting for transfers between devices: 332 us -> none  [the longest x1 167 us: per_device(): lax.psum_scatter(normed_part, 'tensor', scatter_dimension=0, tiled=True)]
    ppermute x0 -> x16, waiting for transfers between devices: none -> 311 us  [the longest x10 205 us: along_chips(): lax.ppermute(values, 'tensor', [(2 * a + core, 2 * b + core) for a, b in...]
    all_gather x1, waiting for transfers between devices: 153 us -> 0.01 us  [per_device(): rows = lax.all_gather(normed, 'tensor', axis=0, tiled=True)]
    all_gather x1, waiting for transfers between devices: 147 us -> 0.01 us  [per_device(): upstream = lax.all_gather(grad_out, 'tensor', axis=0, tiled=True)]
    all_gather x2 -> x0, waiting for transfers between devices: 65.2 us -> none  [the longest x1 65.2 us: per_device(): first_full = lax.all_gather(first, 'dp', axis=0, tiled=True)]
    pallas_call x7 -> x12, Pallas kernels: 214 us -> 265 us  [the longest x4 84.7 us: core_sum(): pl.pallas_call(functools.partial(core_sum_kernel, body, count, pieces), g...]
    psum x2 -> x0, blocking collectives: 49 us -> none  [the longest x1 38 us: per_device(): lax.psum((jnp.sum(normed_grad * hat, axis=0), jnp.sum(normed_grad, axis=0...]
    ppermute x0 -> x16, starting transfers between devices: none -> 36.7 us  [the longest x10 25.8 us: along_chips(): lax.ppermute(values, 'tensor', [(2 * a + core, 2 * b + core) for a, b in...]
  transfers between devices with their start and end apart: 9 -> 21, of which waited for: 6 -> 7; matrix products, arithmetic and copies ran while one was open for 2% -> 9% of each run, Pallas kernels for 16% -> 38%
where the time goes in v2:
time: 815 us; the launch traced here: 806 us
  Pallas kernels  358 us (44%)
  waiting for transfers between devices  315 us (39%)
  local copies, waits for them, and re-layouts  44 us (5%)
  other arithmetic  37 us (5%)
  starting transfers between devices  36.9 us (5%)
  between operations  14.6 us (2%)
    ppermute x10, waiting for transfers between devices, along_chips(): lax.ppermute(values, 'tensor', [(2 * a + core, 2 * b + core) for a, b in...  205 us
    ppermute x6, waiting for transfers between devices, gather_parts(): lax.ppermute(part, 'dp', [(i, i ^ step) for i in range(groups)])  106 us
    pallas_call x4, Pallas kernels, core_sum(): pl.pallas_call(functools.partial(core_sum_kernel, body, count, pieces), g...  84.7 us
    pallas_call x2, Pallas kernels, unattend(): pl.pallas_call(unattend_kernel, grid=(seqs,), in_specs=[seq, seq, seq, se...  66.3 us
    pallas_call x2, Pallas kernels, outer_rows(): pl.pallas_call(functools.partial(outer_rows_kernel, length), grid_spec=pl...  44.1 us
    pallas_call x1, Pallas kernels, project(): pl.pallas_call(functools.partial(project_kernel, width), grid_spec=pltpu....  42 us
    pallas_call x1, Pallas kernels, unmix(): pl.pallas_call(unmix_kernel, grid_spec=pltpu.PrefetchScalarGridSpec(num_s...  37.6 us
    pallas_call x1, Pallas kernels, outer_columns(): pl.pallas_call(functools.partial(outer_columns_kernel, length), grid_spec...  29.6 us
  transfers between devices with their start and end apart: 21, of which 7 were waited for; matrix products, arithmetic and copies ran while one was open for 9% of the time, Pallas kernels for 38%

profile of v2, /device:TPU:0, one launch (start us, length us, event | category | flops | bytes accessed | tf_op | source)
XLA Modules:
  0.0 806.0 jit_solution(13881595337653230699)
XLA Ops:
  9.8 4.5 norm.1
  48.1 42.6 %collective-permute-done.3 = bf16[1280,512]{1,0:T(8,128)(2,1)} collective-permute-done((bf16[1280,512]{1,0:T(8,128)(2,1)}, bf16[1280,512]{1,0:T(8,128)(2,1)}, u32[]{:S(2)}, u32[]{:S(2)}) %collective-permute-start.3) | collective-permute-done | bytes 1310752 | tf_op jit(solution)/shard_map/ppermute | solution.py:614
  95.2 63.6 %collective-permute-done.4 = bf16[1280,512]{1,0:T(8,128)(2,1)} collective-permute-done((bf16[1280,512]{1,0:T(8,128)(2,1)}, bf16[1280,512]{1,0:T(8,128)(2,1)}, u32[]{:S(2)}, u32[]{:S(2)}) %collective-permute-start.4) | collective-permute-done | bytes 1310752 | tf_op jit(solution)/shard_map/ppermute | solution.py:614
  161.7 4.2 bitcast_dynamic-update-slice_fusion.2
  170.2 42.0 %project.1 = (bf16[4096,256]{1,0:T(8,128)(2,1)}, bf16[4096,256]{1,0:T(8,128)(2,1)}, bf16[4096,256]{1,0:T(8,128)(2,1)}, bf16[4096,1024]{1,0:T(8,128)(2,1)}, f32[4096,1024]{1,0:T(8,128)}) custom-call(s32[4]{0:T(128)} %add_xor_fusion.order, bf16[4096,2048]{1,0:T(8,128)(2,1)} %all-gather.3.cloned.1.call-done.x, bf16[2048,1792]{1,0:T(8,128)(2,1)} %bitcast.6.w.refs_2_, ...), custom_call_target="tpu_custom_call" | custom-call | flops 3006477056 | bytes 4928307 | tf_op jit(solution)/shard_map/project/pallas_call | solution.py:184
  212.1 26.6 %attend.1 = (bf16[4096,256]{1,0:T(8,128)(2,1)}, f32[8,4096]{1,0:T(8,128)}) custom-call(bf16[4096,256]{1,0:T(8,128)(2,1)} %get-tuple-element.51.q, bf16[4096,256]{1,0:T(8,128)(2,1)} %get-tuple-element.52.k, bf16[4096,256]{1,0:T(8,128)(2,1)} %get-tuple-element.53.v, s32[4096,1]{1,0:T(8,128)} %bitcast.38, s32[4,1,1024]{2,1,0:T(1,128)} %reshape.134.row_ids), custom_call_target="tpu_custom_call" | custom-call | flops 2748779008 | bytes 838860 | tf_op jit(solution)/shard_map/attend/pallas_call | solution.py:499
  238.8 18.5 %mix.2 = (bf16[512,2048]{1,0:T(8,128)(2,1)}, bf16[512,2048]{1,0:T(8,128)(2,1)}) custom-call(bf16[4096,256]{1,0:T(8,128)(2,1)} %get-tuple-element.69.refs_0_.a, bf16[4096,1024]{1,0:T(8,128)(2,1)} %get-tuple-element.55.refs_1_.b, bf16[4,1280,512]{2,1,0:T(8,128)(2,1)} %copy-done.2), custom_call_target="tpu_custom_call" | custom-call | flops 1073741824 | bytes 1887436 | tf_op jit(solution)/shard_map/mix/pallas_call | solution.py:288
  263.3 88.4 %collective-permute-done.6 = bf16[512,2048]{1,0:T(8,128)(2,1)S(1)} collective-permute-done((bf16[512,2048]{1,0:T(8,128)(2,1)}, bf16[512,2048]{1,0:T(8,128)(2,1)S(1)}, u32[]{:S(2)}, u32[]{:S(2)}) %collective-permute-start.6) | collective-permute-done | bytes 2097184 | tf_op jit(solution)/shard_map/ppermute | solution.py:622
  357.5 18.6 %mix.3 = (bf16[512,2048]{1,0:T(8,128)(2,1)}, bf16[512,2048]{1,0:T(8,128)(2,1)}) custom-call(bf16[4096,256]{1,0:T(8,128)(2,1)} %get-tuple-element.69.refs_0_.a, bf16[4096,1024]{1,0:T(8,128)(2,1)} %get-tuple-element.55.refs_1_.b, bf16[4,1280,512]{2,1,0:T(8,128)(2,1)} %copy-done.2), custom_call_target="tpu_custom_call" | custom-call | flops 1073741824 | bytes 1887436 | tf_op jit(solution)/shard_map/mix/pallas_call | solution.py:288
  376.1 27.2 %collective-permute-done.9 = bf16[512,2048]{1,0:T(8,128)(2,1)} collective-permute-done((bf16[512,2048]{1,0:T(8,128)(2,1)}, bf16[512,2048]{1,0:T(8,128)(2,1)}, u32[]{:S(2)}, u32[]{:S(2)}) %collective-permute-start.9) | collective-permute-done | bytes 2097184 | tf_op jit(solution)/shard_map/ppermute | solution.py:622
  412.9 5.1 collective-permute-start.8
  417.9 37.6 %unmix.1 = (bf16[4096,256]{1,0:T(8,128)(2,1)}, bf16[4096,1024]{1,0:T(8,128)(2,1)}, f32[1,1024]{1,0:T(1,128)}) custom-call(s32[4]{0:T(128)} %add_xor_fusion.order, bf16[4096,2048]{1,0:T(8,128)(2,1)} %all-gather.5.cloned.1.call-done.g, bf16[4,1280,512]{2,1,0:T(8,128)(2,1)} %copy-done.2, f32[4096,1024]{1,0:T(8,128)} %get-tuple-element.62.hidden), custom_call_target="tpu_custom_call" | custom-call | flops 2147483648 | bytes 4718592 | tf_op jit(solution)/shard_map/unmix/pallas_call | solution.py:367
  455.5 33.2 %unattend.2 = (bf16[2048,768]{1,0:T(8,128)(2,1)}, f32[1,768]{1,0:T(1,128)}) custom-call(bf16[4096,256]{1,0:T(8,128)(2,1)} %get-tuple-element.51.q, bf16[4096,256]{1,0:T(8,128)(2,1)} %get-tuple-element.52.k, bf16[4096,256]{1,0:T(8,128)(2,1)} %get-tuple-element.53.v, bf16[4096,256]{1,0:T(8,128)(2,1)} %get-tuple-element.70.g, ...), custom_call_target="tpu_custom_call" | custom-call | flops 3435973888 | bytes 734003 | tf_op jit(solution)/shard_map/unattend/pallas_call | solution.py:574
  488.7 23.7 %unproject.2 = (bf16[512,2048]{1,0:T(8,128)(2,1)}, bf16[512,2048]{1,0:T(8,128)(2,1)}) custom-call(bf16[2048,768]{1,0:T(8,128)(2,1)} %get-tuple-element.66.refs_0_, bf16[4096,1024]{1,0:T(8,128)(2,1)} %get-tuple-element.85.refs_1_.refs_0_, bf16[2048,1792]{1,0:T(8,128)(2,1)} %bitcast.6.w.refs_2_), custom_call_target="tpu_custom_call" | custom-call | flops 1503238528 | bytes 2306867 | tf_op jit(solution)/shard_map/unproject/pallas_call | solution.py:288
  515.8 29.6 %outer_columns.1 = bf16[4,1280,512]{2,1,0:T(8,128)(2,1)} custom-call(s32[4]{0:T(128)} %add_xor_fusion.order, bf16[4096,256]{1,0:T(8,128)(2,1)} %get-tuple-element.69.refs_0_.a, bf16[4096,1024]{1,0:T(8,128)(2,1)} %get-tuple-element.55.refs_1_.b, bf16[4096,2048]{1,0:T(8,128)(2,1)} %all-gather.5.cloned.1.call-done.g), custom_call_target="tpu_custom_call" | custom-call | flops 2147483648 | bytes 3250585 | tf_op jit(solution)/shard_map/outer_columns/pallas_call | solution.py:437
  545.4 6.0 add_convert_fusion.3
  551.4 33.1 %unattend.3 = (bf16[2048,768]{1,0:T(8,128)(2,1)}, f32[1,768]{1,0:T(1,128)}) custom-call(bf16[4096,256]{1,0:T(8,128)(2,1)} %get-tuple-element.51.q, bf16[4096,256]{1,0:T(8,128)(2,1)} %get-tuple-element.52.k, bf16[4096,256]{1,0:T(8,128)(2,1)} %get-tuple-element.53.v, bf16[4096,256]{1,0:T(8,128)(2,1)} %get-tuple-element.70.g, ...), custom_call_target="tpu_custom_call" | custom-call | flops 3435973888 | bytes 734003 | tf_op jit(solution)/shard_map/unattend/pallas_call | solution.py:574
  588.4 23.9 %unproject.3 = (bf16[512,2048]{1,0:T(8,128)(2,1)}, bf16[512,2048]{1,0:T(8,128)(2,1)}) custom-call(bf16[2048,768]{1,0:T(8,128)(2,1)} %get-tuple-element.71.refs_0_.refs_1_, bf16[4096,1024]{1,0:T(8,128)(2,1)} %get-tuple-element.85.refs_1_.refs_0_, bf16[2048,1792]{1,0:T(8,128)(2,1)} %bitcast.6.w.refs_2_), custom_call_target="tpu_custom_call" | custom-call | flops 1503238528 | bytes 2306867 | tf_op jit(solution)/shard_map/unproject/pallas_call | solution.py:288
  612.3 19.6 %outer_rows.2 = bf16[2048,768]{1,0:T(8,128)(2,1)} custom-call(s32[4]{0:T(128)} %add_xor_fusion.order, bf16[4096,2048]{1,0:T(8,128)(2,1)} %all-gather.3.cloned.1.call-done.x, bf16[2048,768]{1,0:T(8,128)(2,1)} %get-tuple-element.66.refs_0_, bf16[2048,768]{1,0:T(8,128)(2,1)} %get-tuple-element.71.refs_0_.refs_1_), custom_call_target="tpu_custom_call" | custom-call | flops 1288490240 | bytes 2621440 | tf_op jit(solution)/shard_map/outer_rows/pallas_call | solution.py:406
  635.2 44.7 %collective-permute-done.14 = bf16[512,2048]{1,0:T(8,128)(2,1)S(1)} collective-permute-done((bf16[512,2048]{1,0:T(8,128)(2,1)}, bf16[512,2048]{1,0:T(8,128)(2,1)S(1)}, u32[]{:S(2)}, u32[]{:S(2)}) %collective-permute-start.14) | collective-permute-done | bytes 2097184 | tf_op jit(solution)/shard_map/ppermute | solution.py:622
  684.2 24.5 %outer_rows.3 = bf16[2048,1024]{1,0:T(8,128)(2,1)} custom-call(s32[4]{0:T(128)} %add_xor_fusion.order, bf16[4096,2048]{1,0:T(8,128)(2,1)} %all-gather.3.cloned.1.call-done.x, bf16[4096,1024]{1,0:T(8,128)(2,1)} %get-tuple-element.85.refs_1_.refs_0_), custom_call_target="tpu_custom_call" | custom-call | flops 1717986944 | bytes 2936012 | tf_op jit(solution)/shard_map/outer_rows/pallas_call | solution.py:406
  714.9 44.4 %collective-permute-done.13.refs_1_ = bf16[512,2048]{1,0:T(8,128)(2,1)} collective-permute-done((bf16[512,2048]{1,0:T(8,128)(2,1)}, bf16[512,2048]{1,0:T(8,128)(2,1)}, u32[]{:S(2)}, u32[]{:S(2)}) %collective-permute-start.13) | collective-permute-done | bytes 2097184 | tf_op jit(solution)/shard_map/ppermute | solution.py:622
  759.3 8.2 %unnorm.1 = (bf16[512,2048]{1,0:T(8,128)(2,1)}, f32[1,2048]{1,0:T(1,128)}, f32[1,2048]{1,0:T(1,128)}) custom-call(bf16[512,2048]{1,0:T(8,128)(2,1)} %x.3, bf16[512,2048]{1,0:T(8,128)(2,1)} %g.1, f32[1,2048]{1,0:T(1,128)} %bitcast.43, bf16[512,2048]{1,0:T(8,128)(2,1)} %get-tuple-element.74.refs_0_, bf16[512,2048]{1,0:T(8,128)(2,1)} %collective-permute-done.13.refs_1_, ...), custom_call_target="tpu_custom_call" | custom-call | flops 3145728 | bytes 1258291 | tf_op jit(solution)/shard_map/unnorm/pallas_call | solution.py:142
  767.5 14.4 %sum_everywhere.1 = (f32[8,2048]{1,0:T(8,128)}, f32[1,1792]{1,0:T(1,128)}) custom-call(f32[1,2048]{1,0:T(1,128)} %get-tuple-element.77.gain, f32[1,2048]{1,0:T(1,128)} %get-tuple-element.78.shift, f32[1,2048]{1,0:T(1,128)} %bitcast.46, f32[1,768]{1,0:T(1,128)} %add.111.qkv, f32[1,1024]{1,0:T(1,128)} %get-tuple-element.81.up), custom_call_target="tpu_custom_call" | custom-call | tf_op jit(solution)/shard_map/sum_everywhere/pallas_call | solution.py:702
  (146 shorter events, 107.1 us)
Async XLA Ops:
  7.2 163.0 %all-gather.3.cloned.1.call-start = ((), (), s32[]{:S(2)}) async-start(), calls=%async_computation.3 | async-start | bytes 18874368 | tf_op jit(solution)/shard_map/all_gather | solution.py:757
  14.4 403.5 %all-gather.5.cloned.1.call-start = ((), (), s32[]{:S(2)}) async-start(), calls=%async_computation.4 | async-start | bytes 18874368 | tf_op jit(solution)/shard_map/all_gather | solution.py:758
  15.2 770.8 %reduce-scatter.6.cloned.1.call-start = ((), (), s32[]{:S(2)}) async-start(), calls=%async_computation.5 | async-start | bytes 3932160 | tf_op jit(solution)/shard_map/reduce_scatter | solution.py:848
  18.5 143.2 %collective-permute-start = (bf16[512,1792]{1,0:T(8,128)(2,1)}, bf16[512,1792]{1,0:T(8,128)(2,1)}, u32[]{:S(2)}, u32[]{:S(2)}) collective-permute-start(bf16[512,1792]{1,0:T(8,128)(2,1)} %constant_dynamic-update-slice_fusion), channel_id=1, source_target_pairs={{0,8},{8,0},{16,24},{24,16},{1,9},{9,1},{17,25},{25,17},{2,10},{10... | collective-permute-start | bytes 5505032 | tf_op jit(solution)/shard_map/ppermute | solution.py:614
  21.5 144.5 %collective-permute-start.1 = (bf16[512,1792]{1,0:T(8,128)(2,1)}, bf16[512,1792]{1,0:T(8,128)(2,1)}, u32[]{:S(2)}, u32[]{:S(2)}) collective-permute-start(bf16[512,1792]{1,0:T(8,128)(2,1)} %constant_dynamic-update-slice_fusion), channel_id=1, source_target_pairs={{0,16},{8,24},{16,0},{24,8},{1,17},{9,25},{17,1},{25,9},{2,18},{10... | collective-permute-start | bytes 5505032 | tf_op jit(solution)/shard_map/ppermute | solution.py:614
  24.7 66.0 %collective-permute-start.3 = (bf16[1280,512]{1,0:T(8,128)(2,1)}, bf16[1280,512]{1,0:T(8,128)(2,1)}, u32[]{:S(2)}, u32[]{:S(2)}) collective-permute-start(bf16[1280,512]{1,0:T(8,128)(2,1)} %constant_dynamic-update-slice_fusion.4), channel_id=1, source_target_pairs={{0,8},{8,0},{16,24},{24,16},{1,9},{9,1},{17,25},{25,17},{2,10},{10... | collective-permute-start | bytes 3932168 | tf_op jit(solution)/shard_map/ppermute | solution.py:614
  25.3 133.5 %collective-permute-start.4 = (bf16[1280,512]{1,0:T(8,128)(2,1)}, bf16[1280,512]{1,0:T(8,128)(2,1)}, u32[]{:S(2)}, u32[]{:S(2)}) collective-permute-start(bf16[1280,512]{1,0:T(8,128)(2,1)} %constant_dynamic-update-slice_fusion.4), channel_id=1, source_target_pairs={{0,16},{8,24},{16,0},{24,8},{1,17},{9,25},{17,1},{25,9},{2,18},{10... | collective-permute-start | bytes 3932168 | tf_op jit(solution)/shard_map/ppermute | solution.py:614
  25.3 134.9 %collective-permute-start.5 = (bf16[1280,512]{1,0:T(8,128)(2,1)}, bf16[1280,512]{1,0:T(8,128)(2,1)}, u32[]{:S(2)}, u32[]{:S(2)}) collective-permute-start(bf16[1280,512]{1,0:T(8,128)(2,1)} %constant_dynamic-update-slice_fusion.4), channel_id=1, source_target_pairs={{0,24},{8,16},{16,8},{24,0},{1,25},{9,17},{17,9},{25,1},{2,26},{10... | collective-permute-start | bytes 3932168 | tf_op jit(solution)/shard_map/ppermute | solution.py:614
  90.7 78.1 %collective-permute-start.2 = (bf16[512,1792]{1,0:T(8,128)(2,1)}, bf16[512,1792]{1,0:T(8,128)(2,1)S(1)}, u32[]{:S(2)}, u32[]{:S(2)}) collective-permute-start(bf16[512,1792]{1,0:T(8,128)(2,1)} %constant_dynamic-update-slice_fusion), channel_id=1, source_target_pairs={{0,24},{8,16},{16,8},{24,0},{1,25},{9,17},{17,9},{25,1},{2,26},{10... | collective-permute-start | bytes 5505032 | tf_op jit(solution)/shard_map/ppermute | solution.py:614
  257.2 94.5 %collective-permute-start.6 = (bf16[512,2048]{1,0:T(8,128)(2,1)}, bf16[512,2048]{1,0:T(8,128)(2,1)S(1)}, u32[]{:S(2)}, u32[]{:S(2)}) collective-permute-start(bf16[512,2048]{1,0:T(8,128)(2,1)} %get-tuple-element.56), channel_id=1, source_target_pairs={{0,2},{1,3},{6,4},{7,5},{8,10},{9,11},{14,12},{15,13},{16,18},{17,... | collective-permute-start | bytes 6291464 | tf_op jit(solution)/shard_map/ppermute | solution.py:622
  260.6 142.7 %collective-permute-start.9 = (bf16[512,2048]{1,0:T(8,128)(2,1)}, bf16[512,2048]{1,0:T(8,128)(2,1)}, u32[]{:S(2)}, u32[]{:S(2)}) collective-permute-start(bf16[512,2048]{1,0:T(8,128)(2,1)} %get-tuple-element.60), channel_id=1, source_target_pairs={{0,2},{1,3},{6,4},{7,5},{8,10},{9,11},{14,12},{15,13},{16,18},{17,... | collective-permute-start | bytes 6291464 | tf_op jit(solution)/shard_map/ppermute | solution.py:622
  355.4 48.0 %copy-start.8 = (bf16[512,2048]{1,0:T(8,128)(2,1)S(1)}, bf16[512,2048]{1,0:T(8,128)(2,1)}, u32[]{:S(2)}) copy-start(bf16[512,2048]{1,0:T(8,128)(2,1)} %get-tuple-element.56) | copy-start | bytes 6291460
  355.4 53.8 %collective-permute-start.7 = (bf16[512,2048]{1,0:T(8,128)(2,1)}, bf16[512,2048]{1,0:T(8,128)(2,1)}, u32[]{:S(2)}, u32[]{:S(2)}) collective-permute-start(bf16[512,2048]{1,0:T(8,128)(2,1)} %add_convert_fusion.6), channel_id=1, source_target_pairs={{2,4},{3,5},{4,2},{5,3},{10,12},{11,13},{12,10},{13,11},{18,20},{1... | collective-permute-start | bytes 6291464 | tf_op jit(solution)/shard_map/ppermute | solution.py:622
  407.2 138.2 %collective-permute-start.10 = (bf16[512,2048]{1,0:T(8,128)(2,1)}, bf16[512,2048]{1,0:T(8,128)(2,1)}, u32[]{:S(2)}, u32[]{:S(2)}) collective-permute-start(bf16[512,2048]{1,0:T(8,128)(2,1)} %add_convert_fusion.4), channel_id=1, source_target_pairs={{2,4},{3,5},{4,2},{5,3},{10,12},{11,13},{12,10},{13,11},{18,20},{1... | collective-permute-start | bytes 6291464 | tf_op jit(solution)/shard_map/ppermute | solution.py:622
  412.9 132.5 %collective-permute-start.8 = (bf16[512,2048]{1,0:T(8,128)(2,1)}, bf16[512,2048]{1,0:T(8,128)(2,1)}, u32[]{:S(2)}, u32[]{:S(2)}) collective-permute-start(bf16[512,2048]{1,0:T(8,128)(2,1)} %add_convert_fusion.5), channel_id=1, source_target_pairs={{0,2},{1,3},{2,0},{3,1},{4,6},{5,7},{6,4},{7,5},{8,10},{9,11},{10,... | collective-permute-start | bytes 6291464 | tf_op jit(solution)/shard_map/ppermute | solution.py:622
  512.5 72.0 %collective-permute-start.11 = (bf16[512,2048]{1,0:T(8,128)(2,1)}, bf16[512,2048]{1,0:T(8,128)(2,1)}, u32[]{:S(2)}, u32[]{:S(2)}) collective-permute-start(bf16[512,2048]{1,0:T(8,128)(2,1)} %get-tuple-element.68), channel_id=1, source_target_pairs={{0,2},{1,3},{6,4},{7,5},{8,10},{9,11},{14,12},{15,13},{16,18},{17,... | collective-permute-start | bytes 6291464 | tf_op jit(solution)/shard_map/ppermute | solution.py:622
  631.9 48.0 %copy-start.5 = (bf16[512,2048]{1,0:T(8,128)(2,1)S(1)}, bf16[512,2048]{1,0:T(8,128)(2,1)}, u32[]{:S(2)}) copy-start(bf16[512,2048]{1,0:T(8,128)(2,1)} %get-tuple-element.68) | copy-start | bytes 6291460
  631.9 156.3 %reduce-scatter.10.cloned.1.call-start = ((), (), s32[]{:S(2)}) async-start(), calls=%async_computation.7 | async-start | bytes 6553600
  632.5 163.1 %reduce-scatter.8.cloned.1.call-start = ((), (), s32[]{:S(2)}) async-start(), calls=%async_computation.6 | async-start | bytes 5242880 | tf_op jit(solution)/shard_map/reduce_scatter | solution.py:849
  632.6 49.5 %copy-start.7 = (bf16[512,2048]{1,0:T(8,128)(2,1)S(1)}, bf16[512,2048]{1,0:T(8,128)(2,1)}, u32[]{:S(2)}) copy-start(bf16[512,2048]{1,0:T(8,128)(2,1)} %get-tuple-element.75) | copy-start | bytes 6291460
  632.6 47.4 %collective-permute-start.14 = (bf16[512,2048]{1,0:T(8,128)(2,1)}, bf16[512,2048]{1,0:T(8,128)(2,1)S(1)}, u32[]{:S(2)}, u32[]{:S(2)}) collective-permute-start(bf16[512,2048]{1,0:T(8,128)(2,1)} %get-tuple-element.72), channel_id=1, source_target_pairs={{0,2},{1,3},{6,4},{7,5},{8,10},{9,11},{14,12},{15,13},{16,18},{17,... | collective-permute-start | bytes 6291464 | tf_op jit(solution)/shard_map/ppermute | solution.py:622
  634.1 47.9 %collective-permute-start.12 = (bf16[512,2048]{1,0:T(8,128)(2,1)}, bf16[512,2048]{1,0:T(8,128)(2,1)S(1)}, u32[]{:S(2)}, u32[]{:S(2)}) collective-permute-start(bf16[512,2048]{1,0:T(8,128)(2,1)} %add_convert_fusion.2), channel_id=1, source_target_pairs={{2,4},{3,5},{4,2},{5,3},{10,12},{11,13},{12,10},{13,11},{18,20},{1... | collective-permute-start | bytes 6291464 | tf_op jit(solution)/shard_map/ppermute | solution.py:622
  708.7 6.2 collective-permute-start.15
  710.8 48.5 %collective-permute-start.13 = (bf16[512,2048]{1,0:T(8,128)(2,1)}, bf16[512,2048]{1,0:T(8,128)(2,1)}, u32[]{:S(2)}, u32[]{:S(2)}) collective-permute-start(bf16[512,2048]{1,0:T(8,128)(2,1)} %add_convert_fusion.1), channel_id=1, source_target_pairs={{0,2},{1,3},{2,0},{3,1},{4,6},{5,7},{6,4},{7,5},{8,10},{9,11},{10,... | collective-permute-start | bytes 6291464 | tf_op jit(solution)/shard_map/ppermute | solution.py:622
  (22 other events, 289.2 us)
Sparse Core Ops, SparseCore 0:
  14.5 153.7 all-gather.2
  169.9 195.4 all-gather.4
  632.1 42.4 reduce-scatter.5
  677.4 61.4 reduce-scatter.9
  741.6 53.9 reduce-scatter.7

commit v3 on v2

--- a/solution.py
+++ b/solution.py
@@ -107,8 +107,8 @@
     )(x, gain, shift)
 
 
-def unnorm_kernel(terms, x, g, gain, *refs):
-    parts, (out, gain_sum, shift_sum) = refs[:terms], refs[terms:]
+def unnorm_kernel(terms, skipped, flag, x, g, gain, *refs):
+    parts, (out, gain_sum, shift_sum) = refs[:terms], refs[terms + skipped :]
 
     @pl.when(pl.program_id(0) == 0)
     def _():
@@ -121,7 +121,10 @@
     hat = centered * scale
     back = parts[0][...].astype(F32)
     for part in parts[1:]:
-        back = back + part[...].astype(F32)
+        term = part[...].astype(F32)
+        if part is parts[-1]:
+            term = jnp.where(flag[0] == 1, term, 0.0)
+        back = back + term
     gain_sum[...] += jnp.sum(back * hat, axis=0, keepdims=True)
     shift_sum[...] += jnp.sum(back, axis=0, keepdims=True)
     e = back * gain[...]
@@ -131,31 +134,330 @@
     out[...] = (g[...].astype(F32) + inner * scale).astype(BF16)
 
 
-def unnorm(x, g, gain, parts, tile=128):
+def unnorm(flag, x, g, gain, parts, wait_for=(), tile=128):
     rows, depth = x.shape
-    row = pl.BlockSpec((tile, depth), lambda i: (i, 0))
-    one = once((1, depth), lambda i: (0, 0))
-    late = [
-        pl.BlockSpec((tile, depth), lambda i, o=o: (i + o // tile, 0)) for _, o in parts
-    ]
-    total = pl.BlockSpec((1, depth), lambda i: (0, 0))
+    row = pl.BlockSpec((tile, depth), lambda i, f: (i, 0))
+    one = once((1, depth), lambda i, f: (0, 0))
+    total = pl.BlockSpec((1, depth), lambda i, f: (0, 0))
     return pl.pallas_call(
-        functools.partial(unnorm_kernel, len(parts)),
-        grid=(rows // tile,),
-        in_specs=[row, row, one] + late,
-        out_specs=[row, total, total],
+        functools.partial(unnorm_kernel, len(parts), len(wait_for)),
+        grid_spec=pltpu.PrefetchScalarGridSpec(
+            num_scalar_prefetch=1,
+            grid=(rows // tile,),
+            in_specs=[row, row, one] + [row] * len(parts) + [ANYWHERE] * len(wait_for),
+            out_specs=[row, total, total],
+        ),
         out_shape=[
             jax.ShapeDtypeStruct((rows, depth), BF16),
             jax.ShapeDtypeStruct((1, depth), F32),
             jax.ShapeDtypeStruct((1, depth), F32),
         ],
         compiler_params=params(("arbitrary",)),
-        cost_estimate=cost(30 * rows * depth, (6 + 2 * len(parts)) * rows * depth),
+        cost_estimate=cost(30 * rows * depth, 14 * rows * depth),
         name="unnorm",
-    )(x, g, gain, *(p for p, _ in parts))
-
-
-def project_kernel(width, order, x, w, bias, cos, low, high, q, k, v, active, hidden):
+    )(flag, x, g, gain, *parts, *wait_for)
+
+
+MESH = pl.DeviceIdType.MESH
+ANYWHERE = pl.BlockSpec(memory_space=pl.ANY)
+
+
+def places():
+    me = lax.axis_index("tensor")
+    core, chip = lax.rem(me, 2), lax.div(me, 2)
+    beside = chip + 1 - 2 * lax.rem(chip, 2)
+    inner = jnp.logical_or(chip == 1, chip == 2)
+    return dict(
+        core=core,
+        partner=me + 1 - 2 * core,
+        beside=2 * beside + core,
+        opposite=2 * (3 - chip) + core,
+        inner=inner,
+        outer=jnp.logical_not(inner),
+        all=None,
+    )
+
+
+def greet(at, others=()):
+    barrier = pltpu.get_barrier_semaphore()
+    ids = [{"tensor": at[name]} for name in ("partner", "beside", "opposite")] + list(others)
+    for device in ids:
+        pl.semaphore_signal(barrier, inc=1, device_id=device, device_id_type=MESH)
+    pl.semaphore_wait(barrier, len(ids))
+
+
+def to_device(src, dst, sent, got, device):
+    return pltpu.make_async_remote_copy(
+        src_ref=src,
+        dst_ref=dst,
+        send_sem=sent,
+        recv_sem=got,
+        device_id=device,
+        device_id_type=MESH,
+    )
+
+
+def under(condition, act):
+    if condition is None:
+        act()
+    else:
+        pl.when(condition)(act)
+
+
+def start_all(at, copies):
+    for sender, _, copy in copies:
+        under(at[sender], copy.start)
+
+
+def finish_all(at, copies):
+    for sender, receiver, copy in copies:
+        under(at[receiver], copy.wait_recv)
+        under(at[sender], copy.wait_send)
+
+
+class Gather:
+    MOVES = {
+        1: (("all", "all", 3, 2, "beside"), ("inner", "inner", 3, 0, "opposite")),
+        2: (("inner", "inner", 2, 1, "opposite"), ("inner", "outer", 0, 1, "beside")),
+        3: (("inner", "outer", 1, 0, "beside"),),
+        "own": (("all", "all", 3, 3, "partner"),),
+        "first": (("all", "all", 2, 2, "partner"), ("inner", "inner", 0, 0, "partner")),
+        "second": (("all", "all", 1, 1, "partner"),),
+        "third": (("outer", "outer", 0, 0, "partner"),),
+    }
+
+    def __init__(self, *moves):
+        self.moves = [(m, lo, hi) for name, lo, hi in moves for m in self.MOVES[name]]
+        self.count = len(self.moves)
+
+    def copies(self, at, full, sent, got):
+        found = []
+        for i, ((sender, receiver, src, dst, target), lo, hi) in enumerate(self.moves):
+            rows = pl.ds(lo, hi - lo)
+            found.append(
+                (
+                    sender,
+                    receiver,
+                    to_device(
+                        full.at[src, at["core"], rows],
+                        full.at[dst, at["core"], rows],
+                        sent.at[i],
+                        got.at[i],
+                        {"tensor": at[target]},
+                    ),
+                )
+            )
+        return found
+
+
+class Riding:
+    def __init__(self, ins, outs, aliased, count, copies):
+        self.ins, self.outs, self.aliased, self.count, self.copies = ins, outs, aliased, count, copies
+
+
+def like(array):
+    return jax.ShapeDtypeStruct(array.shape, array.dtype)
+
+
+def gathering(full, *moves):
+    plan = Gather(*moves)
+
+    def copies(at, ins, outs, sent, got):
+        return plan.copies(at, outs[0], sent, got)
+
+    return Riding([full], [like(full)], True, plan.count, copies)
+
+
+SENDS = {
+    "in": ("outer", "inner", "beside"),
+    "middle": ("inner", "inner", "opposite"),
+    "side": ("all", "all", "beside"),
+}
+
+
+def sending(values, kind, lo, hi, into=None):
+    sender, receiver, target = SENDS[kind]
+
+    def copies(at, ins, outs, sent, got):
+        rows = pl.ds(lo, hi - lo)
+        copy = to_device(
+            ins[0].at[rows], outs[0].at[rows], sent.at[0], got.at[0], {"tensor": at[target]}
+        )
+        return [(sender, receiver, copy)]
+
+    return Riding([values] + ([] if into is None else [into]), [like(values)], into is not None, 1, copies)
+
+
+def launch(body, args, ins, outs, shapes, grid, name, estimate, scratch=(), riding=(), ident=None, place=False, wait_for=()):
+    if ident is None:
+        return pl.pallas_call(
+            body,
+            grid=(grid,),
+            in_specs=ins,
+            out_specs=outs,
+            out_shape=shapes,
+            scratch_shapes=list(scratch),
+            compiler_params=params(("arbitrary",)),
+            cost_estimate=estimate,
+            name=name,
+        )(*args)
+    riding = list(riding) + [Riding([a], [], False, 1, lambda *_: []) for a in wait_for]
+    extra_in = [a for r in riding for a in r.ins]
+    extra_out = [o for r in riding for o in r.outs]
+    aliases, n_in, n_out = {}, len(args), len(shapes)
+    for r in riding:
+        if r.aliased:
+            aliases[n_in + len(r.ins) - 1] = n_out
+        n_in, n_out = n_in + len(r.ins), n_out + len(r.outs)
+
+    def kernel(*refs):
+        take = iter(refs)
+        some = lambda n: [next(take) for _ in range(n)]
+        own_ins, ride_ins = some(len(args)), [some(len(r.ins)) for r in riding]
+        own_outs, ride_outs = some(len(shapes)), [some(len(r.outs)) for r in riding]
+        own_scratch = some(len(scratch))
+        at = places()
+        copies = []
+        for r, i, o in zip(riding, ride_ins, ride_outs):
+            copies += r.copies(at, i, o, *some(2))
+
+        @pl.when(pl.program_id(0) == 0)
+        def _():
+            greet(at)
+            start_all(at, copies)
+
+        body(*([at] if place else []), *own_ins, *own_outs, *own_scratch)
+
+        @pl.when(pl.program_id(0) == grid - 1)
+        def _():
+            finish_all(at, copies)
+
+    return pl.pallas_call(
+        kernel,
+        grid=(grid,),
+        in_specs=ins + [ANYWHERE] * len(extra_in),
+        out_specs=outs + [ANYWHERE] * len(extra_out),
+        out_shape=shapes + extra_out,
+        input_output_aliases=aliases,
+        scratch_shapes=list(scratch)
+        + [pltpu.SemaphoreType.DMA((r.count,)) for r in riding for _ in range(2)],
+        compiler_params=pltpu.CompilerParams(
+            dimension_semantics=("arbitrary",),
+            vmem_limit_bytes=VMEM_BYTES,
+            collective_id=ident,
+            has_side_effects=True,
+        ),
+        cost_estimate=estimate,
+        name=name,
+    )(*args, *extra_in)
+
+
+def gather_kernel(tile, groups, x, gain, shift, g, first, second, rows_full, g_full, first_full, second_full, own, kept, first_kept, second_kept, local, w_sent, w_got, *sems):
+    at = places()
+    dp = lax.axis_index("dp")
+    peers = [{"dp": jnp.bitwise_xor(dp, step)} for step in range(1, groups)]
+    greet(at, peers)
+    loads = [
+        pltpu.make_async_copy(src, dst, local.at[i])
+        for i, (src, dst) in enumerate(((first, first_kept), (second, second_kept), (g, kept)))
+    ]
+    stores = [
+        pltpu.make_async_copy(src, dst, local.at[i])
+        for i, (src, dst) in enumerate(
+            (
+                (first_kept, first_full.at[dp]),
+                (second_kept, second_full.at[dp]),
+                (kept, g_full.at[3, at["core"]]),
+                (own, rows_full.at[3, at["core"]]),
+            )
+        )
+    ]
+    weights = [
+        [to_device(src, dst.at[dp], w_sent.at[k, i], w_got.at[k, i], peer) for i, peer in enumerate(peers)]
+        for k, (src, dst) in enumerate(((first, first_full), (second, second_full)))
+    ]
+    for copy in loads + weights[0]:
+        copy.start()
+    share = own.shape[0]
+
+    @pl.loop(0, share // tile)
+    def _(i):
+        rows = pl.ds(pl.multiple_of(i * tile, tile), tile)
+        values = x[rows, :].astype(F32)
+        centered = values - jnp.mean(values, axis=1, keepdims=True)
+        scale = lax.rsqrt(jnp.mean(centered * centered, axis=1, keepdims=True) + EPS)
+        own[rows, :] = (centered * scale * gain[...] + shift[...]).astype(BF16)
+
+    stores[3].start()
+    for load, store in zip(loads, stores):
+        load.wait()
+        store.start()
+    stores[3].wait()
+    half = share // 2
+    lows, highs = (0, half), (half, share)
+    plans = [
+        Gather((1, *lows)),
+        Gather((1, *highs), ("own", 0, share)),
+        Gather((2, *lows), ("first", *lows)),
+        Gather((2, *highs), ("first", *highs)),
+        Gather((3, *lows), ("second", *lows)),
+        Gather((3, *highs), ("second", *highs)),
+        Gather(("third", *lows)),
+        Gather(("third", *highs)),
+    ]
+    moves = [p.copies(at, rows_full, sems[2 * i], sems[2 * i + 1]) for i, p in enumerate(plans)]
+    mine = Gather(("own", 0, share)).copies(at, g_full, sems[16], sems[17])
+    start_all(at, moves[0])
+    start_all(at, moves[1])
+    for store in stores[:3]:
+        store.wait()
+    start_all(at, mine)
+    for copy in weights[1]:
+        copy.start()
+    for i in range(6):
+        finish_all(at, moves[i])
+        start_all(at, moves[i + 2])
+    finish_all(at, moves[6])
+    finish_all(at, moves[7])
+    finish_all(at, mine)
+    for copy in weights[0] + weights[1]:
+        copy.wait()
+
+
+def gather(ident, x, gain, shift, g, first, second, groups, tile=64):
+    rows, depth = x.shape
+    whole = pl.BlockSpec(memory_space=pltpu.VMEM)
+    full = jax.ShapeDtypeStruct((4, 2, rows, depth), BF16)
+    sizes = [2, 3, 4, 4, 2, 2, 1, 1, 1]
+    return pl.pallas_call(
+        functools.partial(gather_kernel, tile, groups),
+        in_specs=[whole] * 3 + [ANYWHERE] * 3,
+        out_specs=[ANYWHERE] * 4,
+        out_shape=[
+            full,
+            full,
+            jax.ShapeDtypeStruct((groups,) + first.shape, BF16),
+            jax.ShapeDtypeStruct((groups,) + second.shape, BF16),
+        ],
+        scratch_shapes=[
+            pltpu.VMEM((rows, depth), BF16),
+            pltpu.VMEM((rows, depth), BF16),
+            pltpu.VMEM(first.shape, BF16),
+            pltpu.VMEM(second.shape, BF16),
+            pltpu.SemaphoreType.DMA((4,)),
+            pltpu.SemaphoreType.DMA((2, groups - 1)),
+            pltpu.SemaphoreType.DMA((2, groups - 1)),
+        ]
+        + [pltpu.SemaphoreType.DMA((n,)) for n in sizes for _ in range(2)],
+        compiler_params=pltpu.CompilerParams(
+            vmem_limit_bytes=VMEM_BYTES, collective_id=ident, has_side_effects=True
+        ),
+        cost_estimate=cost(10 * rows * depth, 60 * rows * depth),
+        name="gather",
+    )(x, gain, shift, g, first, second)
+
+
+def project_tile(width, x, w, bias, cos, low, high, q, k, v, active, hidden):
     rows = x[...]
     tables = (cos[...], low[...], high[...])
     q[...] = (
@@ -175,38 +477,32 @@
         active[:, start : start + step] = gelu(h).astype(BF16)
 
 
-def project(order, x, w, bias, tables, width, units, length, tile=512):
+def project(x, w, bias, tables, width, units, length, riding=(), ident=None, tile=512):
     rows, depth = x.shape
     per = length // tile
-    row = lambda n: pl.BlockSpec((tile, n), lambda i, o: (i, 0))
-    table = pl.BlockSpec((tile, 128), lambda i, o: (i % per, 0))
+    row = lambda n: pl.BlockSpec((tile, n), lambda i: (i, 0))
+    table = pl.BlockSpec((tile, 128), lambda i: (i % per, 0))
     total = 3 * width + units
-    return pl.pallas_call(
-        functools.partial(project_kernel, width),
-        grid_spec=pltpu.PrefetchScalarGridSpec(
-            num_scalar_prefetch=1,
-            grid=(rows // tile,),
-            in_specs=[
-                pl.BlockSpec((tile, depth), lambda i, o: (o[i // per] * per + i % per, 0)),
-                once((depth, total), lambda i, o: (0, 0)),
-                once((1, total), lambda i, o: (0, 0)),
-                table,
-                table,
-                table,
-            ],
-            out_specs=[row(width), row(width), row(width), row(units), row(units)],
-        ),
-        out_shape=[
-            jax.ShapeDtypeStruct((rows, width), BF16),
-            jax.ShapeDtypeStruct((rows, width), BF16),
-            jax.ShapeDtypeStruct((rows, width), BF16),
-            jax.ShapeDtypeStruct((rows, units), BF16),
-            jax.ShapeDtypeStruct((rows, units), F32),
+    return launch(
+        functools.partial(project_tile, width),
+        [x, w, bias, *tables],
+        [
+            row(depth),
+            once((depth, total), lambda i: (0, 0)),
+            once((1, total), lambda i: (0, 0)),
+            table,
+            table,
+            table,
         ],
-        compiler_params=params(("arbitrary",)),
-        cost_estimate=cost(2 * rows * depth * total, 2 * depth * (rows + total) + rows * units * 6),
-        name="project",
-    )(order, x, w, bias, *tables)
+        [row(width), row(width), row(width), row(units), row(units)],
+        [jax.ShapeDtypeStruct((rows, width), BF16)] * 3
+        + [jax.ShapeDtypeStruct((rows, units), BF16), jax.ShapeDtypeStruct((rows, units), F32)],
+        rows // tile,
+        "project",
+        cost(2 * rows * depth * total, 2 * depth * (rows + total) + rows * units * 6),
+        riding=riding,
+        ident=ident,
+    )
 
 
 def each_tile_kernel(body, *refs):
@@ -228,90 +524,70 @@
     )(*arrays, w)
 
 
-def core_sum_kernel(body, count, pieces, *refs):
-    ins, outs, (w, sent, got, value, send_sem, got_sem) = (
-        refs[: -count - 6],
-        refs[-count - 5 : -5],
-        (refs[-count - 6],) + refs[-5:],
-    )
+def core_sum_body(body, count, pieces, n_in, at, *refs):
+    ins, w, outs = refs[:n_in], refs[n_in], refs[n_in + 1 : n_in + 1 + count]
+    sent, got, value, send_sem, got_sem = refs[n_in + 1 + count :]
     slot = pl.program_id(0)
-    me = lax.axis_index("tensor")
-    core = lax.rem(me, 2)
-    partner = me + 1 - 2 * core
+    core = at["core"]
     share = sent.shape[1]
     piece = share // pieces
-
-    @pl.when(slot == 0)
-    def _():
-        barrier = pltpu.get_barrier_semaphore()
-        pl.semaphore_signal(
-            barrier, inc=1, device_id={"tensor": partner}, device_id_type=pl.DeviceIdType.MESH
-        )
-        pl.semaphore_wait(barrier, 1)
 
     def term(owner, i, to):
         rows = pl.ds(pl.multiple_of(owner * share + i * piece, piece), piece)
         body(*(r.at[rows, :] for r in ins), w, to)
 
     def copy(i):
-        at = pl.ds(i * piece, piece)
-        return pltpu.make_async_remote_copy(
-            src_ref=sent.at[slot, at],
-            dst_ref=got.at[slot, at],
-            send_sem=send_sem.at[slot, i],
-            recv_sem=got_sem.at[slot, i],
-            device_id={"tensor": partner},
-            device_id_type=pl.DeviceIdType.MESH,
+        rows = pl.ds(i * piece, piece)
+        return to_device(
+            sent.at[slot, rows],
+            got.at[slot, rows],
+            send_sem.at[slot, i],
+            got_sem.at[slot, i],
+            {"tensor": at["partner"]},
         )
 
     for i in range(pieces):
         term(1 - core, i, sent.at[slot, pl.ds(i * piece, piece)])
         copy(i).start()
     for i in range(pieces):
-        at = pl.ds(i * piece, piece)
+        rows = pl.ds(i * piece, piece)
         term(core, i, value)
         copy(i).wait_recv()
         for n, out in enumerate(outs):
 
             @pl.when(slot == n)
             def _(out=out):
-                out[at, :] = (value[...] + got[slot, at].astype(F32)).astype(BF16)
+                out[rows, :] = (value[...] + got[slot, rows].astype(F32)).astype(BF16)
 
     for i in range(pieces):
         copy(i).wait_send()
 
 
-def core_sum(body, ident, count, length, arrays, w, depth, name, pieces=2):
+def core_sum(body, ident, count, length, arrays, w, depth, name, pieces=2, riding=()):
     share = length // 2
     out = pl.BlockSpec((share, depth), lambda i: (0, 0), pipeline_mode=pl.Buffered(1))
     size = sum(a.shape[1] for a, _ in arrays)
-    return pl.pallas_call(
-        functools.partial(core_sum_kernel, body, count, pieces),
-        grid=(count,),
-        in_specs=[
-            pl.BlockSpec((length, a.shape[1]), lambda i, f=f: (f + i, 0)) for a, f in arrays
-        ]
+    return launch(
+        functools.partial(core_sum_body, body, count, pieces, len(arrays)),
+        [a for a, _ in arrays] + [w],
+        [pl.BlockSpec((length, a.shape[1]), lambda i, f=f: (f + i, 0)) for a, f in arrays]
         + [once(w.shape, lambda i, n=len(w.shape): (0,) * n)],
-        out_specs=[out] * count,
-        out_shape=[jax.ShapeDtypeStruct((share, depth), BF16)] * count,
-        scratch_shapes=[
+        [out] * count,
+        [jax.ShapeDtypeStruct((share, depth), BF16)] * count,
+        count,
+        name,
+        cost(2 * count * length * size * depth, 2 * count * length * (size + depth) + 2 * size * depth),
+        scratch=[
             pltpu.VMEM((count, share, depth), BF16),
             pltpu.VMEM((count, share, depth), BF16),
             pltpu.VMEM((share // pieces, depth), F32),
             pltpu.SemaphoreType.DMA((count, pieces)),
             pltpu.SemaphoreType.DMA((count, pieces)),
         ],
-        compiler_params=pltpu.CompilerParams(
-            dimension_semantics=("arbitrary",),
-            vmem_limit_bytes=VMEM_BYTES,
-            collective_id=ident,
-            has_side_effects=True,
-        ),
-        cost_estimate=cost(
-            2 * count * length * size * depth, 2 * count * length * (size + depth) + 2 * size * depth
-        ),
-        name=name,
-    )(*(a for a, _ in arrays), w)
+        riding=riding,
+        ident=ident,
+        place=True,
+    )
 
 
 def mix_body(attended, active, w, out):
@@ -334,7 +610,7 @@
         ).astype(out.dtype)
 
 
-def unmix_kernel(order, g, w, hidden, attended_grad, hidden_grad, sums):
+def unmix_tile(g, w, hidden, attended_grad, hidden_grad, sums):
     parts, inner, columns = w.shape
     width = attended_grad.shape[1]
     units = hidden.shape[1]
@@ -358,101 +634,195 @@
         sums[:, at] += jnp.sum(low.astype(F32), axis=0, keepdims=True)
 
 
-def unmix(order, g, w, hidden, width, length, tile=512):
-    rows, depth = g.shape
+def unmix(g, w, hidden, width, first, count, length, riding=(), ident=None, tile=512):
+    rows = count * length
     units = hidden.shape[1]
     parts, inner, columns = w.shape
+    depth = parts * columns
     per = length // tile
-    row = lambda n: pl.BlockSpec((tile, n), lambda i, o: (i, 0))
-    return pl.pallas_call(
-        unmix_kernel,
-        grid_spec=pltpu.PrefetchScalarGridSpec(
-            num_scalar_prefetch=1,
-            grid=(rows // tile,),
-            in_specs=[
-                pl.BlockSpec((tile, depth), lambda i, o: (o[i // per] * per + i % per, 0)),
-                once(w.shape, lambda i, o: (0, 0, 0)),
-                row(units),
-            ],
-            out_specs=[row(width), row(units), pl.BlockSpec((1, units), lambda i, o: (0, 0))],
-        ),
-        out_shape=[
+    row = lambda n: pl.BlockSpec((tile, n), lambda i: (i, 0))
+    late = lambda n: pl.BlockSpec((tile, n), lambda i: (first * per + i, 0))
+    return launch(
+        unmix_tile,
+        [g, w, hidden],
+        [late(depth), once(w.shape, lambda i: (0, 0, 0)), late(units)],
+        [row(width), row(units), pl.BlockSpec((1, units), lambda i: (0, 0))],
+        [
             jax.ShapeDtypeStruct((rows, width), BF16),
             jax.ShapeDtypeStruct((rows, units), BF16),
             jax.ShapeDtypeStruct((1, units), F32),
         ],
-        compiler_params=params(("arbitrary",)),
+        rows // tile,
+        "unmix",
+        cost(2 * rows * inner * depth, 2 * depth * (rows + inner) + rows * units * 6),
+        riding=riding,
+        ident=ident,
+    )
+
+
+def unmix_gather_body(first, tile, moves, last_moves, at, w, hidden, whole_in, attended_grad, hidden_grad, sums, full, g, local, *sems):
+    step, last = pl.program_id(0), pl.num_programs(0) - 1
+    share = full.shape[2]
+    per = share // tile
+    early = Gather(*moves).copies(at, full, *sems[:2])
+    late = Gather(*last_moves).copies(at, full, *sems[2:])
+
+    def load(i):
+        n = first * 2 * per + i
+        rows = pl.ds(pl.multiple_of(lax.rem(n, per) * tile, tile), tile)
+        return pltpu.make_async_copy(
+            full.at[lax.div(n, 2 * per), lax.rem(lax.div(n, per), 2), rows],
+            g.at[lax.rem(i, 2)],
+            local.at[lax.rem(i, 2)],
+        )
+
+    @pl.when(step == 0)
+    def _():
+        start_all(at, early)
+        load(step).start()
+
+    @pl.when(step < last)
+    def _():
+        load(step + 1).start()
+
+    load(step).wait()
+    unmix_tile(g.at[lax.rem(step, 2)], w, hidden, attended_grad, hidden_grad, sums)
+
+    @pl.when(step == last)
+    def _():
+        finish_all(at, early)
+        start_all(at, late)
+        finish_all(at, late)
+
+
+def unmix_gather(full, w, hidden, width, first, count, length, moves, last_moves, ident, riding=(), tile=512):
+    rows = count * length
+    units = hidden.shape[1]
+    parts, inner, columns = w.shape
+    depth = parts * columns
+    per = length // tile
+    row = lambda n: pl.BlockSpec((tile, n), lambda i: (i, 0))
+    counts = [Gather(*moves).count, Gather(*last_moves).count]
+
+    body = functools.partial(unmix_gather_body, first, tile, moves, last_moves)
+    extra = list(riding)
+    args = [w, hidden, full] + [a for r in extra for a in r.ins]
+    shapes = [
+        jax.ShapeDtypeStruct((rows, width), BF16),
+        jax.ShapeDtypeStruct((rows, units), BF16),
+        jax.ShapeDtypeStruct((1, units), F32),
+        like(full),
+    ]
+    aliases, n_in, n_out = {2: 3}, 3, 4
+    for r in extra:
+        if r.aliased:
+            aliases[n_in + len(r.ins) - 1] = n_out
+        n_in, n_out = n_in + len(r.ins), n_out + len(r.outs)
+
+    def kernel(*refs):
+        take = iter(refs)
+        some = lambda n: [next(take) for _ in range(n)]
+        own_ins, ride_ins = some(3), [some(len(r.ins)) for r in extra]
+        own_outs, ride_outs = some(4), [some(len(r.outs)) for r in extra]
+        own_scratch = some(6)
+        at = places()
+        copies = []
+        for r, i, o in zip(extra, ride_ins, ride_outs):
+            copies += r.copies(at, i, o, *some(2))
+
+        @pl.when(pl.program_id(0) == 0)
+        def _():
+            greet(at)
+            start_all(at, copies)
+
+        body(at, *own_ins, *own_outs, *own_scratch)
+
+        @pl.when(pl.program_id(0) == rows // tile - 1)
+        def _():
+            finish_all(at, copies)
+
+    return pl.pallas_call(
+        kernel,
+        grid=(rows // tile,),
+        in_specs=[
+            once(w.shape, lambda i: (0, 0, 0)),
+            pl.BlockSpec((tile, units), lambda i: (first * per + i, 0)),
+        ]
+        + [ANYWHERE] * (len(args) - 2),
+        out_specs=[row(width), row(units), pl.BlockSpec((1, units), lambda i: (0, 0)), ANYWHERE]
+        + [ANYWHERE for r in extra for _ in r.outs],
+        out_shape=shapes + [o for r in extra for o in r.outs],
+        input_output_aliases=aliases,
+        scratch_shapes=[pltpu.VMEM((2, tile, depth), BF16), pltpu.SemaphoreType.DMA((2,))]
+        + [pltpu.SemaphoreType.DMA((n,)) for n in counts for _ in range(2)]
+        + [pltpu.SemaphoreType.DMA((r.count,)) for r in extra for _ in range(2)],
+        compiler_params=pltpu.CompilerParams(
+            dimension_semantics=("arbitrary",),
+            vmem_limit_bytes=VMEM_BYTES,
+            collective_id=ident,
+            has_side_effects=True,
+        ),
         cost_estimate=cost(2 * rows * inner * depth, 2 * depth * (rows + inner) + rows * units * 6),
         name="unmix",
-    )(order, g, w, hidden)
-
-
-def outer_rows_kernel(length, order, x, *refs):
+    )(*args)
+
+
+def outer_rows_kernel(x, *refs):
     parts, out = refs[:-1], refs[-1]
-    total, slot = None, 0
+    total, start = None, 0
     for part in parts:
-        for at in range(0, part.shape[0], length):
-            start = pl.multiple_of(order[slot] * length, length)
-            term = tn(x[pl.ds(start, length), :], part[at : at + length, :])
-            total = term if total is None else total + term
-            slot += 1
+        term = tn(x[start : start + part.shape[0], :], part[...])
+        total = term if total is None else total + term
+        start += part.shape[0]
     out[...] = total.astype(out.dtype)
 
 
-def outer_rows(order, x, parts, length, tile=512):
+def outer_rows(x, parts, riding=(), ident=None, tile=512, wait_for=()):
     rows, depth = x.shape
     n = parts[0].shape[1]
     tile = min(tile, depth)
-    return pl.pallas_call(
-        functools.partial(outer_rows_kernel, length),
-        grid_spec=pltpu.PrefetchScalarGridSpec(
-            num_scalar_prefetch=1,
-            grid=(depth // tile,),
-            in_specs=[pl.BlockSpec((rows, tile), lambda i, o: (0, i))]
-            + [once(p.shape, lambda i, o: (0, 0)) for p in parts],
-            out_specs=pl.BlockSpec((tile, n), lambda i, o: (i, 0)),
-        ),
-        out_shape=jax.ShapeDtypeStruct((depth, n), BF16),
-        compiler_params=params(("arbitrary",)),
-        cost_estimate=cost(2 * rows * depth * n, 2 * (rows * (depth + n) + depth * n)),
-        name="outer_rows",
-    )(order, x, *parts)
-
-
-def outer_columns_kernel(length, order, a, b, g, out):
+    return launch(
+        outer_rows_kernel,
+        [x, *parts],
+        [pl.BlockSpec((rows, tile), lambda i: (0, i))]
+        + [once(p.shape, lambda i: (0, 0)) for p in parts],
+        [pl.BlockSpec((tile, n), lambda i: (i, 0))],
+        [jax.ShapeDtypeStruct((depth, n), BF16)],
+        depth // tile,
+        "outer_rows",
+        cost(2 * rows * depth * n, 2 * (rows * (depth + n) + depth * n)),
+        riding=riding,
+        ident=ident,
+        wait_for=wait_for,
+    )
+
+
+def outer_columns_kernel(a, b, g, out):
     width = a.shape[1]
-    for src, lo, hi in ((a, 0, width), (b, width, out.shape[1])):
-        total = None
-        for slot in range(a.shape[0] // length):
-            start = pl.multiple_of(order[slot] * length, length)
-            term = tn(src[slot * length : (slot + 1) * length, :], g[pl.ds(start, length), :])
-            total = term if total is None else total + term
-        out[0, lo:hi, :] = total.astype(out.dtype)
-
-
-def outer_columns(order, a, b, g, parts, length):
+    out[0, :width, :] = tn(a[...], g[...]).astype(out.dtype)
+    out[0, width:, :] = tn(b[...], g[...]).astype(out.dtype)
+
+
+def outer_columns(a, b, g, parts, riding=(), ident=None):
     rows, depth = g.shape
     width, units = a.shape[1], b.shape[1]
     tile = depth // parts
-    return pl.pallas_call(
-        functools.partial(outer_columns_kernel, length),
-        grid_spec=pltpu.PrefetchScalarGridSpec(
-            num_scalar_prefetch=1,
-            grid=(parts,),
-            in_specs=[
-                once((rows, width), lambda i, o: (0, 0)),
-                once((rows, units), lambda i, o: (0, 0)),
-                pl.BlockSpec((rows, tile), lambda i, o: (0, i)),
-            ],
-            out_specs=pl.BlockSpec((1, width + units, tile), lambda i, o: (i, 0, 0)),
-        ),
-        out_shape=jax.ShapeDtypeStruct((parts, width + units, tile), BF16),
-        compiler_params=params(("arbitrary",)),
-        cost_estimate=cost(
-            2 * rows * depth * (width + units), 2 * (rows * (depth + width + units) + depth * (width + units))
-        ),
-        name="outer_columns",
-    )(order, a, b, g)
+    return launch(
+        outer_columns_kernel,
+        [a, b, g],
+        [
+            once((rows, width), lambda i: (0, 0)),
+            once((rows, units), lambda i: (0, 0)),
+            pl.BlockSpec((rows, tile), lambda i: (0, i)),
+        ],
+        [pl.BlockSpec((1, width + units, tile), lambda i: (i, 0, 0))],
+        [jax.ShapeDtypeStruct((parts, width + units, tile), BF16)],
+        parts,
+        "outer_columns",
+        cost(2 * rows * depth * (width + units), 2 * (rows * (depth + width + units) + depth * (width + units))),
+        riding=riding,
+        ident=ident,
+    )
 
 
 def head_lanes(width, head):
@@ -491,32 +861,29 @@
         log_sums[:, begin : begin + tile] = sums.T[:8, :]
 
 
-def attend(q, k, v, column_ids, row_ids):
+def attend(q, k, v, column_ids, row_ids, riding=(), ident=None):
     rows, width = q.shape
     seqs, _, length = row_ids.shape
     heads = width // HEAD_DIM
     seq = pl.BlockSpec((length, width), lambda s: (s, 0))
-    return pl.pallas_call(
+    return launch(
         attend_kernel,
-        grid=(seqs,),
-        in_specs=[
+        [q, k, v, column_ids, row_ids],
+        [
             seq,
             seq,
             seq,
             pl.BlockSpec((length, 1), lambda s: (s, 0)),
             pl.BlockSpec((None, 1, length), lambda s: (s, 0, 0)),
         ],
-        out_specs=[seq, pl.BlockSpec((8, length), lambda s: (0, s))],
-        out_shape=[
-            jax.ShapeDtypeStruct((rows, width), BF16),
-            jax.ShapeDtypeStruct((8, rows), F32),
-        ],
-        compiler_params=params(("arbitrary",)),
-        cost_estimate=cost(
-            8 * seqs * heads * length * length * 256 * 0.8, 8 * rows * width, seqs * heads * length**2
-        ),
-        name="attend",
-    )(q, k, v, column_ids, row_ids)
+        [seq, pl.BlockSpec((8, length), lambda s: (0, s))],
+        [jax.ShapeDtypeStruct((rows, width), BF16), jax.ShapeDtypeStruct((8, rows), F32)],
+        seqs,
+        "attend",
+        cost(8 * seqs * heads * length * length * 256 * 0.8, 8 * rows * width, seqs * heads * length**2),
+        riding=riding,
+        ident=ident,
+    )
 
 
 def unattend_kernel(
@@ -564,21 +931,21 @@
     sums[:, 2 * width :] += jnp.sum(turned.astype(F32), axis=0, keepdims=True)
 
 
-def unattend(first, count, q, k, v, g, log_sums, column_ids, row_ids, tables):
+def unattend(first, count, q, k, v, g, g_first, log_sums, column_ids, row_ids, tables, riding=(), ident=None, wait_for=()):
     width = q.shape[1]
     length = row_ids.shape[2]
     rows, seqs = count * length, count
     heads = width // HEAD_DIM
     seq = pl.BlockSpec((length, width), lambda s: (first + s, 0))
     table = once((length, 128), lambda s: (0, 0))
-    return pl.pallas_call(
+    return launch(
         unattend_kernel,
-        grid=(seqs,),
-        in_specs=[
+        [q, k, v, g, log_sums, column_ids, row_ids, *tables],
+        [
             seq,
             seq,
             seq,
-            seq,
+            pl.BlockSpec((length, width), lambda s: (g_first + s, 0)),
             pl.BlockSpec((8, length), lambda s: (0, first + s)),
             pl.BlockSpec((length, 1), lambda s: (first + s, 0)),
             pl.BlockSpec((None, 1, length), lambda s: (first + s, 0, 0)),
@@ -586,47 +953,19 @@
             table,
             table,
         ],
-        out_specs=[
+        [
             pl.BlockSpec((length, 3 * width), lambda s: (s, 0)),
             pl.BlockSpec((1, 3 * width), lambda s: (0, 0)),
         ],
-        out_shape=[
-            jax.ShapeDtypeStruct((rows, 3 * width), BF16),
-            jax.ShapeDtypeStruct((1, 3 * width), F32),
-        ],
-        scratch_shapes=[pltpu.VMEM((length, width), F32), pltpu.VMEM((length, width), F32)],
-        compiler_params=params(("arbitrary",)),
-        cost_estimate=cost(
-            20 * seqs * heads * length * length * 256 * 0.8,
-            14 * rows * width,
-            seqs * heads * length**2,
-        ),
-        name="unattend",
-    )(q, k, v, g, log_sums, column_ids, row_ids, *tables)
-
-
-def gather_parts(part, groups):
-    if groups != 4:
-        return lax.all_gather(part, "dp", axis=0)
-    mine = lax.axis_index("dp")
-    full = jnp.zeros((groups,) + part.shape, part.dtype)
-    pieces = [part] + [
-        lax.ppermute(part, "dp", [(i, i ^ step) for i in range(groups)]) for step in (1, 2, 3)
-    ]
-    for step, piece in enumerate(pieces):
-        full = lax.dynamic_update_slice(full, piece[None], (mine ^ step,) + (0,) * part.ndim)
-    return full
-
-
-def along_chips(values, hops):
-    return lax.ppermute(
-        values, "tensor", [(2 * a + core, 2 * b + core) for a, b in hops for core in range(2)]
-    )
-
-
-INWARD = ((0, 1), (3, 2))
-MIDDLE = ((1, 2), (2, 1))
-SIDES = ((0, 1), (1, 0), (2, 3), (3, 2))
+        [jax.ShapeDtypeStruct((rows, 3 * width), BF16), jax.ShapeDtypeStruct((1, 3 * width), F32)],
+        count,
+        "unattend",
+        cost(20 * seqs * heads * length * length * 256 * 0.8, 14 * rows * width, seqs * heads * length**2),
+        scratch=[pltpu.VMEM((length, width), F32), pltpu.VMEM((length, width), F32)],
+        riding=riding,
+        ident=ident,
+        wait_for=wait_for,
+    )
 
 
 def add_up(*parts):
@@ -746,113 +1085,245 @@
     units = up_weight.shape[1]
     groups, members = lax.axis_size("dp"), lax.axis_size("tensor")
     gain, shift = norm_gain.astype(F32)[None, :], norm_bias.astype(F32)[None, :]
-    paired = members == 8 and seqs == 4 and 2 * share == length
+    paired = groups == 4 and members == 8 and seqs == 4 and 2 * share == length
     me = lax.axis_index("tensor")
     if paired:
-        order = jnp.arange(3, -1, -1, dtype=jnp.int32) ^ (me // 2)
+        chip = me // 2
+        order = jnp.arange(3, -1, -1, dtype=jnp.int32) ^ chip
+        inner = ((chip == 1) | (chip == 2)).astype(jnp.int32)
     else:
         order = jnp.arange(seqs, dtype=jnp.int32)
 
-    normed = norm(inputs, gain, shift)
-    rows = lax.all_gather(normed, "tensor", axis=0, tiled=True)
-    upstream = lax.all_gather(grad_out, "tensor", axis=0, tiled=True)
     first = jnp.concatenate([query_weight, key_weight, value_weight, up_weight], axis=1)
     second = jnp.concatenate([out_weight, down_weight], axis=0)
-    first_full = gather_parts(first, groups).reshape(depth, 3 * width + units)
-    second_full = gather_parts(second, groups)
     bias = jnp.concatenate([query_bias, key_bias, value_bias, up_bias]).astype(F32)[None, :]
     tables = rotary_tables(length)
     ids = block_ids[order]
     column_ids = ids.reshape(seqs * length, 1)
     row_ids = ids.reshape(seqs, 1, length)
-
-    q, k, v, active, hidden = project(order, rows, first_full, bias, tables, width, units, length)
-    attended, log_sums = attend(q, k, v, column_ids, row_ids)
     pair = seqs // 2
+    everything = seqs * length
+
+    idents = iter(range(1, 100))
 
     if paired:
-        far = core_sum(
-            mix_body, 1, pair, length, [(attended, 0), (active, 0)], second_full, depth, "mix"
-        )
-        from_end, from_end_2 = along_chips(far[0], INWARD), along_chips(far[1], INWARD)
-        near = core_sum(
+        kept = lambda values: jnp.where(inner == 1, values, jnp.zeros_like(values))
+        rows, full, first_full, second_full = gather(
+            next(idents), inputs, gain, shift, grad_out, first, second, groups
+        )
+        rows = rows.reshape(everything, depth)
+        first_full = first_full.reshape(depth, 3 * width + units)
+        q, k, v, active, hidden, full = project(
+            rows,
+            first_full,
+            bias,
+            tables,
+            width,
+            units,
+            length,
+            riding=[gathering(full, (1, 0, share))],
+            ident=next(idents),
+        )
+        half, more = share // 2, share * 9 // 16
+        attended, log_sums, full = attend(
+            q,
+            k,
+            v,
+            column_ids,
+            row_ids,
+            riding=[gathering(full, (2, 0, more), ("first", 0, share))],
+            ident=next(idents),
+        )
+        *far, full = core_sum(
             mix_body,
-            2,
+            next(idents),
+            pair,
+            length,
+            [(attended, 0), (active, 0)],
+            second_full,
+            depth,
+            "mix",
+            riding=[gathering(full, (2, more, share))],
+        )
+        *near, full, end = core_sum(
+            mix_body,
+            next(idents),
             pair,
             length,
             [(attended, pair), (active, pair)],
-            after(second_full, far[0]),
+            second_full,
             depth,
             "mix",
-        )
-        crossing = add_up(far[1], from_end)
-        crossed = along_chips(crossing, MIDDLE)
-        upstream = after(upstream, near[0], crossing)
+            riding=[
+                gathering(full, (3, 0, half), ("second", 0, share)),
+                sending(far[0], "in", 0, half),
+            ],
+        )
+        near_attended_grad, near_hidden_grad, near_up_sum, full, end = unmix_gather(
+            full,
+            second_full,
+            hidden,
+            width,
+            pair,
+            pair,
+            length,
+            [(3, half, share), ("third", 0, half)],
+            [("third", half, share)],
+            next(idents),
+            riding=[sending(far[0], "in", half, share, end)],
+        )
+        upstream = full.reshape(everything, depth)
+        cut = share * 3 // 8
+        crossing = add_up(far[1], end)
+        far_attended_grad, far_hidden_grad, far_up_sum, end, middle = unmix(
+            upstream,
+            second_full,
+            hidden,
+            width,
+            0,
+            pair,
+            length,
+            riding=[sending(far[1], "in", 0, cut), sending(crossing, "middle", 0, cut)],
+            ident=next(idents),
+        )
+        up_sum = near_up_sum + far_up_sum
+        far_grad, far_sum, end, middle = unattend(
+            0,
+            pair,
+            q,
+            k,
+            v,
+            far_attended_grad,
+            0,
+            log_sums,
+            column_ids,
+            row_ids,
+            tables,
+            riding=[
+                sending(far[1], "in", cut, share, end),
+                sending(crossing, "middle", cut, share, middle),
+            ],
+            ident=next(idents),
+        )
+        to_side = add_up(near[0], kept(middle))
+        to_middle = add_up(far[0], end)
+        mine = near[1]
+        *far, side, middle = core_sum(
+            unproject_body,
+            next(idents),
+            pair,
+            length,
+            [(far_grad, 0), (far_hidden_grad, 0)],
+            first_full,
+            depth,
+            "unproject",
+            riding=[sending(to_side, "side", 0, half), sending(to_middle, "middle", 0, half)],
+        )
+        second_part, side, middle, end = outer_columns(
+            attended,
+            active,
+            upstream,
+            groups,
+            riding=[
+                sending(to_side, "side", half, share, side),
+                sending(to_middle, "middle", half, share, middle),
+                sending(far[0], "in", 0, half),
+            ],
+            ident=next(idents),
+        )
+        terms = [mine, side, kept(middle)]
+        second_grad = lax.psum_scatter(second_part, "dp", scatter_dimension=0)
+        up_part, end = outer_rows(
+            rows,
+            [far_hidden_grad, near_hidden_grad],
+            riding=[sending(far[0], "in", half, share, end)],
+            ident=next(idents),
+            wait_for=[second_part],
+        )
+        up_grad = lax.psum_scatter(up_part, "dp", scatter_dimension=0, tiled=True)
     else:
+        first_full = lax.all_gather(first, "dp", axis=0, tiled=True)
+        second_full = lax.all_gather(second, "dp", axis=0)
+        rows = lax.all_gather(norm(inputs, gain, shift), "tensor", axis=0, tiled=True)
+        upstream = lax.all_gather(grad_out, "tensor", axis=0, tiled=True)
+        q, k, v, active, hidden = project(rows, first_full, bias, tables, width, units, length)
+        attended, log_sums = attend(q, k, v, column_ids, row_ids)
         whole = each_tile(mix_body, [attended, active], second_full, depth, "mix")
         terms = [lax.psum_scatter(whole, "tensor", scatter_dimension=0, tiled=True)]
-
-    attended_grad, hidden_grad, up_sum = unmix(order, upstream, second_full, hidden, width, length)
-    if paired:
-        to_side = add_up(near[0], crossed)
-        to_middle = add_up(far[0], from_end_2)
-        terms = [near[1], along_chips(to_side, SIDES), along_chips(to_middle, MIDDLE)]
-        attended_grad = after(attended_grad, to_side, to_middle)
+        attended_grad, hidden_grad, up_sum = unmix(
+            upstream, second_full, hidden, width, 0, seqs, length
+        )
     total = inputs.astype(F32) + out_bias.astype(F32) + down_bias.astype(F32)
     for values in terms:
         total = total + values.astype(F32)
     output = total.astype(BF16)
 
-    def back(at, count, g):
-        return unattend(at, count, q, k, v, g, log_sums, column_ids, row_ids, tables)
-
     if paired:
-        far_grad, far_sum = back(0, pair, attended_grad)
-        far = core_sum(
-            unproject_body, 3, pair, length, [(far_grad, 0), (hidden_grad, 0)], first_full, depth, "unproject"
-        )
-        from_end, from_end_2 = along_chips(far[0], INWARD), along_chips(far[1], INWARD)
-        second_grad = outer_columns(
-            order, after(attended, far[0]), active, upstream, groups, length
-        )
-        near_grad, near_sum = back(pair, pair, after(attended_grad, second_grad, output))
-        crossing = add_up(far[1], from_end)
-        crossed = along_chips(crossing, MIDDLE)
-        near = core_sum(
+        crossing = add_up(far[1], end)
+        near_grad, near_sum, end, middle = unattend(
+            pair,
+            pair,
+            q,
+            k,
+            v,
+            near_attended_grad,
+            0,
+            log_sums,
+            column_ids,
+            row_ids,
+            tables,
+            riding=[sending(far[1], "in", 0, more), sending(crossing, "middle", 0, more)],
+            ident=next(idents),
+            wait_for=[output],
+        )
+        *near, end, middle = core_sum(
             unproject_body,
-            4,
+            next(idents),
             pair,
             length,
-            [(near_grad, 0), (hidden_grad, pair)],
-            after(first_full, crossing, near_grad),
+            [(near_grad, 0), (near_hidden_grad, 0)],
+            first_full,
             depth,
             "unproject",
+            riding=[
+                sending(far[1], "in", more, share, end),
+                sending(crossing, "middle", more, share, middle),
+            ],
         )
         qkv_sum = far_sum + near_sum
-        first_grad = outer_rows(order, after(rows, near[0]), [far_grad, near_grad], length)
-        to_side = add_up(near[0], crossed)
-        to_middle = add_up(far[0], from_end_2)
-        terms = [near[1], along_chips(to_side, SIDES), along_chips(to_middle, MIDDLE)]
-        up_grad = outer_rows(
-            order, rows, [after(hidden_grad, first_grad, to_side, to_middle)], length
-        )
+        to_side = add_up(near[0], kept(middle))
+        to_middle = add_up(far[0], end)
+        first_part, side, middle = outer_rows(
+            rows,
+            [far_grad, near_grad],
+            riding=[sending(to_side, "side", 0, share), sending(to_middle, "middle", 0, share)],
+            ident=next(idents),
+            wait_for=[second_grad],
+        )
+        first_grad = lax.psum_scatter(first_part, "dp", scatter_dimension=0, tiled=True)
+        terms = [near[1], side, middle]
     else:
-        qkv_grad, qkv_sum = back(0, seqs, attended_grad)
+        inner = jnp.ones((), jnp.int32)
+        qkv_grad, qkv_sum = unattend(
+            0, seqs, q, k, v, attended_grad, 0, log_sums, column_ids, row_ids, tables
+        )
         whole = each_tile(unproject_body, [qkv_grad, hidden_grad], first_full, depth, "unproject")
         terms = [lax.psum_scatter(whole, "tensor", scatter_dimension=0, tiled=True)]
-        second_grad = outer_columns(order, attended, active, upstream, groups, length)
-        first_grad = outer_rows(order, rows, [qkv_grad], length)
-        up_grad = outer_rows(order, rows, [hidden_grad], length)
-
-    second_grad = lax.psum_scatter(second_grad, "dp", scatter_dimension=0).astype(F32)
-    first_grad = lax.psum_scatter(first_grad, "dp", scatter_dimension=0, tiled=True).astype(F32)
-    up_grad = lax.psum_scatter(up_grad, "dp", scatter_dimension=0, tiled=True).astype(F32)
-
-    input_grad, gain_part, shift_part = unnorm(inputs, grad_out, gain, [(t, 0) for t in terms])
+        (second_part,) = outer_columns(attended, active, upstream, groups)
+        (first_part,) = outer_rows(rows, [qkv_grad])
+        (up_part,) = outer_rows(rows, [hidden_grad])
+        second_grad = lax.psum_scatter(second_part, "dp", scatter_dimension=0)
+        first_grad = lax.psum_scatter(first_part, "dp", scatter_dimension=0, tiled=True)
+        up_grad = lax.psum_scatter(up_part, "dp", scatter_dimension=0, tiled=True)
+
+    second_grad, first_grad, up_grad = (t.astype(F32) for t in (second_grad, first_grad, up_grad))
+    input_grad, gain_part, shift_part = unnorm(
+        inner[None], inputs, grad_out, gain, terms, [up_grad] if paired else []
+    )
     bias_part = jnp.sum(grad_out, axis=0, dtype=F32)[None, :]
     if paired and groups == 4:
         wide, narrow = sum_everywhere(
-            5, groups, members, gain_part, shift_part, bias_part, qkv_sum, up_sum
+            next(idents), groups, members, gain_part, shift_part, bias_part, qkv_sum, up_sum
         )
         gain_grad, shift_grad, outer_bias_grad = wide[0], wide[1], wide[2]
         qkv_sum, up_sum = narrow[0, : 3 * width], narrow[0, 3 * width :]

time: 815 us -> 728 us (0.89)
  waiting for transfers between devices: 315 us -> 9.51 us
  Pallas kernels: 358 us -> 643 us
  starting transfers between devices: 36.9 us -> 0.12 us
  local copies, waits for them, and re-layouts: 44 us -> 20.9 us
    ppermute x16 -> x0, waiting for transfers between devices: 311 us -> none  [the longest x10 205 us: along_chips(): lax.ppermute(values, 'tensor', [(2 * a + core, 2 * b + core) for a, b in...]
    pallas_call x14 -> x15, Pallas kernels: 344 us -> 628 us  [the longest x12 438 us: launch(): pl.pallas_call(kernel, grid=(grid,), in_specs=ins + [ANYWHERE] * len(extr...]
    ppermute x16 -> x0, starting transfers between devices: 36.7 us -> none  [the longest x10 25.8 us: along_chips(): lax.ppermute(values, 'tensor', [(2 * a + core, 2 * b + core) for a, b in...]
    dynamic_update_slice x8 -> x0, local copies, waits for them, and re-layouts: 17.2 us -> none  [gather_parts(): lax.dynamic_update_slice(full, piece[None], (mine ^ step,) + (0,) * part....]
    convert_element_type x6 -> x5, other arithmetic: 19.2 us -> 20.3 us  [add_up(): return total.astype(BF16)]
  transfers between devices with their start and end apart: 21 -> 3, of which waited for: 7 -> 1; matrix products, arithmetic and copies ran while one was open for 9% -> 4% of each run, Pallas kernels for 38% -> 23%
where the time goes in v3:
time: 728 us; the launch traced here: 724 us
  Pallas kernels  643 us (88%)
  other arithmetic  36.9 us (5%)
  local copies, waits for them, and re-layouts  20.9 us (3%)
  between operations  14.5 us (2%)
  waiting for transfers between devices  9.51 us (1%)
    pallas_call x12, Pallas kernels, launch(): pl.pallas_call(kernel, grid=(grid,), in_specs=ins + [ANYWHERE] * len(extr...  438 us
    pallas_call x1, Pallas kernels, gather(): pl.pallas_call(functools.partial(gather_kernel, tile, groups), in_specs=[...  149 us
    pallas_call x1, Pallas kernels, unmix_gather(): pl.pallas_call(kernel, grid=(rows // tile,), in_specs=[once(w.shape, lamb...  32.6 us
    convert_element_type x5, other arithmetic, add_up(): return total.astype(BF16)  20.3 us
  transfers between devices with their start and end apart: 3, of which 1 were waited for; matrix products, arithmetic and copies ran while one was open for 4% of the time, Pallas kernels for 23%

profile of v3, /device:TPU:0, one launch (start us, length us, event | category | flops | bytes accessed | tf_op | source)
XLA Modules:
  0.0 724.5 jit_solution(7113562468083158908)
XLA Ops:
  23.1 149.4 %gather.7 = (bf16[4,2,512,2048]{3,2,1,0:T(8,128)(2,1)}, bf16[4,2,512,2048]{3,2,1,0:T(8,128)(2,1)}, bf16[4,512,1792]{2,1,0:T(8,128)(2,1)}, bf16[4,1280,512]{2,1,0:T(8,128)(2,1)}) custom-call(bf16[512,2048]{1,0:T(8,128)(2,1)} %x.3, f32[1,2048]{1,0:T(1,128)} %bitcast.36, f32[1,2048]{1,0:T(1,128)} %bitcast.39, bf16[512,2048]{1,0:T(8,128)(2,1)} %g.3, ...), custom_call_target="tpu_custom_call" | custom-call | flops 1048576 | bytes 6291456 | tf_op jit(solution)/shard_map/gather/pallas_call | solution.py:432
  172.5 54.3 %project.1 = (bf16[4096,256]{1,0:T(8,128)(2,1)}, bf16[4096,256]{1,0:T(8,128)(2,1)}, bf16[4096,256]{1,0:T(8,128)(2,1)}, bf16[4096,1024]{1,0:T(8,128)(2,1)}, f32[4...) custom-call(bf16[4096,2048]{1,0:T(8,128)(2,1)} %bitcast.25, ...), custom_call_target="tpu_custom_call", output_to_operand_aliasing={{5}: (6, {})} | custom-call | flops 3006477056 | bytes 4928307 | tf_op jit(solution)/shard_map/project/pallas_call | solution.py:335
  226.8 32.3 %attend.1 = (bf16[4096,256]{1,0:T(8,128)(2,1)}, f32[8,4096]{1,0:T(8,128)}, bf16[4,2,512,2048]{3,2,1,0:T(8,128)(2,1)}) custom-call(bf16[4096,256]{1,0:T(8,128)(2,1)} %get-tuple-element.79.refs_0_, bf16[4096,256]{1,0:T(8,128)(2,1)} %get-tuple-element.80.refs_1_, bf16[4096,256]{1,0:T(8,128)(2,1)} %get-tuple-element.81.refs_2_, ...), custom_call_target="tpu_custom_call", output_to_operand_aliasing={{2}: (5, {})} | custom-call | flops 2748779008 | bytes 838860 | tf_op jit(solution)/shard_map/attend/pallas_call | solution.py:335
  259.1 27.6 %mix.2 = (bf16[512,2048]{1,0:T(8,128)(2,1)}, bf16[512,2048]{1,0:T(8,128)(2,1)}, bf16[4,2,512,2048]{3,2,1,0:T(8,128)(2,1)}) custom-call(bf16[4096,256]{1,0:T(8,128)(2,1)} %get-tuple-element.83.refs_0_, bf16[4096,1024]{1,0:T(8,128)(2,1)} %get-tuple-element.84.refs_1_, ...), custom_call_target="tpu_custom_call", output_to_operand_aliasing={{2}: (3, {})} | custom-call | flops 1073741824 | bytes 1887436 | tf_op jit(solution)/shard_map/mix/pallas_call | solution.py:335
  286.7 30.8 %mix.3 = (bf16[512,2048]{1,0:T(8,128)(2,1)}, bf16[512,2048]{1,0:T(8,128)(2,1)}, bf16[4,2,512,2048]{3,2,1,0:T(8,128)(2,1)}, bf16[512,2048]{1,0:T(8,128)(2,1)}) custom-call(bf16[4096,256]{1,0:T(8,128)(2,1)} %get-tuple-element.83.refs_0_, bf16[4096,1024]{1,0:T(8,128)(2,1)} %get-tuple-element.84.refs_1_, ...), custom_call_target="tpu_custom_call", output_to_operand_aliasing={{2}: (3, {})} | custom-call | flops 1073741824 | bytes 1887436 | tf_op jit(solution)/shard_map/mix/pallas_call | solution.py:335
  317.5 32.6 %unmix.2 = (bf16[2048,256]{1,0:T(8,128)(2,1)}, bf16[2048,1024]{1,0:T(8,128)(2,1)}, f32[1,1024]{1,0:T(1,128)}, bf16[4,2,512,2048]{3,2,1,0:T(8,128)(2,1)}, bf16[512,2048]{1,0:T(8,128)(2,1)}) custom-call(bf16[4,1280,512]{2,1,0:T(8,128)(2,1)} %get-tuple-element.85.refs_2_.refs_0_.refs_1_, ...), custom_call_target="tpu_custom_call", output_to_operand_aliasing={{3}: (2, {}), {4}: (4, {})} | custom-call | flops 1073741824 | bytes 2621440 | tf_op jit(solution)/shard_map/unmix/pallas_call | solution.py:744
  350.1 3.8 add_convert_fusion.6.refs_4_.refs_12_
  353.9 24.2 %unmix.3 = (bf16[2048,256]{1,0:T(8,128)(2,1)}, bf16[2048,1024]{1,0:T(8,128)(2,1)}, f32[1,1024]{1,0:T(1,128)}, bf16[512,2048]{1,0:T(8,128)(2,1)}, bf16[512,2048]{1,0:T(8,128)(2,1)}) custom-call(bf16[4096,2048]{1,0:T(8,128)(2,1)} %bitcast.23, bf16[4,1280,512]{2,1,0:T(8,128)(2,1)} %get-tuple-element.85.refs_2_.refs_0_.refs_1_, ...), custom_call_target="tpu_custom_call" | custom-call | flops 1073741824 | bytes 2621440 | tf_op jit(solution)/shard_map/unmix/pallas_call | solution.py:335
  378.2 35.7 %unattend.2 = (bf16[2048,768]{1,0:T(8,128)(2,1)}, f32[1,768]{1,0:T(1,128)}, bf16[512,2048]{1,0:T(8,128)(2,1)}, bf16[512,2048]{1,0:T(8,128)(2,1)}) custom-call(bf16[4096,256]{1,0:T(8,128)(2,1)} %get-tuple-element.79.refs_0_, bf16[4096,256]{1,0:T(8,128)(2,1)} %get-tuple-element.80.refs_1_, ...), custom_call_target="tpu_custom_call", output_to_operand_aliasing={{2}: (11, {}), {3}: (13, {})} | custom-call | flops 3435973888 | bytes 734003 | tf_op jit(solution)/shard_map/unattend/pallas_call | solution.py:335
  413.9 6.6 add_convert_fusion.4
  420.4 33.3 %unproject.2 = (bf16[512,2048]{1,0:T(8,128)(2,1)}, bf16[512,2048]{1,0:T(8,128)(2,1)}, bf16[512,2048]{1,0:T(8,128)(2,1)}, bf16[512,2048]{1,0:T(8,128)(2,1)}) custom-call(bf16[2048,768]{1,0:T(8,128)(2,1)} %get-tuple-element.102.refs_0_.refs_1_, bf16[2048,1024]{1,0:T(8,128)(2,1)} %get-tuple-element.103.refs_1_, bf16[2048,1792]{1,0:T(8,128)(2,1)} %bitcast.29, ...), custom_call_target="tpu_custom_call" | custom-call | flops 1503238528 | bytes 2306867 | tf_op jit(solution)/shard_map/unproject/pallas_call | solution.py:335
  453.7 53.1 %outer_columns.1 = (bf16[4,1280,512]{2,1,0:T(8,128)(2,1)}, bf16[512,2048]{1,0:T(8,128)(2,1)}, bf16[512,2048]{1,0:T(8,128)(2,1)}, bf16[512,2048]{1,0:T(8,128)(2,1)}) custom-call(bf16[4096,256]{1,0:T(8,128)(2,1)} %get-tuple-element.83.refs_0_, bf16[4096,1024]{1,0:T(8,128)(2,1)} %get-tuple-element.84.refs_1_, ...), custom_call_target="tpu_custom_call", output_to_operand_aliasing={{1}: (4, {}), {2}: (6, {})} | custom-call | flops 2147483648 | bytes 3250585 | tf_op jit(solution)/shard_map/outer_columns/pallas_call | solution.py:335
  506.9 29.4 %outer_rows.2 = (bf16[2048,1024]{1,0:T(8,128)(2,1)}, bf16[512,2048]{1,0:T(8,128)(2,1)}) custom-call(bf16[4096,2048]{1,0:T(8,128)(2,1)} %bitcast.26, bf16[2048,1024]{1,0:T(8,128)(2,1)} %get-tuple-element.103.refs_1_, bf16[2048,1024]{1,0:T(8,128)(2,1)} %get-tuple-element.112.refs_2_.refs_1_, ...), custom_call_target="tpu_custom_call", output_to_operand_aliasing={{1}: (4, {})} | custom-call | flops 1717986944 | bytes 2936012 | tf_op jit(solution)/shard_map/outer_rows/pallas_call | solution.py:335
  538.0 3.9 add_convert_fusion.2.refs_11_.refs_5_
  541.8 4.9 add_convert_fusion.3.refs_12_
  546.7 35.5 %unattend.3 = (bf16[2048,768]{1,0:T(8,128)(2,1)}, f32[1,768]{1,0:T(1,128)}, bf16[512,2048]{1,0:T(8,128)(2,1)}, bf16[512,2048]{1,0:T(8,128)(2,1)}) custom-call(bf16[4096,256]{1,0:T(8,128)(2,1)} %get-tuple-element.79.refs_0_, bf16[4096,256]{1,0:T(8,128)(2,1)} %get-tuple-element.80.refs_1_, bf16[4096,256]{1,0:T(8,128)(2,1)} %get-tuple-element.81.refs_2_, ...), custom_call_target="tpu_custom_call" | custom-call | flops 3435973888 | bytes 734003 | tf_op jit(solution)/shard_map/unattend/pallas_call | solution.py:335
  582.3 27.7 %unproject.3 = (bf16[512,2048]{1,0:T(8,128)(2,1)}, bf16[512,2048]{1,0:T(8,128)(2,1)}, bf16[512,2048]{1,0:T(8,128)(2,1)}, bf16[512,2048]{1,0:T(8,128)(2,1)}) custom-call(bf16[2048,768]{1,0:T(8,128)(2,1)} %get-tuple-element.116.refs_0_.refs_2_, bf16[2048,1024]{1,0:T(8,128)(2,1)} %get-tuple-element.112.refs_2_.refs_1_, ...), custom_call_target="tpu_custom_call", output_to_operand_aliasing={{2}: (4, {}), {3}: (6, {})} | custom-call | flops 1503238528 | bytes 2306867 | tf_op jit(solution)/shard_map/unproject/pallas_call | solution.py:335
  610.0 4.0 add_convert_fusion.refs_4_
  616.1 54.2 %outer_rows.3 = (bf16[2048,768]{1,0:T(8,128)(2,1)}, bf16[512,2048]{1,0:T(8,128)(2,1)}, bf16[512,2048]{1,0:T(8,128)(2,1)}) custom-call(bf16[4096,2048]{1,0:T(8,128)(2,1)} %bitcast.27, bf16[2048,768]{1,0:T(8,128)(2,1)} %get-tuple-element.102.refs_0_.refs_1_, bf16[2048,768]{1,0:T(8,128)(2,1)} %get-tuple-element.116.refs_0_.refs_2_, ...), custom_call_target="tpu_custom_call" | custom-call | flops 1288490240 | bytes 2621440 | tf_op jit(solution)/shard_map/outer_rows/pallas_call | solution.py:335
  673.2 2.9 convert_element_type.129.refs_3_
  678.7 8.2 %unnorm.1 = (bf16[512,2048]{1,0:T(8,128)(2,1)}, f32[1,2048]{1,0:T(1,128)}, f32[1,2048]{1,0:T(1,128)}) custom-call(s32[1]{0:T(128)} %bitcast.6.flag, bf16[512,2048]{1,0:T(8,128)(2,1)} %x.3, bf16[512,2048]{1,0:T(8,128)(2,1)} %g.3, f32[1,2048]{1,0:T(1,128)} %bitcast.37, bf16[512,2048]{1,0:T(8,128)(2,1)} %get-tuple-element.119.refs_0_, ...), custom_call_target="tpu_custom_call" | custom-call | flops 3145728 | bytes 1468006 | tf_op jit(solution)/shard_map/unnorm/pallas_call | solution.py:142
  686.9 14.3 %sum_everywhere.1 = (f32[8,2048]{1,0:T(8,128)}, f32[1,1792]{1,0:T(1,128)}) custom-call(f32[1,2048]{1,0:T(1,128)} %get-tuple-element.127.gain, f32[1,2048]{1,0:T(1,128)} %get-tuple-element.128.shift, f32[1,2048]{1,0:T(1,128)} %bitcast.40, f32[1,768]{1,0:T(1,128)} %add.91.qkv, f32[1,1024]{1,0:T(1,128)} %add.92.up), custom_call_target="tpu_custom_call" | custom-call | tf_op jit(solution)/shard_map/sum_everywhere/pallas_call | solution.py:1041
  705.4 9.5 %reduce-scatter.8.cloned.1.call-done = bf16[512,768]{1,0:T(8,128)(2,1)} async-done(((bf16[2048,768]{1,0:T(8,128)(2,1)}), bf16[512,768]{1,0:T(8,128)(2,1)}) %reduce-scatter.8.cloned.1.call-update) | async-done | bytes 786448 | tf_op jit(solution)/shard_map/reduce_scatter | solution.py:1303
  714.8 2.3 fusion.4
  (108 shorter events, 29.7 us)
Async XLA Ops:
  7.2 3.9 copy-start.20
  7.2 4.5 copy-start.21
  7.2 608.9 %reduce-scatter.10.cloned.1.call-start = ((), (), s32[]{:S(2)}) async-start(), calls=%async_computation.5 | async-start | bytes 6553600
  16.3 1.8 copy-start.30
  16.3 1.8 copy-start.31
  16.3 1.9 copy-start.14
  16.3 1.9 copy-start.18
  19.3 1.8 copy-start.15
  19.3 1.8 copy-start.16
  19.3 1.8 copy-start.17
  317.5 32.6 %copy-start.7 = (bf16[512,2048]{1,0:T(8,128)(2,1)S(1)}, bf16[512,2048]{1,0:T(8,128)(2,1)}, u32[]{:S(2)}) copy-start(bf16[512,2048]{1,0:T(8,128)(2,1)} %get-tuple-element.95.refs_3_.refs_10_) | copy-start | bytes 6291460
  378.1 35.7 %copy-start.6 = (bf16[512,2048]{1,0:T(8,128)(2,1)S(1)}, bf16[512,2048]{1,0:T(8,128)(2,1)}, u32[]{:S(2)}) copy-start(bf16[512,2048]{1,0:T(8,128)(2,1)} %get-tuple-element.88.refs_4_.refs_3_) | copy-start | bytes 6291460
  506.8 166.3 %reduce-scatter.6.cloned.1.call-start = ((), (), s32[]{:S(2)}) async-start(), calls=%async_computation.3 | async-start | bytes 5242880 | tf_op jit(solution)/shard_map/reduce_scatter | solution.py:1243
  536.4 178.4 %reduce-scatter.8.cloned.1.call-start = ((), (), s32[]{:S(2)}) async-start(), calls=%async_computation.4 | async-start | bytes 3932160 | tf_op jit(solution)/shard_map/reduce_scatter | solution.py:1303
  538.0 3.9 copy-start.4
  538.0 3.9 copy-start.8
  538.0 3.9 copy-start.9
  582.2 27.7 %copy-start.2 = (bf16[512,2048]{1,0:T(8,128)(2,1)S(1)}, bf16[512,2048]{1,0:T(8,128)(2,1)}, u32[]{:S(2)}) copy-start(bf16[512,2048]{1,0:T(8,128)(2,1)} %get-tuple-element.107.refs_7_.refs_3_) | copy-start | bytes 6291460
  610.0 4.0 copy-start.10
  610.0 4.0 copy-start.12
  670.3 1.8 copy-start.3
  673.2 2.9 copy-start.11
  678.7 39.0 %copy-start.1 = (s32[4,1024]{1,0:T(4,128)S(1)}, s32[4,1024]{1,0:T(4,128)}, u32[]{:S(2)}) copy-start(s32[4,1024]{1,0:T(4,128)} %param.18) | copy-start | bytes 49156
  702.8 14.9 %copy-start.19 = (f32[1,2048]{1,0:T(1,128)}, f32[1,2048]{1,0:T(1,128)S(1)}, u32[]{:S(2)}) copy-start(f32[1,2048]{1,0:T(1,128)S(1)} %get-tuple-element.139) | copy-start | bytes 24580
  (11 other events, 13.0 us)
Sparse Core Ops, SparseCore 0:
  507.0 61.4 reduce-scatter.9
  571.4 52.6 reduce-scatter.5
  670.5 44.2 reduce-scatter.7

commit v4 on v3

--- a/solution.py
+++ b/solution.py
@@ -2,6 +2,7 @@
 
 import jax
 import jax.numpy as jnp
+import numpy as np
 from jax import lax
 from jax.experimental import pallas as pl
 from jax.experimental.pallas import tpu as pltpu
@@ -251,21 +252,22 @@
 
 
 class Riding:
-    def __init__(self, ins, outs, aliased, count, copies):
+    def __init__(self, ins, outs, aliased, count, copies, late=0):
         self.ins, self.outs, self.aliased, self.count, self.copies = ins, outs, aliased, count, copies
+        self.late = late
 
 
 def like(array):
     return jax.ShapeDtypeStruct(array.shape, array.dtype)
 
 
-def gathering(full, *moves):
-    plan = Gather(*moves)
+def gathering(full, *moves, late=()):
+    plan = Gather(*moves, *late)
 
     def copies(at, ins, outs, sent, got):
         return plan.copies(at, outs[0], sent, got)
 
-    return Riding([full], [like(full)], True, plan.count, copies)
+    return Riding([full], [like(full)], True, plan.count, copies, Gather(*late).count)
 
 
 SENDS = {
@@ -317,9 +319,11 @@
         own_outs, ride_outs = some(len(shapes)), [some(len(r.outs)) for r in riding]
         own_scratch = some(len(scratch))
         at = places()
-        copies = []
+        copies, late = [], []
         for r, i, o in zip(riding, ride_ins, ride_outs):
-            copies += r.copies(at, i, o, *some(2))
+            found = r.copies(at, i, o, *some(2))
+            copies += found[: len(found) - r.late]
+            late += found[len(found) - r.late :]
 
         @pl.when(pl.program_id(0) == 0)
         def _():
@@ -331,6 +335,8 @@
         @pl.when(pl.program_id(0) == grid - 1)
         def _():
             finish_all(at, copies)
+            start_all(at, late)
+            finish_all(at, late)
 
     return pl.pallas_call(
         kernel,
@@ -352,33 +358,73 @@
     )(*args, *extra_in)
 
 
-def gather_kernel(tile, groups, x, gain, shift, g, first, second, rows_full, g_full, first_full, second_full, own, kept, first_kept, second_kept, local, w_sent, w_got, *sems):
+def opening_kernel(tile, groups, width, cut, *refs):
+    x, gain, shift, g, *weights = refs[:10]
+    biases, frequency, refs = refs[10:14], refs[14], refs[15:]
+    rows_full, g_full, first_full, second_full, q, k, v, active, hidden, cos, low, high = refs[:12]
+    own, kept, first_kept, second_kept, w, bias, x_tile = refs[12:19]
+    staged, (local, x_sem, out_sem, w_sent, w_got), sems = refs[19:24], refs[24:29], refs[29:]
     at = places()
-    dp = lax.axis_index("dp")
+    core, dp = at["core"], lax.axis_index("dp")
     peers = [{"dp": jnp.bitwise_xor(dp, step)} for step in range(1, groups)]
+    share, depth = own.shape
+    half = share // 2
+    units = hidden.shape[1]
+    lows, highs = (0, half), (half, share)
     greet(at, peers)
+
+    columns = [(0, width), (width, width), (2 * width, width), (3 * width, units)]
     loads = [
-        pltpu.make_async_copy(src, dst, local.at[i])
-        for i, (src, dst) in enumerate(((first, first_kept), (second, second_kept), (g, kept)))
+        pltpu.make_async_copy(src, first_kept.at[:, pl.ds(start, size)], local.at[i])
+        for i, (src, (start, size)) in enumerate(zip(weights[:4], columns))
+    ] + [
+        pltpu.make_async_copy(weights[4], second_kept.at[pl.ds(0, width)], local.at[4]),
+        pltpu.make_async_copy(weights[5], second_kept.at[pl.ds(width, units)], local.at[5]),
+        pltpu.make_async_copy(g, kept, local.at[6]),
     ]
     stores = [
-        pltpu.make_async_copy(src, dst, local.at[i])
-        for i, (src, dst) in enumerate(
-            (
-                (first_kept, first_full.at[dp]),
-                (second_kept, second_full.at[dp]),
-                (kept, g_full.at[3, at["core"]]),
-                (own, rows_full.at[3, at["core"]]),
-            )
-        )
+        pltpu.make_async_copy(first_kept, first_full.at[dp], local.at[0]),
+        pltpu.make_async_copy(second_kept, second_full.at[dp], local.at[1]),
+        pltpu.make_async_copy(kept, g_full.at[3, core], local.at[2]),
+        pltpu.make_async_copy(own, rows_full.at[3, core], local.at[7]),
     ]
-    weights = [
-        [to_device(src, dst.at[dp], w_sent.at[k, i], w_got.at[k, i], peer) for i, peer in enumerate(peers)]
-        for k, (src, dst) in enumerate(((first, first_full), (second, second_full)))
+    spread = [
+        [to_device(src, dst.at[dp], w_sent.at[n, i], w_got.at[n, i], peer) for i, peer in enumerate(peers)]
+        for n, (src, dst) in enumerate(((first_kept, first_full), (second_kept, second_full)))
     ]
-    for copy in loads + weights[0]:
+    plans = dict(
+        n1_low=[(1, *lows)],
+        n1_high=[(1, *highs), ("own", 0, share)],
+        n2_low=[(2, *lows)],
+        n2_high=[(2, *highs)],
+        e2_low=[("first", *lows)],
+        e2_high=[("first", *highs)],
+        n3_low=[(3, *lows)],
+        n3_high=[(3, *highs)],
+        e1_low=[("second", *lows)],
+        e1_high=[("second", *highs)],
+        e0_low=[("third", *lows)],
+        e0_high=[("third", *highs)],
+        g_own=[("own", 0, share)],
+        g1=[(1, 0, cut)],
+    )
+    moves = {
+        name: Gather(*plan).copies(
+            at, g_full if name[0] == "g" else rows_full, sems[2 * i], sems[2 * i + 1]
+        )
+        for i, (name, plan) in enumerate(plans.items())
+    }
+
+    def start(*names):
+        for name in names:
+            start_all(at, moves[name])
+
+    def finish(*names):
+        for name in names:
+            finish_all(at, moves[name])
+
+    for copy in loads:
         copy.start()
-    share = own.shape[0]
 
     @pl.loop(0, share // tile)
     def _(i):
@@ -386,75 +432,182 @@
         values = x[rows, :].astype(F32)
         centered = values - jnp.mean(values, axis=1, keepdims=True)
         scale = lax.rsqrt(jnp.mean(centered * centered, axis=1, keepdims=True) + EPS)
-        own[rows, :] = (centered * scale * gain[...] + shift[...]).astype(BF16)
+        own[rows, :] = (
+            centered * scale * gain[...].astype(F32) + shift[...].astype(F32)
+        ).astype(BF16)
 
     stores[3].start()
-    for load, store in zip(loads, stores):
+    for copy in loads:
+        copy.wait()
+    for copy in spread[0]:
+        copy.start()
+    for copy in stores[:3]:
+        copy.start()
+    stores[3].wait()
+    start("n1_low", "n1_high")
+
+    lane = lax.broadcasted_iota(jnp.int32, (1, 128), 1) % HEAD_DIM
+    position = lax.broadcasted_iota(jnp.int32, cos.shape, 0).astype(F32)
+    angle = position * frequency[...]
+    sine = jnp.sin(angle)
+    cos[...] = jnp.where(lane < ROT, jnp.cos(angle), 1.0)
+    low[...] = jnp.where(lane < ROT // 2, -sine, 0.0)
+    high[...] = jnp.where(jnp.logical_and(lane >= ROT // 2, lane < ROT), sine, 0.0)
+    for ref, (begin, size) in zip(biases, columns):
+        bias[:, begin : begin + size] = ref[...].astype(F32)
+
+    for copy in stores[:3]:
+        copy.wait()
+    start("g_own")
+    for copy in spread[1]:
+        copy.start()
+    finish("n1_low")
+    start("n2_low", "e2_low")
+    finish("n1_high")
+    start("n2_high", "e2_high")
+    finish("n2_low")
+    start("n3_low", "e1_low")
+    for copy in spread[0]:
+        copy.wait()
+    fetch = [
+        pltpu.make_async_copy(
+            first_full.at[d], w.at[pl.ds(d * first_full.shape[1], first_full.shape[1])], local.at[d]
+        )
+        for d in range(groups)
+    ]
+    for copy in fetch:
+        copy.start()
+    for copy in fetch:
+        copy.wait()
+
+    outs = (q, k, v, active, hidden)
+
+    def results(i):
+        part = jnp.where(lax.rem(i, 2) == 0, core, 1 - core)
+        slot = 3 - lax.div(i, 2)
+        rows = pl.ds(pl.multiple_of((2 * slot + part) * share, share), share)
+        return [
+            pltpu.make_async_copy(src.at[lax.rem(i, 2)], dst.at[rows], out_sem.at[lax.rem(i, 2), n])
+            for n, (src, dst) in enumerate(zip(staged, outs))
+        ]
+
+    @pl.loop(0, 8)
+    def _(i):
+        @pl.when(i == 2)
+        def _():
+            finish("n2_high")
+            start("n3_high", "e1_high")
+            finish("e2_low", "e2_high")
+
+        @pl.when(i == 4)
+        def _():
+            finish("e1_low", "e1_high")
+
+        @pl.when(i == 6)
+        def _():
+            finish("n3_low")
+            start("e0_low")
+            finish("n3_high")
+            start("e0_high")
+            finish("g_own")
+            start("g1")
+
+        @pl.when(i == 7)
+        def _():
+            finish("e0_low", "e0_high")
+
+        part = jnp.where(lax.rem(i, 2) == 0, core, 1 - core)
+        load = pltpu.make_async_copy(rows_full.at[3 - lax.div(i, 2), part], x_tile, x_sem)
+        load.start()
+
+        @pl.when(i >= 2)
+        def _():
+            for copy in results(i - 2):
+                copy.wait()
+
         load.wait()
-        store.start()
-    stores[3].wait()
-    half = share // 2
-    lows, highs = (0, half), (half, share)
-    plans = [
-        Gather((1, *lows)),
-        Gather((1, *highs), ("own", 0, share)),
-        Gather((2, *lows), ("first", *lows)),
-        Gather((2, *highs), ("first", *highs)),
-        Gather((3, *lows), ("second", *lows)),
-        Gather((3, *highs), ("second", *highs)),
-        Gather(("third", *lows)),
-        Gather(("third", *highs)),
-    ]
-    moves = [p.copies(at, rows_full, sems[2 * i], sems[2 * i + 1]) for i, p in enumerate(plans)]
-    mine = Gather(("own", 0, share)).copies(at, g_full, sems[16], sems[17])
-    start_all(at, moves[0])
-    start_all(at, moves[1])
-    for store in stores[:3]:
-        store.wait()
-    start_all(at, mine)
-    for copy in weights[1]:
-        copy.start()
-    for i in range(6):
-        finish_all(at, moves[i])
-        start_all(at, moves[i + 2])
-    finish_all(at, moves[6])
-    finish_all(at, moves[7])
-    finish_all(at, mine)
-    for copy in weights[0] + weights[1]:
+        here = pl.ds(pl.multiple_of(part * share, share), share)
+        project_tile(
+            width,
+            x_tile,
+            w,
+            bias,
+            cos.at[here],
+            low.at[here],
+            high.at[here],
+            *(r.at[lax.rem(i, 2)] for r in staged),
+        )
+        for copy in results(i):
+            copy.start()
+
+    for i in (6, 7):
+        for copy in results(i):
+            copy.wait()
+    finish("g1")
+    for copy in spread[1]:
         copy.wait()
 
 
-def gather(ident, x, gain, shift, g, first, second, groups, tile=64):
+OPENING_PLANS = (2, 3, 2, 2, 2, 2, 1, 1, 1, 1, 1, 1, 1, 2)
+
+
+def opening(ident, x, gain, shift, g, weights, biases, groups, length, cut, tile=64):
     rows, depth = x.shape
+    width, units = weights[0].shape[1], weights[3].shape[1]
+    total = 3 * width + units
+    inner = width + units
+    columns = weights[4].shape[1]
+    everything = 8 * rows
     whole = pl.BlockSpec(memory_space=pltpu.VMEM)
     full = jax.ShapeDtypeStruct((4, 2, rows, depth), BF16)
-    sizes = [2, 3, 4, 4, 2, 2, 1, 1, 1]
+    exponent = np.arange(ROT // 2, dtype=np.float32) * np.float32(2.0 / ROT)
+    frequency = np.tile(np.power(np.float32(10000.0), -exponent), 8)[None, :]
+    table = jax.ShapeDtypeStruct((length, 128), F32)
+    narrow = jax.ShapeDtypeStruct((everything, width), BF16)
     return pl.pallas_call(
-        functools.partial(gather_kernel, tile, groups),
-        in_specs=[whole] * 3 + [ANYWHERE] * 3,
-        out_specs=[ANYWHERE] * 4,
+        functools.partial(opening_kernel, tile, groups, width, cut),
+        in_specs=[whole] * 3 + [ANYWHERE] * 7 + [whole] * 5,
+        out_specs=[ANYWHERE] * 9 + [whole] * 3,
         out_shape=[
             full,
             full,
-            jax.ShapeDtypeStruct((groups,) + first.shape, BF16),
-            jax.ShapeDtypeStruct((groups,) + second.shape, BF16),
+            jax.ShapeDtypeStruct((groups, depth // groups, total), BF16),
+            jax.ShapeDtypeStruct((groups, inner, columns), BF16),
+            narrow,
+            narrow,
+            narrow,
+            jax.ShapeDtypeStruct((everything, units), BF16),
+            jax.ShapeDtypeStruct((everything, units), F32),
+            table,
+            table,
+            table,
         ],
         scratch_shapes=[
             pltpu.VMEM((rows, depth), BF16),
             pltpu.VMEM((rows, depth), BF16),
-            pltpu.VMEM(first.shape, BF16),
-            pltpu.VMEM(second.shape, BF16),
-            pltpu.SemaphoreType.DMA((4,)),
+            pltpu.VMEM((depth // groups, total), BF16),
+            pltpu.VMEM((inner, columns), BF16),
+            pltpu.VMEM((depth, total), BF16),
+            pltpu.VMEM((1, total), F32),
+            pltpu.VMEM((rows, depth), BF16),
+            pltpu.VMEM((2, rows, width), BF16),
+            pltpu.VMEM((2, rows, width), BF16),
+            pltpu.VMEM((2, rows, width), BF16),
+            pltpu.VMEM((2, rows, units), BF16),
+            pltpu.VMEM((2, rows, units), F32),
+            pltpu.SemaphoreType.DMA((8,)),
+            pltpu.SemaphoreType.DMA,
+            pltpu.SemaphoreType.DMA((2, 5)),
             pltpu.SemaphoreType.DMA((2, groups - 1)),
             pltpu.SemaphoreType.DMA((2, groups - 1)),
         ]
-        + [pltpu.SemaphoreType.DMA((n,)) for n in sizes for _ in range(2)],
+        + [pltpu.SemaphoreType.DMA((n,)) for n in OPENING_PLANS for _ in range(2)],
         compiler_params=pltpu.CompilerParams(
             vmem_limit_bytes=VMEM_BYTES, collective_id=ident, has_side_effects=True
         ),
-        cost_estimate=cost(10 * rows * depth, 60 * rows * depth),
-        name="gather",
-    )(x, gain, shift, g, first, second)
+        cost_estimate=cost(2 * everything * depth * total, 60 * rows * depth),
+        name="opening",
+    )(x, gain, shift, g, *weights, *biases, jnp.asarray(frequency))
 
 
 def project_tile(width, x, w, bias, cos, low, high, q, k, v, active, hidden):
@@ -754,7 +907,7 @@
         out_shape=shapes + [o for r in extra for o in r.outs],
         input_output_aliases=aliases,
         scratch_shapes=[pltpu.VMEM((2, tile, depth), BF16), pltpu.SemaphoreType.DMA((2,))]
-        + [pltpu.SemaphoreType.DMA((n,)) for n in counts for _ in range(2)]
+        + [pltpu.SemaphoreType.DMA((max(n, 1),)) for n in counts for _ in range(2)]
         + [pltpu.SemaphoreType.DMA((r.count,)) for r in extra for _ in range(2)],
         compiler_params=pltpu.CompilerParams(
             dimension_semantics=("arbitrary",),
@@ -797,24 +950,27 @@
     )
 
 
-def outer_columns_kernel(a, b, g, out):
-    width = a.shape[1]
-    out[0, :width, :] = tn(a[...], g[...]).astype(out.dtype)
+def outer_columns_kernel(parts, b, g, *refs):
+    many, out = refs[:parts], refs[-1]
+    width = many[0].shape[1]
+    total, start = None, 0
+    for a in many:
+        term = tn(a[...], g[start : start + a.shape[0], :])
+        total = term if total is None else total + term
+        start += a.shape[0]
+    out[0, :width, :] = total.astype(out.dtype)
     out[0, width:, :] = tn(b[...], g[...]).astype(out.dtype)
 
 
-def outer_columns(a, b, g, parts, riding=(), ident=None):
+def outer_columns(many, b, g, parts, riding=(), ident=None):
     rows, depth = g.shape
-    width, units = a.shape[1], b.shape[1]
+    width, units = many[0].shape[1], b.shape[1]
     tile = depth // parts
     return launch(
-        outer_columns_kernel,
-        [a, b, g],
-        [
-            once((rows, width), lambda i: (0, 0)),
-            once((rows, units), lambda i: (0, 0)),
-            pl.BlockSpec((rows, tile), lambda i: (0, i)),
-        ],
+        functools.partial(outer_columns_kernel, len(many)),
+        [b, g, *many],
+        [once((rows, units), lambda i: (0, 0)), pl.BlockSpec((rows, tile), lambda i: (0, i))]
+        + [once(a.shape, lambda i: (0, 0)) for a in many],
         [pl.BlockSpec((1, width + units, tile), lambda i: (i, 0, 0))],
         [jax.ShapeDtypeStruct((parts, width + units, tile), BF16)],
         parts,
@@ -861,11 +1017,13 @@
         log_sums[:, begin : begin + tile] = sums.T[:8, :]
 
 
-def attend(q, k, v, column_ids, row_ids, riding=(), ident=None):
-    rows, width = q.shape
-    seqs, _, length = row_ids.shape
+def attend(first, count, q, k, v, column_ids, row_ids, riding=(), ident=None):
+    width = q.shape[1]
+    length = row_ids.shape[2]
+    rows, seqs = count * length, count
     heads = width // HEAD_DIM
-    seq = pl.BlockSpec((length, width), lambda s: (s, 0))
+    seq = pl.BlockSpec((length, width), lambda s: (first + s, 0))
+    out = pl.BlockSpec((length, width), lambda s: (s, 0))
     return launch(
         attend_kernel,
         [q, k, v, column_ids, row_ids],
@@ -873,10 +1031,10 @@
             seq,
             seq,
             seq,
-            pl.BlockSpec((length, 1), lambda s: (s, 0)),
-            pl.BlockSpec((None, 1, length), lambda s: (s, 0, 0)),
+            pl.BlockSpec((length, 1), lambda s: (first + s, 0)),
+            pl.BlockSpec((None, 1, length), lambda s: (first + s, 0, 0)),
         ],
-        [seq, pl.BlockSpec((8, length), lambda s: (0, s))],
+        [out, pl.BlockSpec((8, length), lambda s: (0, s))],
         [jax.ShapeDtypeStruct((rows, width), BF16), jax.ShapeDtypeStruct((8, rows), F32)],
         seqs,
         "attend",
@@ -931,7 +1089,7 @@
     sums[:, 2 * width :] += jnp.sum(turned.astype(F32), axis=0, keepdims=True)
 
 
-def unattend(first, count, q, k, v, g, g_first, log_sums, column_ids, row_ids, tables, riding=(), ident=None, wait_for=()):
+def unattend(first, count, q, k, v, g, g_first, log_sums, sums_first, column_ids, row_ids, tables, riding=(), ident=None, wait_for=()):
     width = q.shape[1]
     length = row_ids.shape[2]
     rows, seqs = count * length, count
@@ -946,7 +1104,7 @@
             seq,
             seq,
             pl.BlockSpec((length, width), lambda s: (g_first + s, 0)),
-            pl.BlockSpec((8, length), lambda s: (0, first + s)),
+            pl.BlockSpec((8, length), lambda s: (0, sums_first + s)),
             pl.BlockSpec((length, 1), lambda s: (first + s, 0)),
             pl.BlockSpec((None, 1, length), lambda s: (first + s, 0, 0)),
             table,
@@ -1094,72 +1252,100 @@
     else:
         order = jnp.arange(seqs, dtype=jnp.int32)
 
-    first = jnp.concatenate([query_weight, key_weight, value_weight, up_weight], axis=1)
-    second = jnp.concatenate([out_weight, down_weight], axis=0)
-    bias = jnp.concatenate([query_bias, key_bias, value_bias, up_bias]).astype(F32)[None, :]
-    tables = rotary_tables(length)
     ids = block_ids[order]
     column_ids = ids.reshape(seqs * length, 1)
     row_ids = ids.reshape(seqs, 1, length)
     pair = seqs // 2
     everything = seqs * length
-
     idents = iter(range(1, 100))
 
     if paired:
         kept = lambda values: jnp.where(inner == 1, values, jnp.zeros_like(values))
-        rows, full, first_full, second_full = gather(
-            next(idents), inputs, gain, shift, grad_out, first, second, groups
+        cuts = lambda fraction: int(share * fraction) // 32 * 32
+        g1, g1_more = cuts(0.25), cuts(0.56)
+        rows, full, first_full, second_full, q, k, v, active, hidden, *tables = opening(
+            next(idents),
+            inputs,
+            norm_gain[None, :],
+            norm_bias[None, :],
+            grad_out,
+            [query_weight, key_weight, value_weight, up_weight, out_weight, down_weight],
+            [b[None, :] for b in (query_bias, key_bias, value_bias, up_bias)],
+            groups,
+            length,
+            g1,
         )
         rows = rows.reshape(everything, depth)
         first_full = first_full.reshape(depth, 3 * width + units)
-        q, k, v, active, hidden, full = project(
-            rows,
-            first_full,
-            bias,
-            tables,
-            width,
-            units,
-            length,
-            riding=[gathering(full, (1, 0, share))],
-            ident=next(idents),
-        )
-        half, more = share // 2, share * 9 // 16
-        attended, log_sums, full = attend(
-            q,
-            k,
-            v,
-            column_ids,
-            row_ids,
-            riding=[gathering(full, (2, 0, more), ("first", 0, share))],
-            ident=next(idents),
-        )
-        *far, full = core_sum(
-            mix_body,
-            next(idents),
+
+        def heads(at, riding):
+            return attend(at, pair, q, k, v, column_ids, row_ids, riding=riding, ident=next(idents))
+
+        def mixed(values, at, riding):
+            return core_sum(
+                mix_body,
+                next(idents),
+                pair,
+                length,
+                [(values, 0), (active, at)],
+                second_full,
+                depth,
+                "mix",
+                riding=riding,
+            )
+
+        def unheads(at, count, g, g_at, sums, sums_at, riding, wait_for=()):
+            return unattend(
+                at,
+                count,
+                q,
+                k,
+                v,
+                g,
+                g_at,
+                sums,
+                sums_at,
+                column_ids,
+                row_ids,
+                tables,
+                riding=riding,
+                ident=next(idents),
+                wait_for=wait_for,
+            )
+
+        def unprojected(count, grads, riding):
+            return core_sum(
+                unproject_body,
+                next(idents),
+                count,
+                length,
+                grads,
+                first_full,
+                depth,
+                "unproject",
+                riding=riding,
+            )
+
+        far_attended, far_sums, full = heads(0, [gathering(full, (1, g1, g1_more))])
+        *far, full = mixed(far_attended, 0, [gathering(full, (1, g1_more, share))])
+
+        part = cuts(0.44)
+        near_attended, near_sums, full, end = heads(
             pair,
-            length,
-            [(attended, 0), (active, 0)],
-            second_full,
-            depth,
-            "mix",
-            riding=[gathering(full, (2, more, share))],
-        )
-        *near, full, end = core_sum(
-            mix_body,
-            next(idents),
+            [
+                gathering(full, (2, 0, part), ("first", 0, share)),
+                sending(far[0], "in", 0, part),
+            ],
+        )
+        *near, full, end = mixed(
+            near_attended,
             pair,
-            length,
-            [(attended, pair), (active, pair)],
-            second_full,
-            depth,
-            "mix",
-            riding=[
-                gathering(full, (3, 0, half), ("second", 0, share)),
-                sending(far[0], "in", 0, half),
-            ],
-        )
-        near_attended_grad, near_hidden_grad, near_up_sum, full, end = unmix_gather(
+            [gathering(full, (2, part, share)), sending(far[0], "in", part, share, end)],
+        )
+
+        crossing = add_up(far[1], end)
+        part = cuts(0.4)
+        near_attended_grad, near_hidden_grad, near_up_sum, full, end, middle = unmix_gather(
             full,
             second_full,
             hidden,
@@ -1167,15 +1353,37 @@
             pair,
             pair,
             length,
-            [(3, half, share), ("third", 0, half)],
-            [("third", half, share)],
+            [(3, 0, part), ("second", 0, share)],
+            [],
             next(idents),
-            riding=[sending(far[0], "in", half, share, end)],
+            riding=[sending(far[1], "in", 0, part), sending(crossing, "middle", 0, part)],
+        )
+        near_grad, near_sum, full, end, middle = unheads(
+            pair,
+            pair,
+            near_attended_grad,
+            0,
+            near_sums,
+            0,
+            [
+                gathering(
+                    full, (3, part, share), ("third", 0, part), late=[("third", part, share)]
+                ),
+                sending(far[1], "in", part, share, end),
+                sending(crossing, "middle", part, share, middle),
+            ],
         )
         upstream = full.reshape(everything, depth)
-        cut = share * 3 // 8
-        crossing = add_up(far[1], end)
-        far_attended_grad, far_hidden_grad, far_up_sum, end, middle = unmix(
+
+        to_side = add_up(near[0], kept(middle))
+        to_middle = add_up(far[0], end)
+        mine = near[1]
+        part, more = cuts(0.4), cuts(0.75)
+
+        def outward(lo, hi, side=None, middle=None):
+            return [sending(to_side, "side", lo, hi, side), sending(to_middle, "middle", lo, hi, middle)]
+
+        far_attended_grad, far_hidden_grad, far_up_sum, side, middle = unmix(
             upstream,
             second_full,
             hidden,
@@ -1183,71 +1391,52 @@
             0,
             pair,
             length,
-            riding=[sending(far[1], "in", 0, cut), sending(crossing, "middle", 0, cut)],
+            riding=outward(0, part),
             ident=next(idents),
         )
         up_sum = near_up_sum + far_up_sum
-        far_grad, far_sum, end, middle = unattend(
-            0,
-            pair,
-            q,
-            k,
-            v,
-            far_attended_grad,
-            0,
-            log_sums,
-            column_ids,
-            row_ids,
-            tables,
-            riding=[
-                sending(far[1], "in", cut, share, end),
-                sending(crossing, "middle", cut, share, middle),
-            ],
-            ident=next(idents),
-        )
-        to_side = add_up(near[0], kept(middle))
-        to_middle = add_up(far[0], end)
-        mine = near[1]
-        *far, side, middle = core_sum(
-            unproject_body,
-            next(idents),
-            pair,
-            length,
-            [(far_grad, 0), (far_hidden_grad, 0)],
-            first_full,
-            depth,
-            "unproject",
-            riding=[sending(to_side, "side", 0, half), sending(to_middle, "middle", 0, half)],
-        )
-        second_part, side, middle, end = outer_columns(
-            attended,
+        grads_0, sum_0, side, middle = unheads(
+            0, 1, far_attended_grad, 0, far_sums, 0, outward(part, more, side, middle)
+        )
+        far_0, side, middle = unprojected(
+            1, [(grads_0, 0), (far_hidden_grad, 0)], outward(more, share, side, middle)
+        )
+        terms = [mine, side, kept(middle)]
+
+        part, more = cuts(0.5), cuts(0.8)
+        second_part, end = outer_columns(
+            [far_attended, near_attended],
             active,
             upstream,
             groups,
-            riding=[
-                sending(to_side, "side", half, share, side),
-                sending(to_middle, "middle", half, share, middle),
-                sending(far[0], "in", 0, half),
-            ],
+            riding=[sending(far_0, "in", 0, part)],
             ident=next(idents),
         )
-        terms = [mine, side, kept(middle)]
         second_grad = lax.psum_scatter(second_part, "dp", scatter_dimension=0)
-        up_part, end = outer_rows(
-            rows,
-            [far_hidden_grad, near_hidden_grad],
-            riding=[sending(far[0], "in", half, share, end)],
-            ident=next(idents),
+        grads_1, sum_1, end = unheads(
+            1,
+            1,
+            far_attended_grad,
+            1,
+            far_sums,
+            1,
+            [sending(far_0, "in", part, more, end)],
             wait_for=[second_part],
         )
-        up_grad = lax.psum_scatter(up_part, "dp", scatter_dimension=0, tiled=True)
+        far_1, end = unprojected(
+            1, [(grads_1, 0), (far_hidden_grad, 1)], [sending(far_0, "in", more, share, end)]
+        )
     else:
+        tables = rotary_tables(length)
+        first = jnp.concatenate([query_weight, key_weight, value_weight, up_weight], axis=1)
+        second = jnp.concatenate([out_weight, down_weight], axis=0)
+        bias = jnp.concatenate([query_bias, key_bias, value_bias, up_bias]).astype(F32)[None, :]
         first_full = lax.all_gather(first, "dp", axis=0, tiled=True)
         second_full = lax.all_gather(second, "dp", axis=0)
         rows = lax.all_gather(norm(inputs, gain, shift), "tensor", axis=0, tiled=True)
         upstream = lax.all_gather(grad_out, "tensor", axis=0, tiled=True)
         q, k, v, active, hidden = project(rows, first_full, bias, tables, width, units, length)
-        attended, log_sums = attend(q, k, v, column_ids, row_ids)
+        attended, log_sums = attend(0, seqs, q, k, v, column_ids, row_ids)
         whole = each_tile(mix_body, [attended, active], second_full, depth, "mix")
         terms = [lax.psum_scatter(whole, "tensor", scatter_dimension=0, tiled=True)]
         attended_grad, hidden_grad, up_sum = unmix(
@@ -1259,43 +1448,30 @@
     output = total.astype(BF16)
 
     if paired:
-        crossing = add_up(far[1], end)
-        near_grad, near_sum, end, middle = unattend(
-            pair,
-            pair,
-            q,
-            k,
-            v,
-            near_attended_grad,
-            0,
-            log_sums,
-            column_ids,
-            row_ids,
-            tables,
-            riding=[sending(far[1], "in", 0, more), sending(crossing, "middle", 0, more)],
+        crossing = add_up(far_1, end)
+        part = cuts(0.5)
+        up_part, end, middle = outer_rows(
+            rows,
+            [far_hidden_grad, near_hidden_grad],
+            riding=[sending(far_1, "in", 0, part), sending(crossing, "middle", 0, part)],
             ident=next(idents),
             wait_for=[output],
         )
-        *near, end, middle = core_sum(
-            unproject_body,
-            next(idents),
+        up_grad = lax.psum_scatter(up_part, "dp", scatter_dimension=0, tiled=True)
+        *near, end, middle = unprojected(
             pair,
-            length,
             [(near_grad, 0), (near_hidden_grad, 0)],
-            first_full,
-            depth,
-            "unproject",
-            riding=[
-                sending(far[1], "in", more, share, end),
-                sending(crossing, "middle", more, share, middle),
+            [
+                sending(far_1, "in", part, share, end),
+                sending(crossing, "middle", part, share, middle),
             ],
         )
-        qkv_sum = far_sum + near_sum
+        qkv_sum = sum_0 + sum_1 + near_sum
         to_side = add_up(near[0], kept(middle))
-        to_middle = add_up(far[0], end)
+        to_middle = add_up(far_0, end)
         first_part, side, middle = outer_rows(
             rows,
-            [far_grad, near_grad],
+            [grads_0, grads_1, near_grad],
             riding=[sending(to_side, "side", 0, share), sending(to_middle, "middle", 0, share)],
             ident=next(idents),
             wait_for=[second_grad],
@@ -1305,11 +1481,11 @@
     else:
         inner = jnp.ones((), jnp.int32)
         qkv_grad, qkv_sum = unattend(
-            0, seqs, q, k, v, attended_grad, 0, log_sums, column_ids, row_ids, tables
+            0, seqs, q, k, v, attended_grad, 0, log_sums, 0, column_ids, row_ids, tables
         )
         whole = each_tile(unproject_body, [qkv_grad, hidden_grad], first_full, depth, "unproject")
         terms = [lax.psum_scatter(whole, "tensor", scatter_dimension=0, tiled=True)]
-        (second_part,) = outer_columns(attended, active, upstream, groups)
+        (second_part,) = outer_columns([attended], active, upstream, groups)
         (first_part,) = outer_rows(rows, [qkv_grad])
         (up_part,) = outer_rows(rows, [hidden_grad])
         second_grad = lax.psum_scatter(second_part, "dp", scatter_dimension=0)

time: 728 us -> 688 us (0.945)
  Pallas kernels: 643 us -> 609 us
    pallas_call x12 -> x14, Pallas kernels: 438 us -> 401 us  [launch(): pl.pallas_call(kernel, grid=(grid,), in_specs=ins + [ANYWHERE] * len(extr...]
    pallas_call x1, Pallas kernels: 149 us -> 163 us  [opening(): pl.pallas_call(functools.partial(opening_kernel, tile, groups, width, cut...]
    pallas_call x1, Pallas kernels: 32.6 us -> 23.8 us  [unmix_gather(): pl.pallas_call(kernel, grid=(rows // tile,), in_specs=[once(w.shape, lamb...]
  transfers between devices with their start and end apart: 3 -> 3, of which waited for: 1 -> 1; matrix products, arithmetic and copies ran while one was open for 4% -> 4% of each run, Pallas kernels for 23% -> 26%
where the time goes in v4:
time: 688 us; the launch traced here: 681 us
  Pallas kernels  609 us (89%)
  other arithmetic  30.3 us (4%)
  local copies, waits for them, and re-layouts  17.8 us (3%)
  between operations  14.5 us (2%)
  waiting for transfers between devices  9.14 us (1%)
    pallas_call x14, Pallas kernels, launch(): pl.pallas_call(kernel, grid=(grid,), in_specs=ins + [ANYWHERE] * len(extr...  401 us
    pallas_call x1, Pallas kernels, opening(): pl.pallas_call(functools.partial(opening_kernel, tile, groups, width, cut...  163 us
    pallas_call x1, Pallas kernels, unmix_gather(): pl.pallas_call(kernel, grid=(rows // tile,), in_specs=[once(w.shape, lamb...  23.8 us
    convert_element_type x5, other arithmetic, add_up(): return total.astype(BF16)  21.1 us
  transfers between devices with their start and end apart: 3, of which 1 were waited for; matrix products, arithmetic and copies ran while one was open for 4% of the time, Pallas kernels for 26%

profile of v4, /device:TPU:0, one launch (start us, length us, event | category | flops | bytes accessed | tf_op | source)
XLA Modules:
  0.0 681.5 jit_solution(13474705585742305085)
XLA Ops:
  14.6 163.1 %opening.1 = (bf16[4,2,512,2048]{3,2,1,0:T(8,128)(2,1)}, bf16[4,2,512,2048]{3,2,1,0:T(8,128)(2,1)}, bf16[4,512,1792]{2,1,0:T(8,128)(2,1)}, bf16[4,1280,512]{2,1,...) custom-call(bf16[512,2048]{1,0:T(8,128)(2,1)} %x.1, ...), custom_call_target="tpu_custom_call" | custom-call | flops 3006477056 | bytes 6291456 | tf_op jit(solution)/shard_map/opening/pallas_call | solution.py:567
  177.8 17.1 %attend.2 = (bf16[2048,256]{1,0:T(8,128)(2,1)}, f32[8,2048]{1,0:T(8,128)}, bf16[4,2,512,2048]{3,2,1,0:T(8,128)(2,1)}) custom-call(bf16[4096,256]{1,0:T(8,128)(2,1)} %get-tuple-element.87.refs_0_, bf16[4096,256]{1,0:T(8,128)(2,1)} %get-tuple-element.88.refs_1_, bf16[4096,256]{1,0:T(8,128)(2,1)} %get-tuple-element.89.refs_2_, ...), custom_call_target="tpu_custom_call", output_to_operand_aliasing={{2}: (5, {})} | custom-call | flops 1374389504 | bytes 419430 | tf_op jit(solution)/shard_map/attend/pallas_call | solution.py:341
  194.9 30.5 %mix.2 = (bf16[512,2048]{1,0:T(8,128)(2,1)}, bf16[512,2048]{1,0:T(8,128)(2,1)}, bf16[4,2,512,2048]{3,2,1,0:T(8,128)(2,1)}) custom-call(bf16[2048,256]{1,0:T(8,128)(2,1)} %get-tuple-element.91.refs_0_.refs_2_, bf16[4096,1024]{1,0:T(8,128)(2,1)} %get-tuple-element.92.refs_1_.refs_0_, ...), custom_call_target="tpu_custom_call", output_to_operand_aliasing={{2}: (3, {})} | custom-call | flops 1073741824 | bytes 1887436 | tf_op jit(solution)/shard_map/mix/pallas_call | solution.py:341
  225.3 25.4 %attend.3 = (bf16[2048,256]{1,0:T(8,128)(2,1)}, f32[8,2048]{1,0:T(8,128)}, bf16[4,2,512,2048]{3,2,1,0:T(8,128)(2,1)}, bf16[512,2048]{1,0:T(8,128)(2,1)}) custom-call(bf16[4096,256]{1,0:T(8,128)(2,1)} %get-tuple-element.87.refs_0_, bf16[4096,256]{1,0:T(8,128)(2,1)} %get-tuple-element.88.refs_1_, ...), custom_call_target="tpu_custom_call", output_to_operand_aliasing={{2}: (5, {})} | custom-call | flops 1374389504 | bytes 419430 | tf_op jit(solution)/shard_map/attend/pallas_call | solution.py:341
  250.8 33.7 %mix.3 = (bf16[512,2048]{1,0:T(8,128)(2,1)}, bf16[512,2048]{1,0:T(8,128)(2,1)}, bf16[4,2,512,2048]{3,2,1,0:T(8,128)(2,1)}, bf16[512,2048]{1,0:T(8,128)(2,1)}) custom-call(bf16[2048,256]{1,0:T(8,128)(2,1)} %get-tuple-element.97.refs_0_.refs_3_, bf16[4096,1024]{1,0:T(8,128)(2,1)} %get-tuple-element.92.refs_1_.refs_0_, ...), custom_call_target="tpu_custom_call", output_to_operand_aliasing={{2}: (3, {}), {3}: (5, {})} | custom-call | flops 1073741824 | bytes 1887436 | tf_op jit(solution)/shard_map/mix/pallas_call | solution.py:341
  284.5 3.8 add_convert_fusion.6.refs_4_.refs_13_
  288.3 23.8 %unmix.2 = (bf16[2048,256]{1,0:T(8,128)(2,1)}, bf16[2048,1024]{1,0:T(8,128)(2,1)}, f32[1,1024]{1,0:T(1,128)}, bf16[4,2,512,2048]{3,2,1,0:T(8,128)(2,1)}, bf16[51...) custom-call(bf16[4,1280,512]{2,1,0:T(8,128)(2,1)} %get-tuple-element.93.refs_2_.refs_0_.refs_1_, ...), custom_call_target="tpu_custom_call", output_to_operand_aliasing={{3}: (2, {})} | custom-call | flops 1073741824 | bytes 2621440 | tf_op jit(solution)/shard_map/unmix/pallas_call | solution.py:897
  312.1 38.6 %unattend.3 = (bf16[2048,768]{1,0:T(8,128)(2,1)}, f32[1,768]{1,0:T(1,128)}, bf16[4,2,512,2048]{3,2,1,0:T(8,128)(2,1)}, bf16[512,2048]{1,0:T(8,128)(2,1)}, bf16[512,2048]{1,0:T(8,128)(2,1)}) custom-call(bf16[4096,256]{1,0:T(8,128)(2,1)} %get-tuple-element.87.refs_0_, ...), custom_call_target="tpu_custom_call", output_to_operand_aliasing={{2}: (10, {}), {3}: (12, {}), {4}: (14, {})} | custom-call | flops 3435973888 | bytes 734003 | tf_op jit(solution)/shard_map/unattend/pallas_call | solution.py:341
  350.7 6.6 add_convert_fusion.4
  357.3 25.1 %unmix.3 = (bf16[2048,256]{1,0:T(8,128)(2,1)}, bf16[2048,1024]{1,0:T(8,128)(2,1)}, f32[1,1024]{1,0:T(1,128)}, bf16[512,2048]{1,0:T(8,128)(2,1)}, bf16[512,2048]{1,0:T(8,128)(2,1)}) custom-call(bf16[4096,2048]{1,0:T(8,128)(2,1)} %bitcast.21, bf16[4,1280,512]{2,1,0:T(8,128)(2,1)} %get-tuple-element.93.refs_2_.refs_0_.refs_1_, ...), custom_call_target="tpu_custom_call" | custom-call | flops 1073741824 | bytes 2621440 | tf_op jit(solution)/shard_map/unmix/pallas_call | solution.py:341
  382.4 24.1 %unattend.4 = (bf16[1024,768]{1,0:T(8,128)(2,1)}, f32[1,768]{1,0:T(1,128)}, bf16[512,2048]{1,0:T(8,128)(2,1)}, bf16[512,2048]{1,0:T(8,128)(2,1)}) custom-call(bf16[4096,256]{1,0:T(8,128)(2,1)} %get-tuple-element.87.refs_0_, bf16[4096,256]{1,0:T(8,128)(2,1)} %get-tuple-element.88.refs_1_, ...), custom_call_target="tpu_custom_call", output_to_operand_aliasing={{2}: (11, {}), {3}: (13, {})} | custom-call | flops 1717986944 | bytes 367001 | tf_op jit(solution)/shard_map/unattend/pallas_call | solution.py:341
  406.5 19.4 %unproject.3 = (bf16[512,2048]{1,0:T(8,128)(2,1)}, bf16[512,2048]{1,0:T(8,128)(2,1)}, bf16[512,2048]{1,0:T(8,128)(2,1)}) custom-call(bf16[1024,768]{1,0:T(8,128)(2,1)} %get-tuple-element.121.refs_0_.refs_1_, bf16[2048,1024]{1,0:T(8,128)(2,1)} %get-tuple-element.122.refs_1_, ...), custom_call_target="tpu_custom_call", output_to_operand_aliasing={{1}: (4, {}), {2}: (6, {})} | custom-call | flops 751619264 | bytes 1520435 | tf_op jit(solution)/shard_map/unproject/pallas_call | solution.py:341
  425.9 31.0 %outer_columns.1 = (bf16[4,1280,512]{2,1,0:T(8,128)(2,1)}, bf16[512,2048]{1,0:T(8,128)(2,1)}) custom-call(bf16[4096,1024]{1,0:T(8,128)(2,1)} %get-tuple-element.92.refs_1_.refs_0_, bf16[4096,2048]{1,0:T(8,128)(2,1)} %bitcast.22, bf16[2048,256]{1,0:T(8,128)(2,1)} %get-tuple-element.91.refs_0_.refs_2_, bf16[2048,256]{1,0:T(8,128)(2,1)} %get-tuple-element.97.refs_0_.refs_3_, ...), custom_call_target="tpu_custom_call" | custom-call | flops 2147483648 | bytes 3250585 | tf_op jit(solution)/shard_map/outer_columns/pallas_call | solution.py:341
  457.6 19.7 %unattend.5 = (bf16[1024,768]{1,0:T(8,128)(2,1)}, f32[1,768]{1,0:T(1,128)}, bf16[512,2048]{1,0:T(8,128)(2,1)}) custom-call(bf16[4096,256]{1,0:T(8,128)(2,1)} %get-tuple-element.87.refs_0_, bf16[4096,256]{1,0:T(8,128)(2,1)} %get-tuple-element.88.refs_1_, bf16[4096,256]{1,0:T(8,128)(2,1)} %get-tuple-element.89.refs_2_, ...), custom_call_target="tpu_custom_call", output_to_operand_aliasing={{2}: (11, {})} | custom-call | flops 1717986944 | bytes 367001 | tf_op jit(solution)/shard_map/unattend/pallas_call | solution.py:341
  477.2 18.6 %unproject.4 = (bf16[512,2048]{1,0:T(8,128)(2,1)}, bf16[512,2048]{1,0:T(8,128)(2,1)}) custom-call(bf16[1024,768]{1,0:T(8,128)(2,1)} %get-tuple-element.133.refs_0_.refs_2_, bf16[2048,1024]{1,0:T(8,128)(2,1)} %get-tuple-element.122.refs_1_, bf16[2048,1792]{1,0:T(8,128)(2,1)} %bitcast.31, ...), custom_call_target="tpu_custom_call", output_to_operand_aliasing={{1}: (4, {})} | custom-call | flops 751619264 | bytes 1520435 | tf_op jit(solution)/shard_map/unproject/pallas_call | solution.py:341
  495.8 4.6 add_convert_fusion.2.refs_4_.refs_5_
  500.5 3.3 add_convert_fusion.3.refs_5_
  503.7 29.5 %outer_rows.2 = (bf16[2048,1024]{1,0:T(8,128)(2,1)}, bf16[512,2048]{1,0:T(8,128)(2,1)}, bf16[512,2048]{1,0:T(8,128)(2,1)}) custom-call(bf16[4096,2048]{1,0:T(8,128)(2,1)} %bitcast.28, bf16[2048,1024]{1,0:T(8,128)(2,1)} %get-tuple-element.122.refs_1_, bf16[2048,1024]{1,0:T(8,128)(2,1)} %get-tuple-element.129.refs_2_.refs_1_, ...), custom_call_target="tpu_custom_call" | custom-call | flops 1717986944 | bytes 2936012 | tf_op jit(solution)/shard_map/outer_rows/pallas_call | solution.py:341
  533.3 32.4 %unproject.5 = (bf16[512,2048]{1,0:T(8,128)(2,1)}, bf16[512,2048]{1,0:T(8,128)(2,1)}, bf16[512,2048]{1,0:T(8,128)(2,1)}, bf16[512,2048]{1,0:T(8,128)(2,1)}) custom-call(bf16[2048,768]{1,0:T(8,128)(2,1)} %get-tuple-element.128.refs_0_.refs_3_, bf16[2048,1024]{1,0:T(8,128)(2,1)} %get-tuple-element.129.refs_2_.refs_1_, ...), custom_call_target="tpu_custom_call", output_to_operand_aliasing={{2}: (4, {}), {3}: (6, {})} | custom-call | flops 1503238528 | bytes 2306867 | tf_op jit(solution)/shard_map/unproject/pallas_call | solution.py:341
  565.8 4.0 add_convert_fusion.refs_5_
  571.9 56.0 %outer_rows.3 = (bf16[2048,768]{1,0:T(8,128)(2,1)}, bf16[512,2048]{1,0:T(8,128)(2,1)}, bf16[512,2048]{1,0:T(8,128)(2,1)}) custom-call(bf16[4096,2048]{1,0:T(8,128)(2,1)} %bitcast.29, bf16[1024,768]{1,0:T(8,128)(2,1)} %get-tuple-element.121.refs_0_.refs_1_, bf16[1024,768]{1,0:T(8,128)(2,1)} %get-tuple-element.133.refs_0_.refs_2_, ...), custom_call_target="tpu_custom_call" | custom-call | flops 1288490240 | bytes 2621440 | tf_op jit(solution)/shard_map/outer_rows/pallas_call | solution.py:341
  637.3 8.3 %unnorm.1 = (bf16[512,2048]{1,0:T(8,128)(2,1)}, f32[1,2048]{1,0:T(1,128)}, f32[1,2048]{1,0:T(1,128)}) custom-call(s32[1]{0:T(128)} %bitcast.3.flag, bf16[512,2048]{1,0:T(8,128)(2,1)} %x.1, bf16[512,2048]{1,0:T(8,128)(2,1)} %g.1, f32[1,2048]{1,0:T(1,128)} %reshape_convert_fusion.gain, bf16[512,2048]{1,0:T(8,128)(2,1)} %get-tuple-element.140.refs_0_, ...), custom_call_target="tpu_custom_call" | custom-call | flops 3145728 | bytes 1468006 | tf_op jit(solution)/shard_map/unnorm/pallas_call | solution.py:143
  645.6 13.0 %sum_everywhere.1 = (f32[8,2048]{1,0:T(8,128)}, f32[1,1792]{1,0:T(1,128)}) custom-call(f32[1,2048]{1,0:T(1,128)} %get-tuple-element.148.gain, f32[1,2048]{1,0:T(1,128)} %get-tuple-element.149.shift, f32[1,2048]{1,0:T(1,128)} %bitcast.36, f32[1,768]{1,0:T(1,128)} %add_add_fusion.qkv, f32[1,1024]{1,0:T(1,128)} %add.96.up), custom_call_target="tpu_custom_call" | custom-call | tf_op jit(solution)/shard_map/sum_everywhere/pallas_call | solution.py:1199
  662.7 9.1 %reduce-scatter.8.cloned.1.call-done = bf16[512,768]{1,0:T(8,128)(2,1)} async-done(((bf16[2048,768]{1,0:T(8,128)(2,1)}), bf16[512,768]{1,0:T(8,128)(2,1)}) %reduce-scatter.8.cloned.1.call-update) | async-done | bytes 786448 | tf_op jit(solution)/shard_map/reduce_scatter | solution.py:1479
  (90 shorter events, 26.5 us)
Async XLA Ops:
  7.2 3.9 copy-start.14
  7.2 4.5 copy-start.15
  7.2 5.1 copy-start.23
  7.2 5.7 copy-start.24
  7.2 6.2 copy-start.25
  7.2 6.8 copy-start.26
  7.3 564.7 %reduce-scatter.10.cloned.1.call-start = ((), (), s32[]{:S(2)}) async-start(), calls=%async_computation.5 | async-start | bytes 6553600
  250.8 33.7 %copy-start.4 = (bf16[512,2048]{1,0:T(8,128)(2,1)S(1)}, bf16[512,2048]{1,0:T(8,128)(2,1)}, u32[]{:S(2)}) copy-start(bf16[512,2048]{1,0:T(8,128)(2,1)} %get-tuple-element.103.refs_3_.refs_11_) | copy-start | bytes 6291460
  312.1 38.6 %copy-start.3 = (bf16[512,2048]{1,0:T(8,128)(2,1)S(1)}, bf16[512,2048]{1,0:T(8,128)(2,1)}, u32[]{:S(2)}) copy-start(bf16[512,2048]{1,0:T(8,128)(2,1)} %get-tuple-element.96.refs_6_.refs_4_) | copy-start | bytes 6291460
  456.9 174.9 %reduce-scatter.6.cloned.1.call-start = ((), (), s32[]{:S(2)}) async-start(), calls=%async_computation.3 | async-start | bytes 5242880 | tf_op jit(solution)/shard_map/reduce_scatter | solution.py:1460
  477.2 23.2 %copy-start.12 = (bf16[512,2048]{1,0:T(8,128)(2,1)S(1)}, bf16[512,2048]{1,0:T(8,128)(2,1)}, u32[]{:S(2)}) copy-start(bf16[512,2048]{1,0:T(8,128)(2,1)} %get-tuple-element.100) | copy-start | bytes 6291460
  495.8 4.6 copy-start.5
  495.8 4.6 copy-start.6
  495.8 4.6 copy-start.8
  533.3 138.5 %reduce-scatter.8.cloned.1.call-start = ((), (), s32[]{:S(2)}) async-start(), calls=%async_computation.4 | async-start | bytes 3932160 | tf_op jit(solution)/shard_map/reduce_scatter | solution.py:1479
  533.3 32.5 %copy-start.2 = (bf16[512,2048]{1,0:T(8,128)(2,1)S(1)}, bf16[512,2048]{1,0:T(8,128)(2,1)}, u32[]{:S(2)}) copy-start(bf16[512,2048]{1,0:T(8,128)(2,1)} %get-tuple-element.130.refs_4_.refs_10_.refs_3_) | copy-start | bytes 6291460
  565.8 4.0 copy-start.9
  565.8 4.0 copy-start.11
  628.0 3.2 copy-start.20
  628.0 3.1 copy-start.21
  628.0 3.1 copy-start.22
  630.6 4.1 copy-start.10
  637.3 37.4 %copy-start.1 = (s32[4,1024]{1,0:T(4,128)S(1)}, s32[4,1024]{1,0:T(4,128)}, u32[]{:S(2)}) copy-start(s32[4,1024]{1,0:T(4,128)} %param.19) | copy-start | bytes 49156
  660.2 14.5 %copy-start.13 = (f32[1,2048]{1,0:T(1,128)}, f32[1,2048]{1,0:T(1,128)S(1)}, u32[]{:S(2)}) copy-start(f32[1,2048]{1,0:T(1,128)S(1)} %get-tuple-element.161) | copy-start | bytes 24580
  (6 other events, 5.1 us)
Sparse Core Ops, SparseCore 0:
  457.0 60.3 reduce-scatter.9
  533.4 53.9 reduce-scatter.5
  628.2 43.5 reduce-scatter.7

commit v5 on v4

--- a/solution.py
+++ b/solution.py
@@ -81,8 +81,8 @@
 
 def gelu_slope(v):
     square = v * v
-    t = jnp.tanh(GELU_A * (v + GELU_B * (v * square)))
-    return 0.5 * (1.0 + t) + 0.5 * v * (1.0 - t * t) * (GELU_A * (1.0 + 3.0 * GELU_B * square))
+    half = 0.5 + 0.5 * jnp.tanh(v * (GELU_A + GELU_A * GELU_B * square))
+    return half + (half - half * half) * (v * (2.0 * GELU_A + 6.0 * GELU_A * GELU_B * square))
 
 
 def norm_kernel(x, gain, shift, out):
@@ -108,55 +108,83 @@
     )(x, gain, shift)
 
 
-def unnorm_kernel(terms, skipped, flag, x, g, gain, *refs):
-    parts, (out, gain_sum, shift_sum) = refs[:terms], refs[terms + skipped :]
+def closing_kernel(terms, flag, x, g, gain, bias, other_bias, second, up, *refs):
+    parts, more, refs = refs[:terms], refs[terms : 2 * terms], refs[2 * terms :]
+    input_grad, output, gain_sum, shift_sum, out_grad, down_grad, up_grad = refs
 
     @pl.when(pl.program_id(0) == 0)
     def _():
         gain_sum[...] = jnp.zeros_like(gain_sum)
         shift_sum[...] = jnp.zeros_like(shift_sum)
-
+        width = out_grad.shape[0]
+        out_grad[...] = second[:width, :].astype(F32)
+        down_grad[...] = second[width:, :].astype(F32)
+
+    def total(many):
+        result = many[0][...].astype(F32)
+        for part in many[1:]:
+            term = part[...].astype(F32)
+            if part is many[-1]:
+                term = jnp.where(flag[0] == 1, term, 0.0)
+            result = result + term
+        return result
+
+    up_grad[...] = up[...].astype(F32)
     values = x[...].astype(F32)
+    output[...] = (
+        values + total(more) + bias[...].astype(F32) + other_bias[...].astype(F32)
+    ).astype(BF16)
     centered = values - jnp.mean(values, axis=1, keepdims=True)
     scale = lax.rsqrt(jnp.mean(centered * centered, axis=1, keepdims=True) + EPS)
     hat = centered * scale
-    back = parts[0][...].astype(F32)
-    for part in parts[1:]:
-        term = part[...].astype(F32)
-        if part is parts[-1]:
-            term = jnp.where(flag[0] == 1, term, 0.0)
-        back = back + term
+    back = total(parts)
     gain_sum[...] += jnp.sum(back * hat, axis=0, keepdims=True)
     shift_sum[...] += jnp.sum(back, axis=0, keepdims=True)
     e = back * gain[...]
     inner = (
         e - jnp.mean(e, axis=1, keepdims=True) - hat * jnp.mean(e * hat, axis=1, keepdims=True)
     )
-    out[...] = (g[...].astype(F32) + inner * scale).astype(BF16)
-
-
-def unnorm(flag, x, g, gain, parts, wait_for=(), tile=128):
+    input_grad[...] = (g[...].astype(F32) + inner * scale).astype(BF16)
+
+
+def closing(flag, x, g, gain, bias, other_bias, second, up, width, parts, more, tile=128):
     rows, depth = x.shape
     row = pl.BlockSpec((tile, depth), lambda i, f: (i, 0))
     one = once((1, depth), lambda i, f: (0, 0))
     total = pl.BlockSpec((1, depth), lambda i, f: (0, 0))
+    still = lambda shape: once(shape, lambda i, f: (0, 0))
+    step = up.shape[0] // (rows // tile)
+    ups = pl.BlockSpec((step, up.shape[1]), lambda i, f: (i, 0))
+    inner, columns = second.shape
     return pl.pallas_call(
-        functools.partial(unnorm_kernel, len(parts), len(wait_for)),
+        functools.partial(closing_kernel, len(parts)),
         grid_spec=pltpu.PrefetchScalarGridSpec(
             num_scalar_prefetch=1,
             grid=(rows // tile,),
-            in_specs=[row, row, one] + [row] * len(parts) + [ANYWHERE] * len(wait_for),
-            out_specs=[row, total, total],
+            in_specs=[row, row, one, one, one, still(second.shape), ups] + [row] * (2 * len(parts)),
+            out_specs=[
+                row,
+                row,
+                total,
+                total,
+                still((width, columns)),
+                still((inner - width, columns)),
+                ups,
+            ],
         ),
         out_shape=[
             jax.ShapeDtypeStruct((rows, depth), BF16),
+            jax.ShapeDtypeStruct((rows, depth), BF16),
             jax.ShapeDtypeStruct((1, depth), F32),
             jax.ShapeDtypeStruct((1, depth), F32),
+            jax.ShapeDtypeStruct((width, columns), F32),
+            jax.ShapeDtypeStruct((inner - width, columns), F32),
+            jax.ShapeDtypeStruct(up.shape, F32),
         ],
         compiler_params=params(("arbitrary",)),
         cost_estimate=cost(30 * rows * depth, 14 * rows * depth),
-        name="unnorm",
-    )(flag, x, g, gain, *parts, *wait_for)
+        name="closing",
+    )(flag, x, g, gain, bias, other_bias, second, up, *parts, *more)
 
 
 MESH = pl.DeviceIdType.MESH
@@ -290,19 +318,20 @@
     return Riding([values] + ([] if into is None else [into]), [like(values)], into is not None, 1, copies)
 
 
-def launch(body, args, ins, outs, shapes, grid, name, estimate, scratch=(), riding=(), ident=None, place=False, wait_for=()):
+def launch(body, args, ins, outs, shapes, grid, name, estimate, scratch=(), riding=(), ident=None, place=False, wait_for=(), lazy=(), seen=(), in_turn=False):
     if ident is None:
         return pl.pallas_call(
-            body,
+            functools.partial(body, lambda *which: None) if in_turn else body,
             grid=(grid,),
-            in_specs=ins,
+            in_specs=ins + [once(a.shape, lambda i, n=len(a.shape): (0,) * n) for a in lazy],
             out_specs=outs,
             out_shape=shapes,
             scratch_shapes=list(scratch),
             compiler_params=params(("arbitrary",)),
             cost_estimate=estimate,
             name=name,
-        )(*args)
+        )(*args, *lazy)
+    args, n_own = list(args) + list(lazy), len(args)
     riding = list(riding) + [Riding([a], [], False, 1, lambda *_: []) for a in wait_for]
     extra_in = [a for r in riding for a in r.ins]
     extra_out = [o for r in riding for o in r.outs]
@@ -318,40 +347,54 @@
         own_ins, ride_ins = some(len(args)), [some(len(r.ins)) for r in riding]
         own_outs, ride_outs = some(len(shapes)), [some(len(r.outs)) for r in riding]
         own_scratch = some(len(scratch))
+        loaded = some(len(lazy))
+        loads = [
+            pltpu.make_async_copy(src, dst, some(1)[0])
+            for src, dst in zip(own_ins[n_own:], loaded)
+        ]
         at = places()
         copies, late = [], []
         for r, i, o in zip(riding, ride_ins, ride_outs):
             found = r.copies(at, i, o, *some(2))
             copies += found[: len(found) - r.late]
             late += found[len(found) - r.late :]
-
-        @pl.when(pl.program_id(0) == 0)
-        def _():
-            greet(at)
-            start_all(at, copies)
-
-        body(*([at] if place else []), *own_ins, *own_outs, *own_scratch)
-
-        @pl.when(pl.program_id(0) == grid - 1)
-        def _():
-            finish_all(at, copies)
-            start_all(at, late)
-            finish_all(at, late)
+        for load in loads:
+            load.start()
+        greet(at)
+        start_all(at, copies)
+
+        def ready(*which):
+            @pl.when(pl.program_id(0) == 0)
+            def _():
+                for n in which:
+                    loads[n].wait()
+
+        def step(*blocks):
+            if not in_turn:
+                ready(*range(len(loads)))
+            n_in = n_own + len(seen)
+            body(*([at] if place else []), *([ready] if in_turn else []), *blocks[:n_in], *loaded, *blocks[n_in:], *own_scratch)
+
+        if shapes:
+            pltpu.emit_pipeline(
+                step, grid=(grid,), in_specs=ins + [spec for _, spec in seen], out_specs=outs
+            )(*own_ins[:n_own], *(ride_outs[r][0] for r, _ in seen), *own_outs)
+        finish_all(at, copies)
+        start_all(at, late)
+        finish_all(at, late)
 
     return pl.pallas_call(
         kernel,
-        grid=(grid,),
-        in_specs=ins + [ANYWHERE] * len(extra_in),
-        out_specs=outs + [ANYWHERE] * len(extra_out),
+        in_specs=[ANYWHERE] * (len(args) + len(extra_in)),
+        out_specs=[ANYWHERE] * (len(shapes) + len(extra_out)),
         out_shape=shapes + extra_out,
         input_output_aliases=aliases,
         scratch_shapes=list(scratch)
+        + [pltpu.VMEM(a.shape, a.dtype) for a in lazy]
+        + [pltpu.SemaphoreType.DMA] * len(lazy)
         + [pltpu.SemaphoreType.DMA((r.count,)) for r in riding for _ in range(2)],
         compiler_params=pltpu.CompilerParams(
-            dimension_semantics=("arbitrary",),
-            vmem_limit_bytes=VMEM_BYTES,
-            collective_id=ident,
-            has_side_effects=True,
+            vmem_limit_bytes=VMEM_BYTES, collective_id=ident, has_side_effects=True
         ),
         cost_estimate=estimate,
         name=name,
@@ -373,6 +416,8 @@
     lows, highs = (0, half), (half, share)
     greet(at, peers)
 
+    across = second_kept.shape[1]
+    mine = pl.ds(pl.multiple_of(dp * across, across), across)
     columns = [(0, width), (width, width), (2 * width, width), (3 * width, units)]
     loads = [
         pltpu.make_async_copy(src, first_kept.at[:, pl.ds(start, size)], local.at[i])
@@ -384,13 +429,15 @@
     ]
     stores = [
         pltpu.make_async_copy(first_kept, first_full.at[dp], local.at[0]),
-        pltpu.make_async_copy(second_kept, second_full.at[dp], local.at[1]),
+        pltpu.make_async_copy(second_kept, second_full.at[:, mine], local.at[1]),
         pltpu.make_async_copy(kept, g_full.at[3, core], local.at[2]),
         pltpu.make_async_copy(own, rows_full.at[3, core], local.at[7]),
     ]
     spread = [
-        [to_device(src, dst.at[dp], w_sent.at[n, i], w_got.at[n, i], peer) for i, peer in enumerate(peers)]
-        for n, (src, dst) in enumerate(((first_kept, first_full), (second_kept, second_full)))
+        [to_device(src, dst, w_sent.at[n, i], w_got.at[n, i], peer) for i, peer in enumerate(peers)]
+        for n, (src, dst) in enumerate(
+            ((first_kept, first_full.at[dp]), (second_kept, second_full.at[:, mine]))
+        )
     ]
     plans = dict(
         n1_low=[(1, *lows)],
@@ -572,7 +619,7 @@
             full,
             full,
             jax.ShapeDtypeStruct((groups, depth // groups, total), BF16),
-            jax.ShapeDtypeStruct((groups, inner, columns), BF16),
+            jax.ShapeDtypeStruct((inner, groups * columns), BF16),
             narrow,
             narrow,
             narrow,
@@ -716,40 +763,50 @@
         copy(i).wait_send()
 
 
-def core_sum(body, ident, count, length, arrays, w, depth, name, pieces=2, riding=()):
+def core_sum_parts(count, pieces, length, depth):
     share = length // 2
     out = pl.BlockSpec((share, depth), lambda i: (0, 0), pipeline_mode=pl.Buffered(1))
-    size = sum(a.shape[1] for a, _ in arrays)
-    return launch(
-        functools.partial(core_sum_body, body, count, pieces, len(arrays)),
-        [a for a, _ in arrays] + [w],
-        [pl.BlockSpec((length, a.shape[1]), lambda i, f=f: (f + i, 0)) for a, f in arrays]
-        + [once(w.shape, lambda i, n=len(w.shape): (0,) * n)],
+    return (
         [out] * count,
         [jax.ShapeDtypeStruct((share, depth), BF16)] * count,
-        count,
-        name,
-        cost(2 * count * length * size * depth, 2 * count * length * (size + depth) + 2 * size * depth),
-        scratch=[
+        [
             pltpu.VMEM((count, share, depth), BF16),
             pltpu.VMEM((count, share, depth), BF16),
             pltpu.VMEM((share // pieces, depth), F32),
             pltpu.SemaphoreType.DMA((count, pieces)),
             pltpu.SemaphoreType.DMA((count, pieces)),
         ],
+    )
+
+
+def core_sum(body, ident, count, length, arrays, w, depth, name, pieces=2, riding=()):
+    outs, shapes, scratch = core_sum_parts(count, pieces, length, depth)
+    size = sum(a.shape[1] for a, _ in arrays)
+    return launch(
+        functools.partial(core_sum_body, body, count, pieces, len(arrays)),
+        [a for a, _ in arrays],
+        [pl.BlockSpec((length, a.shape[1]), lambda i, f=f: (f + i, 0)) for a, f in arrays],
+        outs,
+        shapes,
+        count,
+        name,
+        cost(2 * count * length * size * depth, 2 * count * length * (size + depth) + 2 * size * depth),
+        scratch=scratch,
         riding=riding,
         ident=ident,
         place=True,
+        lazy=[w],
     )
 
 
 def mix_body(attended, active, w, out):
-    parts, inner, columns = w.shape
-    width = attended.shape[1]
-    for d in range(parts):
-        out[:, d * columns : (d + 1) * columns] = (
-            nn(attended[...], w[d, :width, :]) + nn(active[...], w[d, width:, :])
-        ).astype(out.dtype)
+    width, depth = attended.shape[1], w.shape[1]
+    step = min(512, depth)
+    for start in range(0, depth, step):
+        at = slice(start, start + step)
+        out[:, at] = (nn(attended[...], w[:width, at]) + nn(active[...], w[width:, at])).astype(
+            out.dtype
+        )
 
 
 def unproject_body(qkv_grad, hidden_grad, w, out):
@@ -763,8 +820,7 @@
         ).astype(out.dtype)
 
 
-def unmix_tile(g, w, hidden, attended_grad, hidden_grad, sums):
-    parts, inner, columns = w.shape
+def unmix_tile(hidden, g, w, attended_grad, hidden_grad, sums):
     width = attended_grad.shape[1]
     units = hidden.shape[1]
 
@@ -772,17 +828,13 @@
     def _():
         sums[...] = jnp.zeros_like(sums)
 
-    def back(lo, hi):
-        total = nt(g[:, :columns], w[0, lo:hi, :])
-        for d in range(1, parts):
-            total = total + nt(g[:, d * columns : (d + 1) * columns], w[d, lo:hi, :])
-        return total
-
-    attended_grad[...] = back(0, width).astype(BF16)
+    rows = g[...]
+    attended_grad[...] = nt(rows, w[:width, :]).astype(BF16)
     step = min(256, units)
     for start in range(0, units, step):
         at = slice(start, start + step)
-        low = (back(width + start, width + start + step) * gelu_slope(hidden[:, at])).astype(BF16)
+        back = nt(rows, w[width + start : width + start + step, :])
+        low = (back * gelu_slope(hidden[:, at])).astype(BF16)
         hidden_grad[:, at] = low
         sums[:, at] += jnp.sum(low.astype(F32), axis=0, keepdims=True)
 
@@ -790,15 +842,19 @@
 def unmix(g, w, hidden, width, first, count, length, riding=(), ident=None, tile=512):
     rows = count * length
     units = hidden.shape[1]
-    parts, inner, columns = w.shape
-    depth = parts * columns
+    inner, depth = w.shape
     per = length // tile
     row = lambda n: pl.BlockSpec((tile, n), lambda i: (i, 0))
     late = lambda n: pl.BlockSpec((tile, n), lambda i: (first * per + i, 0))
+    seen = []
+    if g is None:
+        seen = [
+            (0, pl.BlockSpec((None, None, tile, depth), lambda i: (first + i // 2, i % 2, 0, 0)))
+        ]
     return launch(
         unmix_tile,
-        [g, w, hidden],
-        [late(depth), once(w.shape, lambda i: (0, 0, 0)), late(units)],
+        [hidden] + ([] if g is None else [g]),
+        [late(units)] + ([] if g is None else [late(depth)]),
         [row(width), row(units), pl.BlockSpec((1, units), lambda i: (0, 0))],
         [
             jax.ShapeDtypeStruct((rows, width), BF16),
@@ -810,135 +866,29 @@
         cost(2 * rows * inner * depth, 2 * depth * (rows + inner) + rows * units * 6),
         riding=riding,
         ident=ident,
-    )
-
-
-def unmix_gather_body(first, tile, moves, last_moves, at, w, hidden, whole_in, attended_grad, hidden_grad, sums, full, g, local, *sems):
-    step, last = pl.program_id(0), pl.num_programs(0) - 1
-    share = full.shape[2]
-    per = share // tile
-    early = Gather(*moves).copies(at, full, *sems[:2])
-    late = Gather(*last_moves).copies(at, full, *sems[2:])
-
-    def load(i):
-        n = first * 2 * per + i
-        rows = pl.ds(pl.multiple_of(lax.rem(n, per) * tile, tile), tile)
-        return pltpu.make_async_copy(
-            full.at[lax.div(n, 2 * per), lax.rem(lax.div(n, per), 2), rows],
-            g.at[lax.rem(i, 2)],
-            local.at[lax.rem(i, 2)],
-        )
-
-    @pl.when(step == 0)
-    def _():
-        start_all(at, early)
-        load(step).start()
-
-    @pl.when(step < last)
-    def _():
-        load(step + 1).start()
-
-    load(step).wait()
-    unmix_tile(g.at[lax.rem(step, 2)], w, hidden, attended_grad, hidden_grad, sums)
-
-    @pl.when(step == last)
-    def _():
-        finish_all(at, early)
-        start_all(at, late)
-        finish_all(at, late)
-
-
-def unmix_gather(full, w, hidden, width, first, count, length, moves, last_moves, ident, riding=(), tile=512):
-    rows = count * length
-    units = hidden.shape[1]
-    parts, inner, columns = w.shape
-    depth = parts * columns
-    per = length // tile
-    row = lambda n: pl.BlockSpec((tile, n), lambda i: (i, 0))
-    counts = [Gather(*moves).count, Gather(*last_moves).count]
-
-    body = functools.partial(unmix_gather_body, first, tile, moves, last_moves)
-    extra = list(riding)
-    args = [w, hidden, full] + [a for r in extra for a in r.ins]
-    shapes = [
-        jax.ShapeDtypeStruct((rows, width), BF16),
-        jax.ShapeDtypeStruct((rows, units), BF16),
-        jax.ShapeDtypeStruct((1, units), F32),
-        like(full),
-    ]
-    aliases, n_in, n_out = {2: 3}, 3, 4
-    for r in extra:
-        if r.aliased:
-            aliases[n_in + len(r.ins) - 1] = n_out
-        n_in, n_out = n_in + len(r.ins), n_out + len(r.outs)
-
-    def kernel(*refs):
-        take = iter(refs)
-        some = lambda n: [next(take) for _ in range(n)]
-        own_ins, ride_ins = some(3), [some(len(r.ins)) for r in extra]
-        own_outs, ride_outs = some(4), [some(len(r.outs)) for r in extra]
-        own_scratch = some(6)
-        at = places()
-        copies = []
-        for r, i, o in zip(extra, ride_ins, ride_outs):
-            copies += r.copies(at, i, o, *some(2))
-
-        @pl.when(pl.program_id(0) == 0)
-        def _():
-            greet(at)
-            start_all(at, copies)
-
-        body(at, *own_ins, *own_outs, *own_scratch)
-
-        @pl.when(pl.program_id(0) == rows // tile - 1)
-        def _():
-            finish_all(at, copies)
-
-    return pl.pallas_call(
-        kernel,
-        grid=(rows // tile,),
-        in_specs=[
-            once(w.shape, lambda i: (0, 0, 0)),
-            pl.BlockSpec((tile, units), lambda i: (first * per + i, 0)),
-        ]
-        + [ANYWHERE] * (len(args) - 2),
-        out_specs=[row(width), row(units), pl.BlockSpec((1, units), lambda i: (0, 0)), ANYWHERE]
-        + [ANYWHERE for r in extra for _ in r.outs],
-        out_shape=shapes + [o for r in extra for o in r.outs],
-        input_output_aliases=aliases,
-        scratch_shapes=[pltpu.VMEM((2, tile, depth), BF16), pltpu.SemaphoreType.DMA((2,))]
-        + [pltpu.SemaphoreType.DMA((max(n, 1),)) for n in counts for _ in range(2)]
-        + [pltpu.SemaphoreType.DMA((r.count,)) for r in extra for _ in range(2)],
-        compiler_params=pltpu.CompilerParams(
-            dimension_semantics=("arbitrary",),
-            vmem_limit_bytes=VMEM_BYTES,
-            collective_id=ident,
-            has_side_effects=True,
-        ),
-        cost_estimate=cost(2 * rows * inner * depth, 2 * depth * (rows + inner) + rows * units * 6),
-        name="unmix",
-    )(*args)
-
-
-def outer_rows_kernel(x, *refs):
+        lazy=[w],
+        seen=seen,
+    )
+
+
+def outer_rows_kernel(ready, x, *refs):
     parts, out = refs[:-1], refs[-1]
     total, start = None, 0
-    for part in parts:
+    for n, part in enumerate(parts):
+        ready(n)
         term = tn(x[start : start + part.shape[0], :], part[...])
         total = term if total is None else total + term
         start += part.shape[0]
     out[...] = total.astype(out.dtype)
 
 
-def outer_rows(x, parts, riding=(), ident=None, tile=512, wait_for=()):
+def outer_rows(x, parts, riding=(), ident=None, tile=256, wait_for=()):
     rows, depth = x.shape
     n = parts[0].shape[1]
-    tile = min(tile, depth)
     return launch(
         outer_rows_kernel,
-        [x, *parts],
-        [pl.BlockSpec((rows, tile), lambda i: (0, i))]
-        + [once(p.shape, lambda i: (0, 0)) for p in parts],
+        [x],
+        [pl.BlockSpec((rows, tile), lambda i: (0, i))],
         [pl.BlockSpec((tile, n), lambda i: (i, 0))],
         [jax.ShapeDtypeStruct((depth, n), BF16)],
         depth // tile,
@@ -947,37 +897,44 @@
         riding=riding,
         ident=ident,
         wait_for=wait_for,
-    )
-
-
-def outer_columns_kernel(parts, b, g, *refs):
-    many, out = refs[:parts], refs[-1]
+        lazy=parts,
+        in_turn=True,
+    )
+
+
+def outer_columns_kernel(ready, g, *refs):
+    many, b, out = refs[:-2], refs[-2], refs[-1]
     width = many[0].shape[1]
     total, start = None, 0
-    for a in many:
+    for n, a in enumerate(many):
+        ready(n)
         term = tn(a[...], g[start : start + a.shape[0], :])
         total = term if total is None else total + term
         start += a.shape[0]
     out[0, :width, :] = total.astype(out.dtype)
+    ready(len(many))
     out[0, width:, :] = tn(b[...], g[...]).astype(out.dtype)
 
 
-def outer_columns(many, b, g, parts, riding=(), ident=None):
+def outer_columns(many, b, g, parts, riding=(), ident=None, tile=512):
     rows, depth = g.shape
     width, units = many[0].shape[1], b.shape[1]
-    tile = depth // parts
+    across = depth // parts
+    tile = min(tile, across)
+    per = across // tile
     return launch(
-        functools.partial(outer_columns_kernel, len(many)),
-        [b, g, *many],
-        [once((rows, units), lambda i: (0, 0)), pl.BlockSpec((rows, tile), lambda i: (0, i))]
-        + [once(a.shape, lambda i: (0, 0)) for a in many],
-        [pl.BlockSpec((1, width + units, tile), lambda i: (i, 0, 0))],
-        [jax.ShapeDtypeStruct((parts, width + units, tile), BF16)],
-        parts,
+        outer_columns_kernel,
+        [g],
+        [pl.BlockSpec((rows, tile), lambda i: (0, i))],
+        [pl.BlockSpec((1, width + units, tile), lambda i: (i // per, 0, i % per))],
+        [jax.ShapeDtypeStruct((parts, width + units, across), BF16)],
+        depth // tile,
         "outer_columns",
         cost(2 * rows * depth * (width + units), 2 * (rows * (depth + width + units) + depth * (width + units))),
         riding=riding,
         ident=ident,
+        lazy=list(many) + [b],
+        in_turn=True,
     )
 
 
@@ -1058,29 +1015,39 @@
 
     key_total[...] = jnp.zeros_like(key_total)
     value_total[...] = jnp.zeros_like(value_total)
-    for begin in range(0, length, tile):
-        end = min(length, begin + tile + SPAN)
-        at = slice(begin, begin + tile)
+
+    def products(begin, head):
+        end, at = min(length, begin + tile + SPAN), slice(begin, begin + tile)
+        mine = head_lanes(width, head)
+        q_rows, g_rows = q[at, :], g[at, :]
+        q_head = jnp.where(mine, q_rows, jnp.zeros_like(q_rows))
+        g_head = jnp.where(mine, g_rows, jnp.zeros_like(g_rows))
+        return q_head, g_head, nt(k[:end, :], q_head), nt(v[:end, :], g_head)
+
+    steps = [(begin, head) for begin in range(0, length, tile) for head in range(heads)]
+    ahead = products(*steps[0])
+    query_total = None
+    for n, (begin, head) in enumerate(steps):
+        q_head, g_head, scores, prob_grad = ahead
+        if n + 1 < len(steps):
+            ahead = products(*steps[n + 1])
+        end, at = min(length, begin + tile + SPAN), slice(begin, begin + tile)
         blocked = column_ids[begin:end, :] > row_ids[:, at]
-        q_rows, g_rows = q[at, :], g[at, :]
-        query_total = jnp.zeros((tile, width), F32)
-        for head in range(heads):
-            mine = head_lanes(width, head)
-            q_head = jnp.where(mine, q_rows, jnp.zeros_like(q_rows))
-            g_head = jnp.where(mine, g_rows, jnp.zeros_like(g_rows))
-            scores = nt(k[:end, :], q_head)
-            tail = jnp.where(blocked, -1e9, scores[begin:, :])
-            scores = jnp.concatenate([scores[:begin, :], tail], axis=0) if begin else tail
-            probs = jnp.exp(scores - log_sums[head : head + 1, at])
-            value_total[:end, :] += nn(probs.astype(BF16), g_head)
-            prob_grad = nt(v[:end, :], g_head)
-            inner = jnp.sum(prob_grad * probs, axis=0, keepdims=True)
-            score_grad = (probs * (prob_grad - inner)).astype(BF16)
-            key_total[:end, :] += nn(score_grad, q_head)
-            query_total = jnp.where(mine, tn(score_grad, k[:end, :]), query_total)
-        turned = rotated(query_total * HEAD_DIM**-0.5, *(t[at, :] for t in tables)).astype(BF16)
-        out[at, :width] = turned
-        sums[:, :width] += jnp.sum(turned.astype(F32), axis=0, keepdims=True)
+        tail = jnp.where(blocked, -1e9, scores[begin:, :])
+        scores = jnp.concatenate([scores[:begin, :], tail], axis=0) if begin else tail
+        probs = jnp.exp(scores - log_sums[head : head + 1, at])
+        value_total[:end, :] += nn(probs.astype(BF16), g_head)
+        inner = jnp.sum(prob_grad * probs, axis=0, keepdims=True)
+        score_grad = (probs * (prob_grad - inner)).astype(BF16)
+        key_total[:end, :] += nn(score_grad, q_head)
+        part = tn(score_grad, k[:end, :])
+        query_total = jnp.where(
+            head_lanes(width, head), part, query_total if head else jnp.zeros_like(part)
+        )
+        if head == heads - 1:
+            turned = rotated(query_total * HEAD_DIM**-0.5, *(t[at, :] for t in tables)).astype(BF16)
+            out[at, :width] = turned
+            sums[:, :width] += jnp.sum(turned.astype(F32), axis=0, keepdims=True)
     turned = rotated(key_total[...], *tables).astype(BF16)
     out[:, width : 2 * width] = turned
     sums[:, width : 2 * width] += jnp.sum(turned.astype(F32), axis=0, keepdims=True)
@@ -1126,6 +1093,106 @@
     )
 
 
+def attend_mix_body(count, pieces, at, q, k, v, column_ids, row_ids, active, w, out, log_sums, *refs):
+    attend_kernel(q, k, v, column_ids, row_ids, out, log_sums)
+    core_sum_body(mix_body, count, pieces, 2, at, out, active, w, *refs)
+
+
+def attend_mix(first, count, q, k, v, column_ids, row_ids, active, w, riding, ident, pieces=2):
+    width, units = q.shape[1], active.shape[1]
+    length = row_ids.shape[2]
+    depth = w.shape[1]
+    rows, heads = count * length, width // HEAD_DIM
+    here = lambda n: pl.BlockSpec((length, n), lambda s: (first + s, 0))
+    outs, shapes, scratch = core_sum_parts(count, pieces, length, depth)
+    return launch(
+        functools.partial(attend_mix_body, count, pieces),
+        [q, k, v, column_ids, row_ids, active],
+        [
+            here(width),
+            here(width),
+            here(width),
+            here(1),
+            pl.BlockSpec((None, 1, length), lambda s: (first + s, 0, 0)),
+            here(units),
+        ],
+        [pl.BlockSpec((length, width), lambda s: (s, 0)), pl.BlockSpec((8, length), lambda s: (0, s))]
+        + outs,
+        [jax.ShapeDtypeStruct((rows, width), BF16), jax.ShapeDtypeStruct((8, rows), F32)] + shapes,
+        count,
+        "attend_mix",
+        cost(8 * rows * heads * length * 256 * 0.8, 8 * rows * width, rows * heads * length),
+        scratch=scratch,
+        riding=riding,
+        ident=ident,
+        place=True,
+        lazy=[w],
+    )
+
+
+def unattend_unproject_body(pieces, at, *refs):
+    operands, hidden_grad, w, (out, sums, part), scratch = (
+        refs[:10],
+        refs[10],
+        refs[11],
+        refs[12:15],
+        refs[15:],
+    )
+    unattend_kernel(*operands, out, sums, *scratch[:2])
+    core_sum_body(unproject_body, 1, pieces, 2, at, out, hidden_grad, w, part, *scratch[2:])
+
+
+def unattend_unproject(
+    at, q, k, v, g, g_at, log_sums, sums_at, column_ids, row_ids, tables, hidden_grad, hidden_at, w, riding, ident, pieces=2
+):
+    width, units = q.shape[1], hidden_grad.shape[1]
+    length = row_ids.shape[2]
+    depth = w.shape[0]
+    heads = width // HEAD_DIM
+    here = lambda n, at: pl.BlockSpec((length, n), lambda s: (at, 0))
+    table = pl.BlockSpec((length, 128), lambda s: (0, 0))
+    outs, shapes, scratch = core_sum_parts(1, pieces, length, depth)
+    return launch(
+        functools.partial(unattend_unproject_body, pieces),
+        [q, k, v, g, log_sums, column_ids, row_ids, *tables, hidden_grad],
+        [
+            here(width, at),
+            here(width, at),
+            here(width, at),
+            here(width, g_at),
+            pl.BlockSpec((8, length), lambda s: (0, sums_at)),
+            here(1, at),
+            pl.BlockSpec((None, 1, length), lambda s: (at, 0, 0)),
+            table,
+            table,
+            table,
+            here(units, hidden_at),
+        ],
+        [
+            pl.BlockSpec((length, 3 * width), lambda s: (0, 0)),
+            pl.BlockSpec((1, 3 * width), lambda s: (0, 0)),
+        ]
+        + outs,
+        [
+            jax.ShapeDtypeStruct((length, 3 * width), BF16),
+            jax.ShapeDtypeStruct((1, 3 * width), F32),
+        ]
+        + shapes,
+        1,
+        "unattend_unproject",
+        cost(20 * heads * length * length * 256 * 0.8, 14 * length * width, heads * length**2),
+        scratch=[pltpu.VMEM((length, width), F32), pltpu.VMEM((length, width), F32)] + scratch,
+        riding=riding,
+        ident=ident,
+        place=True,
+        lazy=[w],
+    )
+
+
+def nothing():
+    pass
+
+
 def add_up(*parts):
     total = parts[0].astype(F32)
     for part in parts[1:]:
@@ -1262,7 +1329,7 @@
     if paired:
         kept = lambda values: jnp.where(inner == 1, values, jnp.zeros_like(values))
         cuts = lambda fraction: int(share * fraction) // 32 * 32
-        g1, g1_more = cuts(0.25), cuts(0.56)
+        g1 = cuts(0.25)
         rows, full, first_full, second_full, q, k, v, active, hidden, *tables = opening(
             next(idents),
             inputs,
@@ -1277,22 +1344,6 @@
         )
         rows = rows.reshape(everything, depth)
         first_full = first_full.reshape(depth, 3 * width + units)
-
-        def heads(at, riding):
-            return attend(at, pair, q, k, v, column_ids, row_ids, riding=riding, ident=next(idents))
-
-        def mixed(values, at, riding):
-            return core_sum(
-                mix_body,
-                next(idents),
-                pair,
-                length,
-                [(values, 0), (active, at)],
-                second_full,
-                depth,
-                "mix",
-                riding=riding,
-            )
 
         def unheads(at, count, g, g_at, sums, sums_at, riding, wait_for=()):
             return unattend(
@@ -1326,37 +1377,34 @@
                 riding=riding,
             )
 
-        far_attended, far_sums, full = heads(0, [gathering(full, (1, g1, g1_more))])
-        *far, full = mixed(far_attended, 0, [gathering(full, (1, g1_more, share))])
-
+        def forward(at, riding):
+            return attend_mix(
+                at, pair, q, k, v, column_ids, row_ids, active, second_full, riding, next(idents)
+            )
+
+        far_attended, far_sums, *far, full = forward(0, [gathering(full, (1, g1, share))])
+
+        near_attended, near_sums, *near, full, end = forward(
+            pair,
+            [gathering(full, (2, 0, share), ("first", 0, share)), sending(far[0], "in", 0, share)],
+        )
+
+        crossing = add_up(far[1], end)
         part = cuts(0.44)
-        near_attended, near_sums, full, end = heads(
-            pair,
-            [
-                gathering(full, (2, 0, part), ("first", 0, share)),
-                sending(far[0], "in", 0, part),
-            ],
-        )
-        *near, full, end = mixed(
-            near_attended,
-            pair,
-            [gathering(full, (2, part, share)), sending(far[0], "in", part, share, end)],
-        )
-
-        crossing = add_up(far[1], end)
-        part = cuts(0.4)
-        near_attended_grad, near_hidden_grad, near_up_sum, full, end, middle = unmix_gather(
-            full,
+        near_attended_grad, near_hidden_grad, near_up_sum, full, end, middle = unmix(
+            None,
             second_full,
             hidden,
             width,
             pair,
             pair,
             length,
-            [(3, 0, part), ("second", 0, share)],
-            [],
-            next(idents),
-            riding=[sending(far[1], "in", 0, part), sending(crossing, "middle", 0, part)],
+            riding=[
+                gathering(full, (3, 0, part), ("second", 0, share)),
+                sending(far[1], "in", 0, part),
+                sending(crossing, "middle", 0, part),
+            ],
+            ident=next(idents),
         )
         near_grad, near_sum, full, end, middle = unheads(
             pair,
@@ -1378,7 +1426,7 @@
         to_side = add_up(near[0], kept(middle))
         to_middle = add_up(far[0], end)
         mine = near[1]
-        part, more = cuts(0.4), cuts(0.75)
+        part = cuts(0.4)
 
         def outward(lo, hi, side=None, middle=None):
             return [sending(to_side, "side", lo, hi, side), sending(to_middle, "middle", lo, hi, middle)]
@@ -1395,36 +1443,40 @@
             ident=next(idents),
         )
         up_sum = near_up_sum + far_up_sum
-        grads_0, sum_0, side, middle = unheads(
-            0, 1, far_attended_grad, 0, far_sums, 0, outward(part, more, side, middle)
-        )
-        far_0, side, middle = unprojected(
-            1, [(grads_0, 0), (far_hidden_grad, 0)], outward(more, share, side, middle)
-        )
-        terms = [mine, side, kept(middle)]
-
-        part, more = cuts(0.5), cuts(0.8)
-        second_part, end = outer_columns(
-            [far_attended, near_attended],
-            active,
-            upstream,
-            groups,
+
+        def backward(at, riding, wait_for=()):
+            return unattend_unproject(
+                at,
+                q,
+                k,
+                v,
+                far_attended_grad,
+                at,
+                far_sums,
+                at,
+                column_ids,
+                row_ids,
+                tables,
+                far_hidden_grad,
+                at,
+                first_full,
+                riding + [Riding([a], [], False, 1, lambda *_: []) for a in wait_for],
+                next(idents),
+            )
+
+        grads_0, sum_0, far_0, side, middle = backward(0, outward(part, share, side, middle))
+        output_terms = [mine, side, middle]
+
+        part = cuts(0.45)
+        up_part, end = outer_rows(
+            rows,
+            [far_hidden_grad, near_hidden_grad],
             riding=[sending(far_0, "in", 0, part)],
             ident=next(idents),
         )
-        second_grad = lax.psum_scatter(second_part, "dp", scatter_dimension=0)
-        grads_1, sum_1, end = unheads(
-            1,
-            1,
-            far_attended_grad,
-            1,
-            far_sums,
-            1,
-            [sending(far_0, "in", part, more, end)],
-            wait_for=[second_part],
-        )
-        far_1, end = unprojected(
-            1, [(grads_1, 0), (far_hidden_grad, 1)], [sending(far_0, "in", more, share, end)]
+        up_grad = lax.psum_scatter(up_part, "dp", scatter_dimension=0, tiled=True)
+        grads_1, sum_1, far_1, end = backward(
+            1, [sending(far_0, "in", part, share, end)], [up_part]
         )
     else:
         tables = rotary_tables(length)
@@ -1432,32 +1484,28 @@
         second = jnp.concatenate([out_weight, down_weight], axis=0)
         bias = jnp.concatenate([query_bias, key_bias, value_bias, up_bias]).astype(F32)[None, :]
         first_full = lax.all_gather(first, "dp", axis=0, tiled=True)
-        second_full = lax.all_gather(second, "dp", axis=0)
+        second_full = lax.all_gather(second, "dp", axis=1, tiled=True)
         rows = lax.all_gather(norm(inputs, gain, shift), "tensor", axis=0, tiled=True)
         upstream = lax.all_gather(grad_out, "tensor", axis=0, tiled=True)
         q, k, v, active, hidden = project(rows, first_full, bias, tables, width, units, length)
         attended, log_sums = attend(0, seqs, q, k, v, column_ids, row_ids)
         whole = each_tile(mix_body, [attended, active], second_full, depth, "mix")
-        terms = [lax.psum_scatter(whole, "tensor", scatter_dimension=0, tiled=True)]
+        output_terms = [lax.psum_scatter(whole, "tensor", scatter_dimension=0, tiled=True)]
         attended_grad, hidden_grad, up_sum = unmix(
             upstream, second_full, hidden, width, 0, seqs, length
         )
-    total = inputs.astype(F32) + out_bias.astype(F32) + down_bias.astype(F32)
-    for values in terms:
-        total = total + values.astype(F32)
-    output = total.astype(BF16)
-
     if paired:
         crossing = add_up(far_1, end)
-        part = cuts(0.5)
-        up_part, end, middle = outer_rows(
-            rows,
-            [far_hidden_grad, near_hidden_grad],
+        part = cuts(0.58)
+        second_part, end, middle = outer_columns(
+            [far_attended, near_attended],
+            active,
+            upstream,
+            groups,
             riding=[sending(far_1, "in", 0, part), sending(crossing, "middle", 0, part)],
             ident=next(idents),
-            wait_for=[output],
-        )
-        up_grad = lax.psum_scatter(up_part, "dp", scatter_dimension=0, tiled=True)
+        )
+        second_grad = lax.psum_scatter(second_part, "dp", scatter_dimension=0)
         *near, end, middle = unprojected(
             pair,
             [(near_grad, 0), (near_hidden_grad, 0)],
@@ -1469,14 +1517,31 @@
         qkv_sum = sum_0 + sum_1 + near_sum
         to_side = add_up(near[0], kept(middle))
         to_middle = add_up(far_0, end)
+        part = cuts(0.44)
         first_part, side, middle = outer_rows(
             rows,
             [grads_0, grads_1, near_grad],
-            riding=[sending(to_side, "side", 0, share), sending(to_middle, "middle", 0, share)],
+            riding=[sending(to_side, "side", 0, part), sending(to_middle, "middle", 0, part)],
             ident=next(idents),
-            wait_for=[second_grad],
+            wait_for=[up_grad],
         )
         first_grad = lax.psum_scatter(first_part, "dp", scatter_dimension=0, tiled=True)
+        side, middle = launch(
+            nothing,
+            [],
+            [],
+            [],
+            [],
+            1,
+            "finish",
+            cost(1e9, 1e6),
+            riding=[
+                sending(to_side, "side", part, share, side),
+                sending(to_middle, "middle", part, share, middle),
+            ],
+            ident=next(idents),
+            wait_for=[first_part],
+        )
         terms = [near[1], side, middle]
     else:
         inner = jnp.ones((), jnp.int32)
@@ -1492,9 +1557,19 @@
         first_grad = lax.psum_scatter(first_part, "dp", scatter_dimension=0, tiled=True)
         up_grad = lax.psum_scatter(up_part, "dp", scatter_dimension=0, tiled=True)
 
-    second_grad, first_grad, up_grad = (t.astype(F32) for t in (second_grad, first_grad, up_grad))
-    input_grad, gain_part, shift_part = unnorm(
-        inner[None], inputs, grad_out, gain, terms, [up_grad] if paired else []
+    first_grad = first_grad.astype(F32)
+    input_grad, output, gain_part, shift_part, out_grad, down_grad, up_grad = closing(
+        inner[None],
+        inputs,
+        grad_out,
+        gain,
+        out_bias[None, :],
+        down_bias[None, :],
+        second_grad,
+        up_grad,
+        width,
+        terms,
+        output_terms,
     )
     bias_part = jnp.sum(grad_out, axis=0, dtype=F32)[None, :]
     if paired and groups == 4:
@@ -1519,11 +1594,11 @@
         qkv_sum[width : 2 * width],
         first_grad[:, 2 * width :],
         qkv_sum[2 * width :],
-        second_grad[:width],
+        out_grad,
         outer_bias_grad,
         up_grad,
         up_sum,
-        second_grad[width:],
+        down_grad,
         outer_bias_grad,
     )
 

time: 688 us -> 614 us (0.89)
  Pallas kernels: 609 us -> 552 us
  waiting for transfers between devices: 9.14 us -> 0.07 us
    pallas_call x16 -> x13, Pallas kernels: 433 us -> 376 us  [the longest x12 362 us: launch(): pl.pallas_call(kernel, in_specs=[ANYWHERE] * (len(args) + len(extra_in)),...]
    reduce_scatter x1, waiting for transfers between devices: 9.09 us -> 0.01 us  [per_device(): lax.psum_scatter(first_part, 'dp', scatter_dimension=0, tiled=True)]
  transfers between devices with their start and end apart: 3 -> 3, of which waited for: 1 -> 0; matrix products, arithmetic and copies ran while one was open for 4% -> 3% of each run, Pallas kernels for 26% -> 28%
where the time goes in v5:
time: 614 us; the launch traced here: 607 us
  Pallas kernels  552 us (90%)
  other arithmetic  23.7 us (4%)
  local copies, waits for them, and re-layouts  16.1 us (3%)
  between operations  14.4 us (2%)
    pallas_call x12, Pallas kernels, launch(): pl.pallas_call(kernel, in_specs=[ANYWHERE] * (len(args) + len(extra_in)),...  362 us
    pallas_call x1, Pallas kernels, opening(): pl.pallas_call(functools.partial(opening_kernel, tile, groups, width, cut...  163 us
    convert_element_type x5, other arithmetic, add_up(): return total.astype(BF16)  20.9 us
    pallas_call x1, Pallas kernels, closing(): pl.pallas_call(functools.partial(closing_kernel, len(parts)), grid_spec=p...  14.5 us
    pallas_call x1, Pallas kernels, sum_everywhere(): pl.pallas_call(functools.partial(sum_everywhere_kernel, groups, members),...  13.1 us
  transfers between devices with their start and end apart: 3, of which 0 were waited for; matrix products, arithmetic and copies ran while one was open for 3% of the time, Pallas kernels for 28%

profile of v5, /device:TPU:0, one launch (start us, length us, event | category | flops | bytes accessed | tf_op | source)
XLA Modules:
  0.0 607.1 jit_solution(12092121685754214015)
XLA Ops:
  9.1 2.0 copy.58
  14.6 163.1 %opening.1 = (bf16[4,2,512,2048]{3,2,1,0:T(8,128)(2,1)}, bf16[4,2,512,2048]{3,2,1,0:T(8,128)(2,1)}, bf16[4,512,1792]{2,1,0:T(8,128)(2,1)}, bf16[1280,2048]{1,0:T...) custom-call(bf16[512,2048]{1,0:T(8,128)(2,1)} %x.1, ...), custom_call_target="tpu_custom_call" | custom-call | flops 3006477056 | bytes 6291456 | tf_op jit(solution)/shard_map/opening/pallas_call | solution.py:614
  177.8 35.5 %attend_mix.2 = (bf16[2048,256]{1,0:T(8,128)(2,1)}, f32[8,2048]{1,0:T(8,128)}, bf16[512,2048]{1,0:T(8,128)(2,1)}, bf16[512,2048]{1,0:T(8,128)(2,1)}, bf16[4,2,512,2048]{3,2,1,0:T(8,128)(2,1)}) custom-call(bf16[4096,256]{1,0:T(8,128)(2,1)} %get-tuple-element.87.refs_0_, bf16[4096,256]{1,0:T(8,128)(2,1)} %get-tuple-element.88.refs_1_, ...), custom_call_target="tpu_custom_call", output_to_operand_aliasing={{4}: (7, {})} | custom-call | flops 1374389504 | bytes 419430 | tf_op jit(solution)/shard_map/attend_mix/pallas_call | solution.py:386
  213.3 49.3 %attend_mix.3 = (bf16[2048,256]{1,0:T(8,128)(2,1)}, f32[8,2048]{1,0:T(8,128)}, bf16[512,2048]{1,0:T(8,128)(2,1)}, bf16[512,2048]{1,0:T(8,128)(2,1)}, bf16[4,2,51...) custom-call(bf16[4096,256]{1,0:T(8,128)(2,1)} %get-tuple-element.87.refs_0_, ...), custom_call_target="tpu_custom_call", output_to_operand_aliasing={{4}: (7, {})} | custom-call | flops 1374389504 | bytes 419430 | tf_op jit(solution)/shard_map/attend_mix/pallas_call | solution.py:386
  262.6 3.8 add_convert_fusion.5.refs_4_.refs_13_
  266.4 22.6 %unmix.2 = (bf16[2048,256]{1,0:T(8,128)(2,1)}, bf16[2048,1024]{1,0:T(8,128)(2,1)}, f32[1,1024]{1,0:T(1,128)}, bf16[4,2,512,2048]{3,2,1,0:T(8,128)(2,1)}, bf16[51...) custom-call(f32[4096,1024]{1,0:T(8,128)} %get-tuple-element.90.refs_0_, ...), custom_call_target="tpu_custom_call", output_to_operand_aliasing={{3}: (2, {})} | custom-call | flops 1073741824 | bytes 2621440 | tf_op jit(solution)/shard_map/unmix/pallas_call | solution.py:386
  289.0 33.5 %unattend.1 = (bf16[2048,768]{1,0:T(8,128)(2,1)}, f32[1,768]{1,0:T(1,128)}, bf16[4,2,512,2048]{3,2,1,0:T(8,128)(2,1)}, bf16[512,2048]{1,0:T(8,128)(2,1)}, bf16[512,2048]{1,0:T(8,128)(2,1)}) custom-call(bf16[4096,256]{1,0:T(8,128)(2,1)} %get-tuple-element.87.refs_0_, ...), custom_call_target="tpu_custom_call", output_to_operand_aliasing={{2}: (10, {}), {3}: (12, {}), {4}: (14, {})} | custom-call | flops 3435973888 | bytes 734003 | tf_op jit(solution)/shard_map/unattend/pallas_call | solution.py:386
  322.6 6.6 %add_convert_fusion.3 = (bf16[512,2048]{1,0:T(8,128)(2,1)}, bf16[512,2048]{1,0:T(8,128)(2,1)}) fusion(bf16[512,2048]{1,0:T(8,128)(2,1)} %get-tuple-element.112, bf16[512,2048]{1,0:T(8,128)(2,1)S(1)} %copy-done.4, bf16[512,2048]{1,0:T(8,128)(2,1)} %get-tuple-element.111, pred[]{:T(512)S(6)} %eq.12, bf16[512,2048]{1,0:T(8,128)(2,1)} %get-tuple-element.110), kind=kLoop, calls=%fused_computation.5 | loop fusion | flops 9437184 | bytes 12582913 | tf_op jit(solution)/shard_map/convert_element_type | solution.py:1200
  329.1 21.1 %unmix.3 = (bf16[2048,256]{1,0:T(8,128)(2,1)}, bf16[2048,1024]{1,0:T(8,128)(2,1)}, f32[1,1024]{1,0:T(1,128)}, bf16[512,2048]{1,0:T(8,128)(2,1)}, bf16[512,2048]{1,0:T(8,128)(2,1)}) custom-call(f32[4096,1024]{1,0:T(8,128)} %get-tuple-element.90.refs_0_, bf16[4096,2048]{1,0:T(8,128)(2,1)} %bitcast.20, ...), custom_call_target="tpu_custom_call" | custom-call | flops 1073741824 | bytes 2621440 | tf_op jit(solution)/shard_map/unmix/pallas_call | solution.py:386
  350.2 31.3 %unattend_unproject.2 = (bf16[1024,768]{1,0:T(8,128)(2,1)}, f32[1,768]{1,0:T(1,128)}, bf16[512,2048]{1,0:T(8,128)(2,1)}, bf16[512,2048]{1,0:T(8,128)(2,1)}, bf16[512,2048]{1,0:T(8,128)(2,1)}) custom-call(bf16[4096,256]{1,0:T(8,128)(2,1)} %get-tuple-element.87.refs_0_, ...), custom_call_target="tpu_custom_call", output_to_operand_aliasing={{3}: (13, {}), {4}: (15, {})} | custom-call | flops 1717986944 | bytes 367001 | tf_op jit(solution)/shard_map/unattend_unproject/pallas_call | solution.py:386
  381.5 26.9 %outer_rows.2 = (bf16[2048,1024]{1,0:T(8,128)(2,1)}, bf16[512,2048]{1,0:T(8,128)(2,1)}) custom-call(bf16[4096,2048]{1,0:T(8,128)(2,1)} %bitcast.27, bf16[2048,1024]{1,0:T(8,128)(2,1)} %get-tuple-element.115.refs_10_.refs_1_, bf16[2048,1024]{1,0:T(8,128)(2,1)} %get-tuple-element.121.refs_2_.refs_1_, bf16[512,2048]{1,0:T(8,128)(2,1)} %get-tuple-element.119.refs_3_.refs_12_), custom_call_target="tpu_custom_call" | custom-call | flops 1717986944 | bytes 2936012 | tf_op jit(solution)/shard_map/outer_rows/pallas_call | solution.py:386
  408.7 31.2 %unattend_unproject.3 = (bf16[1024,768]{1,0:T(8,128)(2,1)}, f32[1,768]{1,0:T(1,128)}, bf16[512,2048]{1,0:T(8,128)(2,1)}, bf16[512,2048]{1,0:T(8,128)(2,1)}) custom-call(bf16[4096,256]{1,0:T(8,128)(2,1)} %get-tuple-element.87.refs_0_, bf16[4096,256]{1,0:T(8,128)(2,1)} %get-tuple-element.88.refs_1_, ...), custom_call_target="tpu_custom_call", output_to_operand_aliasing={{3}: (13, {})} | custom-call | flops 1717986944 | bytes 367001 | tf_op jit(solution)/shard_map/unattend_unproject/pallas_call | solution.py:386
  439.9 4.5 add_convert_fusion.2.refs_5_
  444.4 31.4 %outer_columns.1 = (bf16[4,1280,512]{2,1,0:T(8,128)(2,1)}, bf16[512,2048]{1,0:T(8,128)(2,1)}, bf16[512,2048]{1,0:T(8,128)(2,1)}) custom-call(bf16[4096,2048]{1,0:T(8,128)(2,1)} %bitcast.21, bf16[2048,256]{1,0:T(8,128)(2,1)} %get-tuple-element.108.refs_1_, bf16[2048,256]{1,0:T(8,128)(2,1)} %get-tuple-element.109.refs_2_, ...), custom_call_target="tpu_custom_call" | custom-call | flops 2147483648 | bytes 3250585 | tf_op jit(solution)/shard_map/outer_columns/pallas_call | solution.py:386
  476.0 24.7 %unproject.1 = (bf16[512,2048]{1,0:T(8,128)(2,1)}, bf16[512,2048]{1,0:T(8,128)(2,1)}, bf16[512,2048]{1,0:T(8,128)(2,1)}, bf16[512,2048]{1,0:T(8,128)(2,1)}) custom-call(bf16[2048,768]{1,0:T(8,128)(2,1)} %get-tuple-element.127.refs_0_.refs_3_, bf16[2048,1024]{1,0:T(8,128)(2,1)} %get-tuple-element.121.refs_2_.refs_1_, ...), custom_call_target="tpu_custom_call", output_to_operand_aliasing={{2}: (4, {}), {3}: (6, {})} | custom-call | flops 1503238528 | bytes 2306867 | tf_op jit(solution)/shard_map/unproject/pallas_call | solution.py:386
  500.8 4.0 add_convert_fusion.refs_5_.refs_2_
  504.8 2.1 add_convert_fusion.1.refs_4_.refs_0_
  506.9 25.5 %outer_rows.3 = (bf16[2048,768]{1,0:T(8,128)(2,1)}, bf16[512,2048]{1,0:T(8,128)(2,1)}, bf16[512,2048]{1,0:T(8,128)(2,1)}) custom-call(bf16[4096,2048]{1,0:T(8,128)(2,1)} %bitcast.28, bf16[1024,768]{1,0:T(8,128)(2,1)} %get-tuple-element.133.refs_1_, bf16[1024,768]{1,0:T(8,128)(2,1)} %get-tuple-element.134.refs_2_, ...), custom_call_target="tpu_custom_call" | custom-call | flops 1288490240 | bytes 2621440 | tf_op jit(solution)/shard_map/outer_rows/pallas_call | solution.py:386
  537.1 28.6 %finish.1 = (bf16[512,2048]{1,0:T(8,128)(2,1)}, bf16[512,2048]{1,0:T(8,128)(2,1)}) custom-call(bf16[512,2048]{1,0:T(8,128)(2,1)} %add_convert_fusion.1.refs_4_.refs_0_, bf16[512,2048]{1,0:T(8,128)(2,1)} %get-tuple-element.136.refs_1_, bf16[512,2048]{1,0:T(8,128)(2,1)} %add_convert_fusion.refs_5_.refs_2_, ...), custom_call_target="tpu_custom_call", output_to_operand_aliasing={{0}: (1, {}), {1}: (3, {})} | custom-call | flops 100000000 | bytes 100000 | tf_op jit(solution)/shard_map/finish/pallas_call | solution.py:386
  565.7 14.5 %closing.1 = (bf16[512,2048]{1,0:T(8,128)(2,1)}, bf16[512,2048]{1,0:T(8,128)(2,1)}, f32[1,2048]{1,0:T(1,128)}, f32[1,2048]{1,0:T(1,128)}, f32[256,512]{1,0:T(8,1...) custom-call(s32[1]{0:T(128)} %bitcast.flag, bf16[512,2048]{1,0:T(8,128)(2,1)} %x.1, bf16[512,2048]{1,0:T(8,128)(2,1)} %g.1, ...), custom_call_target="tpu_custom_call" | custom-call | flops 3145728 | bytes 1468006 | tf_op jit(solution)/shard_map/closing/pallas_call | solution.py:159
  580.3 13.1 %sum_everywhere.1 = (f32[8,2048]{1,0:T(8,128)}, f32[1,1792]{1,0:T(1,128)}) custom-call(f32[1,2048]{1,0:T(1,128)} %get-tuple-element.146.gain, f32[1,2048]{1,0:T(1,128)} %get-tuple-element.147.shift, f32[1,2048]{1,0:T(1,128)} %bitcast.35, f32[1,768]{1,0:T(1,128)} %add_add_fusion.qkv, f32[1,1024]{1,0:T(1,128)} %add.64.up), custom_call_target="tpu_custom_call" | custom-call | tf_op jit(solution)/shard_map/sum_everywhere/pallas_call | solution.py:1266
  593.4 1.6 fusion.2
  595.0 1.3 slice.55
  597.5 2.3 fusion.1
  (72 shorter events, 12.3 us)
Async XLA Ops:
  7.2 0.7 copy-start
  7.2 3.9 copy-start.9
  7.2 4.5 copy-start.10
  7.2 5.1 copy-start.18
  7.2 5.7 copy-start.19
  7.2 6.2 %copy-start.20 = (bf16[256]{0:T(256)(128)(2,1)S(1)}, bf16[256]{0:T(256)(128)(2,1)}, u32[]{:S(2)}) copy-start(bf16[256]{0:T(256)(128)(2,1)} %param.25) | copy-start | bytes 1540
  7.2 6.8 %copy-start.21 = (bf16[256]{0:T(256)(128)(2,1)S(1)}, bf16[256]{0:T(256)(128)(2,1)}, u32[]{:S(2)}) copy-start(bf16[256]{0:T(256)(128)(2,1)} %param.27) | copy-start | bytes 1540
  7.3 499.7 %reduce-scatter.6.cloned.1.call-start = ((), (), s32[]{:S(2)}) async-start(), calls=%async_computation.3 | async-start | bytes 5242880 | tf_op jit(solution)/shard_map/reduce_scatter | solution.py:1477
  213.2 49.3 %copy-start.3 = (bf16[512,2048]{1,0:T(8,128)(2,1)S(1)}, bf16[512,2048]{1,0:T(8,128)(2,1)}, u32[]{:S(2)}) copy-start(bf16[512,2048]{1,0:T(8,128)(2,1)} %get-tuple-element.97.refs_3_.refs_11_) | copy-start | bytes 6291460
  289.0 33.6 %copy-start.4 = (bf16[512,2048]{1,0:T(8,128)(2,1)S(1)}, bf16[512,2048]{1,0:T(8,128)(2,1)}, u32[]{:S(2)}) copy-start(bf16[512,2048]{1,0:T(8,128)(2,1)} %get-tuple-element.95.refs_8_) | copy-start | bytes 6291460
  408.4 157.3 %reduce-scatter.10.cloned.1.call-start = ((), (), s32[]{:S(2)}) async-start(), calls=%async_computation.5 | async-start | bytes 6553600
  475.8 121.7 %reduce-scatter.8.cloned.1.call-start = ((), (), s32[]{:S(2)}) async-start(), calls=%async_computation.4 | async-start | bytes 3932160 | tf_op jit(solution)/shard_map/reduce_scatter | solution.py:1528
  476.0 24.8 %copy-start.2 = (bf16[512,2048]{1,0:T(8,128)(2,1)S(1)}, bf16[512,2048]{1,0:T(8,128)(2,1)}, u32[]{:S(2)}) copy-start(bf16[512,2048]{1,0:T(8,128)(2,1)} %get-tuple-element.119.refs_3_.refs_12_) | copy-start | bytes 6291460
  500.8 4.0 copy-start.6
  500.8 4.0 copy-start.7
  532.4 1.3 copy-start.12
  532.5 1.9 copy-start.13
  532.5 1.9 copy-start.14
  532.5 2.5 copy-start.5
  532.5 4.0 copy-start.15
  532.5 4.0 copy-start.16
  532.5 4.0 copy-start.17
  565.7 34.7 %copy-start.1 = (s32[4,1024]{1,0:T(4,128)S(1)}, s32[4,1024]{1,0:T(4,128)}, u32[]{:S(2)}) copy-start(s32[4,1024]{1,0:T(4,128)} %param.19) | copy-start | bytes 49156
  594.9 5.4 copy-start.8
  (1 other events, 0.7 us)
Sparse Core Ops, SparseCore 0:
  408.6 51.8 reduce-scatter.5
  475.9 61.1 reduce-scatter.9
  540.4 43.9 reduce-scatter.7

commit v6 on v5

--- a/solution.py
+++ b/solution.py
@@ -140,7 +140,7 @@
     back = total(parts)
     gain_sum[...] += jnp.sum(back * hat, axis=0, keepdims=True)
     shift_sum[...] += jnp.sum(back, axis=0, keepdims=True)
-    e = back * gain[...]
+    e = back * gain[...].astype(F32)
     inner = (
         e - jnp.mean(e, axis=1, keepdims=True) - hat * jnp.mean(e * hat, axis=1, keepdims=True)
     )
@@ -283,6 +283,7 @@
     def __init__(self, ins, outs, aliased, count, copies, late=0):
         self.ins, self.outs, self.aliased, self.count, self.copies = ins, outs, aliased, count, copies
         self.late = late
+        self.scratch, self.summed = [], None
 
 
 def like(array):
@@ -316,6 +317,44 @@
         return [(sender, receiver, copy)]
 
     return Riding([values] + ([] if into is None else [into]), [like(values)], into is not None, 1, copies)
+
+
+def summing(base, plus, kind, lo, hi, into=None, inner_only=False):
+    sender, receiver, target = SENDS[kind]
+
+    def copies(at, ins, outs, sent, got, total, other, sem):
+        copy = to_device(
+            total, outs[0].at[pl.ds(lo, hi - lo)], sent.at[0], got.at[0], {"tensor": at[target]}
+        )
+        return [(sender, receiver, copy)]
+
+    def summed(at, ins, total, other, sem):
+        rows = pl.ds(lo, hi - lo)
+        loads = [
+            pltpu.make_async_copy(src.at[rows], dst, sem.at[n])
+            for n, (src, dst) in enumerate(zip(ins[:2], (total, other)))
+        ]
+
+        def add():
+            for load in loads:
+                load.wait()
+
+            @pl.loop(0, (hi - lo) // 32)
+            def _(i):
+                here = pl.ds(pl.multiple_of(i * 32, 32), 32)
+                term = other[here, :].astype(F32)
+                if inner_only:
+                    term = jnp.where(at["inner"], term, jnp.zeros_like(term))
+                total[here, :] = (total[here, :].astype(F32) + term).astype(BF16)
+
+        return loads, add
+
+    ride = Riding(
+        [base, plus] + ([] if into is None else [into]), [like(base)], into is not None, 1, copies
+    )
+    part = pltpu.VMEM((hi - lo, base.shape[1]), BF16)
+    ride.scratch, ride.summed = [part, part, pltpu.SemaphoreType.DMA((2,))], summed
+    return ride
 
 
 def launch(body, args, ins, outs, shapes, grid, name, estimate, scratch=(), riding=(), ident=None, place=False, wait_for=(), lazy=(), seen=(), in_turn=False):
@@ -353,15 +392,26 @@
             for src, dst in zip(own_ins[n_own:], loaded)
         ]
         at = places()
-        copies, late = [], []
+        copies, late, sums = [], [], []
         for r, i, o in zip(riding, ride_ins, ride_outs):
-            found = r.copies(at, i, o, *some(2))
-            copies += found[: len(found) - r.late]
-            late += found[len(found) - r.late :]
+            sems, room = some(2), some(len(r.scratch))
+            found = r.copies(at, i, o, *sems, *room)
+            if r.summed is None:
+                copies += found[: len(found) - r.late]
+                late += found[len(found) - r.late :]
+            else:
+                sums.append((*r.summed(at, i, *room), found))
+        for first, _, _ in sums:
+            for load in first:
+                load.start()
         for load in loads:
             load.start()
         greet(at)
         start_all(at, copies)
+        for _, add, found in sums:
+            add()
+            start_all(at, found)
+            copies += found
 
         def ready(*which):
             @pl.when(pl.program_id(0) == 0)
@@ -392,7 +442,11 @@
         scratch_shapes=list(scratch)
         + [pltpu.VMEM(a.shape, a.dtype) for a in lazy]
         + [pltpu.SemaphoreType.DMA] * len(lazy)
-        + [pltpu.SemaphoreType.DMA((r.count,)) for r in riding for _ in range(2)],
+        + [
+            entry
+            for r in riding
+            for entry in [pltpu.SemaphoreType.DMA((r.count,))] * 2 + r.scratch
+        ],
         compiler_params=pltpu.CompilerParams(
             vmem_limit_bytes=VMEM_BYTES, collective_id=ident, has_side_effects=True
         ),
@@ -405,8 +459,9 @@
     x, gain, shift, g, *weights = refs[:10]
     biases, frequency, refs = refs[10:14], refs[14], refs[15:]
     rows_full, g_full, first_full, second_full, q, k, v, active, hidden, cos, low, high = refs[:12]
-    own, kept, first_kept, second_kept, w, bias, x_tile = refs[12:19]
-    staged, (local, x_sem, out_sem, w_sent, w_got), sems = refs[19:24], refs[24:29], refs[29:]
+    g_sum, refs = refs[12], refs[13:]
+    own, kept, first_kept, second_kept, w, bias, x_tile = refs[:7]
+    staged, (local, x_sem, out_sem, w_sent, w_got), sems = refs[7:12], refs[12:17], refs[17:]
     at = places()
     core, dp = at["core"], lax.axis_index("dp")
     peers = [{"dp": jnp.bitwise_xor(dp, step)} for step in range(1, groups)]
@@ -502,6 +557,12 @@
     high[...] = jnp.where(jnp.logical_and(lane >= ROT // 2, lane < ROT), sine, 0.0)
     for ref, (begin, size) in zip(biases, columns):
         bias[:, begin : begin + size] = ref[...].astype(F32)
+    g_sum[...] = jnp.zeros_like(g_sum)
+
+    @pl.loop(0, share // tile)
+    def _(i):
+        rows = pl.ds(pl.multiple_of(i * tile, tile), tile)
+        g_sum[...] += jnp.sum(kept[rows, :].astype(F32), axis=0, keepdims=True)
 
     for copy in stores[:3]:
         copy.wait()
@@ -614,7 +675,7 @@
     return pl.pallas_call(
         functools.partial(opening_kernel, tile, groups, width, cut),
         in_specs=[whole] * 3 + [ANYWHERE] * 7 + [whole] * 5,
-        out_specs=[ANYWHERE] * 9 + [whole] * 3,
+        out_specs=[ANYWHERE] * 9 + [whole] * 4,
         out_shape=[
             full,
             full,
@@ -628,6 +689,7 @@
             table,
             table,
             table,
+            jax.ShapeDtypeStruct((1, depth), F32),
         ],
         scratch_shapes=[
             pltpu.VMEM((rows, depth), BF16),
@@ -1204,7 +1266,13 @@
     return lax.optimization_barrier((values,) + others)[0]
 
 
-def sum_everywhere_kernel(groups, members, gain, shift, bias, qkv, up, wide, narrow, buf, in_dp, in_tensor, send_dp, got_dp, send_tensor, got_tensor):
+def sum_everywhere_kernel(groups, members, counts, *refs):
+    vectors, refs = refs[:3], refs[3:]
+    narrows = []
+    for count in counts:
+        narrows.append(refs[:count])
+        refs = refs[count:]
+    wide, narrow, buf, in_dp, in_tensor, send_dp, got_dp, send_tensor, got_tensor = refs
     dp, tensor = lax.axis_index("dp"), lax.axis_index("tensor")
     mesh = pl.DeviceIdType.MESH
     barrier = pltpu.get_barrier_semaphore()
@@ -1214,14 +1282,17 @@
         pl.semaphore_signal(barrier, inc=1, device_id={"tensor": lax.rem(tensor + step, members)}, device_id_type=mesh)
     pl.semaphore_wait(barrier, groups + members - 2)
     lanes = buf.shape[2] // 4
-    for k, ref in enumerate((gain, shift, bias)):
+    for k, ref in enumerate(vectors):
         for r in range(8):
             buf[0, r : r + 1, k * lanes : (k + 1) * lanes] = ref[:, r * lanes : (r + 1) * lanes]
     row = 0
     buf[0, :, 3 * lanes :] = jnp.zeros((8, lanes), F32)
-    for ref in (qkv, up):
-        for start in range(0, ref.shape[1], lanes):
-            buf[0, row : row + 1, 3 * lanes :] = ref[:, start : start + lanes]
+    for many in narrows:
+        for start in range(0, many[0].shape[1], lanes):
+            term = many[0][:, start : start + lanes]
+            for ref in many[1:]:
+                term = term + ref[:, start : start + lanes]
+            buf[0, row : row + 1, 3 * lanes :] = term
             row += 1
 
     def exchange(axis, me, size, source, into, send, got):
@@ -1260,16 +1331,17 @@
             wide[k : k + 1, r * lanes : (r + 1) * lanes] = total[r : r + 1, k * lanes : (k + 1) * lanes]
 
 
-def sum_everywhere(ident, groups, members, gain, shift, bias, qkv, up):
-    depth = gain.shape[1]
+def sum_everywhere(ident, groups, members, vectors, narrows):
+    depth = vectors[0].shape[1]
+    counts = [len(many) for many in narrows]
     whole = pl.BlockSpec(memory_space=pltpu.VMEM)
     return pl.pallas_call(
-        functools.partial(sum_everywhere_kernel, groups, members),
-        in_specs=[whole] * 5,
+        functools.partial(sum_everywhere_kernel, groups, members, counts),
+        in_specs=[whole] * (3 + sum(counts)),
         out_specs=[whole] * 2,
         out_shape=[
             jax.ShapeDtypeStruct((8, depth), F32),
-            jax.ShapeDtypeStruct((1, qkv.shape[1] + up.shape[1]), F32),
+            jax.ShapeDtypeStruct((1, sum(many[0].shape[1] for many in narrows)), F32),
         ],
         scratch_shapes=[
             pltpu.VMEM((2, 8, depth // 2), F32),
@@ -1282,7 +1354,7 @@
         ],
         compiler_params=pltpu.CompilerParams(collective_id=ident, has_side_effects=True),
         name="sum_everywhere",
-    )(gain, shift, bias, qkv, up)
+    )(*vectors, *(v for many in narrows for v in many))
 
 
 def per_device(
@@ -1327,10 +1399,9 @@
     idents = iter(range(1, 100))
 
     if paired:
-        kept = lambda values: jnp.where(inner == 1, values, jnp.zeros_like(values))
         cuts = lambda fraction: int(share * fraction) // 32 * 32
         g1 = cuts(0.25)
-        rows, full, first_full, second_full, q, k, v, active, hidden, *tables = opening(
+        rows, full, first_full, second_full, q, k, v, active, hidden, *tables, bias_part = opening(
             next(idents),
             inputs,
             norm_gain[None, :],
@@ -1389,8 +1460,7 @@
             [gathering(full, (2, 0, share), ("first", 0, share)), sending(far[0], "in", 0, share)],
         )
 
-        crossing = add_up(far[1], end)
-        part = cuts(0.44)
+        ends, part = end, cuts(0.44)
         near_attended_grad, near_hidden_grad, near_up_sum, full, end, middle = unmix(
             None,
             second_full,
@@ -1402,7 +1472,7 @@
             riding=[
                 gathering(full, (3, 0, part), ("second", 0, share)),
                 sending(far[1], "in", 0, part),
-                sending(crossing, "middle", 0, part),
+                summing(far[1], ends, "middle", 0, part),
             ],
             ident=next(idents),
         )
@@ -1418,18 +1488,23 @@
                     full, (3, part, share), ("third", 0, part), late=[("third", part, share)]
                 ),
                 sending(far[1], "in", part, share, end),
-                sending(crossing, "middle", part, share, middle),
+                summing(far[1], ends, "middle", part, share, middle),
             ],
         )
         upstream = full.reshape(everything, depth)
 
-        to_side = add_up(near[0], kept(middle))
-        to_middle = add_up(far[0], end)
+        def outward(side_terms, middle_terms):
+            def rides(lo, hi, side=None, middle=None):
+                return [
+                    summing(*side_terms, "side", lo, hi, side, inner_only=True),
+                    summing(*middle_terms, "middle", lo, hi, middle),
+                ]
+
+            return rides
+
+        send_out = outward((near[0], middle), (far[0], end))
         mine = near[1]
         part = cuts(0.4)
-
-        def outward(lo, hi, side=None, middle=None):
-            return [sending(to_side, "side", lo, hi, side), sending(to_middle, "middle", lo, hi, middle)]
 
         far_attended_grad, far_hidden_grad, far_up_sum, side, middle = unmix(
             upstream,
@@ -1439,10 +1514,9 @@
             0,
             pair,
             length,
-            riding=outward(0, part),
+            riding=send_out(0, part),
             ident=next(idents),
         )
-        up_sum = near_up_sum + far_up_sum
 
         def backward(at, riding, wait_for=()):
             return unattend_unproject(
@@ -1464,7 +1538,7 @@
                 next(idents),
             )
 
-        grads_0, sum_0, far_0, side, middle = backward(0, outward(part, share, side, middle))
+        grads_0, sum_0, far_0, side, middle = backward(0, send_out(part, share, side, middle))
         output_terms = [mine, side, middle]
 
         part = cuts(0.45)
@@ -1495,14 +1569,13 @@
             upstream, second_full, hidden, width, 0, seqs, length
         )
     if paired:
-        crossing = add_up(far_1, end)
-        part = cuts(0.58)
+        ends, part = end, cuts(0.56)
         second_part, end, middle = outer_columns(
             [far_attended, near_attended],
             active,
             upstream,
             groups,
-            riding=[sending(far_1, "in", 0, part), sending(crossing, "middle", 0, part)],
+            riding=[sending(far_1, "in", 0, part), summing(far_1, ends, "middle", 0, part)],
             ident=next(idents),
         )
         second_grad = lax.psum_scatter(second_part, "dp", scatter_dimension=0)
@@ -1511,17 +1584,15 @@
             [(near_grad, 0), (near_hidden_grad, 0)],
             [
                 sending(far_1, "in", part, share, end),
-                sending(crossing, "middle", part, share, middle),
+                summing(far_1, ends, "middle", part, share, middle),
             ],
         )
-        qkv_sum = sum_0 + sum_1 + near_sum
-        to_side = add_up(near[0], kept(middle))
-        to_middle = add_up(far_0, end)
-        part = cuts(0.44)
+        send_out = outward((near[0], middle), (far_0, end))
+        part = cuts(0.5)
         first_part, side, middle = outer_rows(
             rows,
             [grads_0, grads_1, near_grad],
-            riding=[sending(to_side, "side", 0, part), sending(to_middle, "middle", 0, part)],
+            riding=send_out(0, part),
             ident=next(idents),
             wait_for=[up_grad],
         )
@@ -1535,10 +1606,7 @@
             1,
             "finish",
             cost(1e9, 1e6),
-            riding=[
-                sending(to_side, "side", part, share, side),
-                sending(to_middle, "middle", part, share, middle),
-            ],
+            riding=send_out(part, share, side, middle),
             ident=next(idents),
             wait_for=[first_part],
         )
@@ -1562,7 +1630,7 @@
         inner[None],
         inputs,
         grad_out,
-        gain,
+        norm_gain[None, :],
         out_bias[None, :],
         down_bias[None, :],
         second_grad,
@@ -1571,16 +1639,19 @@
         terms,
         output_terms,
     )
-    bias_part = jnp.sum(grad_out, axis=0, dtype=F32)[None, :]
-    if paired and groups == 4:
+    if paired:
         wide, narrow = sum_everywhere(
-            next(idents), groups, members, gain_part, shift_part, bias_part, qkv_sum, up_sum
+            next(idents),
+            groups,
+            members,
+            [gain_part, shift_part, bias_part],
+            [[sum_0, sum_1, near_sum], [near_up_sum, far_up_sum]],
         )
         gain_grad, shift_grad, outer_bias_grad = wide[0], wide[1], wide[2]
         qkv_sum, up_sum = narrow[0, : 3 * width], narrow[0, 3 * width :]
     else:
         gain_grad, shift_grad, outer_bias_grad = lax.psum(
-            (gain_part[0], shift_part[0], bias_part[0]), ("dp", "tensor")
+            (gain_part[0], shift_part[0], jnp.sum(grad_out, axis=0, dtype=F32)), ("dp", "tensor")
         )
         qkv_sum, up_sum = lax.psum((qkv_sum[0], up_sum[0]), "dp")
     return (

time: 614 us -> 594 us (0.967)
  other arithmetic: 23.7 us -> 0.01 us
    convert_element_type x5 -> x0, other arithmetic: 20.9 us -> none  [add_up(): return total.astype(BF16)]
  transfers between devices with their start and end apart: 3 -> 3, of which waited for: 0 -> 0; matrix products, arithmetic and copies ran while one was open for 3% -> 1% of each run, Pallas kernels for 28% -> 29%
where the time goes in v6:
time: 594 us; the launch traced here: 587 us
  Pallas kernels  556 us (94%)
  local copies, waits for them, and re-layouts  16.1 us (3%)
  between operations  14.5 us (2%)
    pallas_call x12, Pallas kernels, launch(): pl.pallas_call(kernel, in_specs=[ANYWHERE] * (len(args) + len(extra_in)),...  365 us
    pallas_call x1, Pallas kernels, opening(): pl.pallas_call(functools.partial(opening_kernel, tile, groups, width, cut...  163 us
    pallas_call x1, Pallas kernels, closing(): pl.pallas_call(functools.partial(closing_kernel, len(parts)), grid_spec=p...  13.9 us
    pallas_call x1, Pallas kernels, sum_everywhere(): pl.pallas_call(functools.partial(sum_everywhere_kernel, groups, members,...  13.5 us
  transfers between devices with their start and end apart: 3, of which 0 were waited for; matrix products, arithmetic and copies ran while one was open for 1% of the time, Pallas kernels for 29%

profile of v6, /device:TPU:0, one launch (start us, length us, event | category | flops | bytes accessed | tf_op | source)
XLA Modules:
  0.0 587.0 jit_solution(2485290201960480478)
XLA Ops:
  8.5 0.6 reshape.73.refs_4_.refs_6_
  9.1 2.0 copy.58
  11.1 0.6 broadcast_in_dim.33.refs_1_.gain
  11.7 0.6 broadcast_in_dim.36.refs_2_
  14.6 163.1 %opening.1 = (bf16[4,2,512,2048]{3,2,1,0:T(8,128)(2,1)}, bf16[4,2,512,2048]{3,2,1,0:T(8,128)(2,1)}, bf16[4,512,1792]{2,1,0:T(8,128)(2,1)}, bf16[1280,2048]{1,0:T...) custom-call(bf16[512,2048]{1,0:T(8,128)(2,1)} %x.1, ...), custom_call_target="tpu_custom_call" | custom-call | flops 3006477056 | bytes 6291456 | tf_op jit(solution)/shard_map/opening/pallas_call | solution.py:675
  177.8 35.5 %attend_mix.2 = (bf16[2048,256]{1,0:T(8,128)(2,1)}, f32[8,2048]{1,0:T(8,128)}, bf16[512,2048]{1,0:T(8,128)(2,1)}, bf16[512,2048]{1,0:T(8,128)(2,1)}, bf16[4,2,512,2048]{3,2,1,0:T(8,128)(2,1)}) custom-call(bf16[4096,256]{1,0:T(8,128)(2,1)} %get-tuple-element.88.refs_0_, bf16[4096,256]{1,0:T(8,128)(2,1)} %get-tuple-element.89.refs_1_, ...), custom_call_target="tpu_custom_call", output_to_operand_aliasing={{4}: (7, {})} | custom-call | flops 1374389504 | bytes 419430 | tf_op jit(solution)/shard_map/attend_mix/pallas_call | solution.py:436
  213.3 49.3 %attend_mix.3 = (bf16[2048,256]{1,0:T(8,128)(2,1)}, f32[8,2048]{1,0:T(8,128)}, bf16[512,2048]{1,0:T(8,128)(2,1)}, bf16[512,2048]{1,0:T(8,128)(2,1)}, bf16[4,2,51...) custom-call(bf16[4096,256]{1,0:T(8,128)(2,1)} %get-tuple-element.88.refs_0_, ...), custom_call_target="tpu_custom_call", output_to_operand_aliasing={{4}: (7, {})} | custom-call | flops 1374389504 | bytes 419430 | tf_op jit(solution)/shard_map/attend_mix/pallas_call | solution.py:436
  262.6 22.6 %unmix.2 = (bf16[2048,256]{1,0:T(8,128)(2,1)}, bf16[2048,1024]{1,0:T(8,128)(2,1)}, f32[1,1024]{1,0:T(1,128)}, bf16[4,2,512,2048]{3,2,1,0:T(8,128)(2,1)}, bf16[51...) custom-call(f32[4096,1024]{1,0:T(8,128)} %get-tuple-element.91.refs_0_, ...), custom_call_target="tpu_custom_call", output_to_operand_aliasing={{3}: (2, {})} | custom-call | flops 1073741824 | bytes 2621440 | tf_op jit(solution)/shard_map/unmix/pallas_call | solution.py:436
  285.2 34.0 %unattend.1 = (bf16[2048,768]{1,0:T(8,128)(2,1)}, f32[1,768]{1,0:T(1,128)}, bf16[4,2,512,2048]{3,2,1,0:T(8,128)(2,1)}, bf16[512,2048]{1,0:T(8,128)(2,1)}, bf16[512,2048]{1,0:T(8,128)(2,1)}) custom-call(bf16[4096,256]{1,0:T(8,128)(2,1)} %get-tuple-element.88.refs_0_, ...), custom_call_target="tpu_custom_call", output_to_operand_aliasing={{2}: (10, {}), {3}: (12, {}), {4}: (15, {})} | custom-call | flops 3435973888 | bytes 734003 | tf_op jit(solution)/shard_map/unattend/pallas_call | solution.py:436
  319.2 21.7 %unmix.3 = (bf16[2048,256]{1,0:T(8,128)(2,1)}, bf16[2048,1024]{1,0:T(8,128)(2,1)}, f32[1,1024]{1,0:T(1,128)}, bf16[512,2048]{1,0:T(8,128)(2,1)}, bf16[512,2048]{1,0:T(8,128)(2,1)}) custom-call(f32[4096,1024]{1,0:T(8,128)} %get-tuple-element.91.refs_0_, bf16[4096,2048]{1,0:T(8,128)(2,1)} %bitcast.19, ...), custom_call_target="tpu_custom_call" | custom-call | flops 1073741824 | bytes 2621440 | tf_op jit(solution)/shard_map/unmix/pallas_call | solution.py:436
  340.9 32.6 %unattend_unproject.2 = (bf16[1024,768]{1,0:T(8,128)(2,1)}, f32[1,768]{1,0:T(1,128)}, bf16[512,2048]{1,0:T(8,128)(2,1)}, bf16[512,2048]{1,0:T(8,128)(2,1)}, bf16[512,2048]{1,0:T(8,128)(2,1)}) custom-call(bf16[4096,256]{1,0:T(8,128)(2,1)} %get-tuple-element.88.refs_0_, ...), custom_call_target="tpu_custom_call", output_to_operand_aliasing={{3}: (14, {}), {4}: (17, {})} | custom-call | flops 1717986944 | bytes 367001 | tf_op jit(solution)/shard_map/unattend_unproject/pallas_call | solution.py:436
  373.5 26.9 %outer_rows.2 = (bf16[2048,1024]{1,0:T(8,128)(2,1)}, bf16[512,2048]{1,0:T(8,128)(2,1)}) custom-call(bf16[4096,2048]{1,0:T(8,128)(2,1)} %bitcast.26, bf16[2048,1024]{1,0:T(8,128)(2,1)} %get-tuple-element.116.refs_10_.refs_1_, bf16[2048,1024]{1,0:T(8,128)(2,1)} %get-tuple-element.122.refs_2_.refs_1_, bf16[512,2048]{1,0:T(8,128)(2,1)} %get-tuple-element.120.refs_3_.refs_12_.refs_6_), custom_call_target="tpu_custom_call" | custom-call | flops 1717986944 | bytes 2936012 | tf_op jit(solution)/shard_map/outer_rows/pallas_call | solution.py:436
  400.7 31.0 %unattend_unproject.3 = (bf16[1024,768]{1,0:T(8,128)(2,1)}, f32[1,768]{1,0:T(1,128)}, bf16[512,2048]{1,0:T(8,128)(2,1)}, bf16[512,2048]{1,0:T(8,128)(2,1)}) custom-call(bf16[4096,256]{1,0:T(8,128)(2,1)} %get-tuple-element.88.refs_0_, bf16[4096,256]{1,0:T(8,128)(2,1)} %get-tuple-element.89.refs_1_, ...), custom_call_target="tpu_custom_call", output_to_operand_aliasing={{3}: (13, {})} | custom-call | flops 1717986944 | bytes 367001 | tf_op jit(solution)/shard_map/unattend_unproject/pallas_call | solution.py:436
  431.7 31.7 %outer_columns.1 = (bf16[4,1280,512]{2,1,0:T(8,128)(2,1)}, bf16[512,2048]{1,0:T(8,128)(2,1)}, bf16[512,2048]{1,0:T(8,128)(2,1)}) custom-call(bf16[4096,2048]{1,0:T(8,128)(2,1)} %bitcast.20, bf16[2048,256]{1,0:T(8,128)(2,1)} %get-tuple-element.109.refs_1_, bf16[2048,256]{1,0:T(8,128)(2,1)} %get-tuple-element.110.refs_2_, ...), custom_call_target="tpu_custom_call" | custom-call | flops 2147483648 | bytes 3250585 | tf_op jit(solution)/shard_map/outer_columns/pallas_call | solution.py:436
  463.7 25.6 %unproject.1 = (bf16[512,2048]{1,0:T(8,128)(2,1)}, bf16[512,2048]{1,0:T(8,128)(2,1)}, bf16[512,2048]{1,0:T(8,128)(2,1)}, bf16[512,2048]{1,0:T(8,128)(2,1)}) custom-call(bf16[2048,768]{1,0:T(8,128)(2,1)} %get-tuple-element.128.refs_0_.refs_3_, bf16[2048,1024]{1,0:T(8,128)(2,1)} %get-tuple-element.122.refs_2_.refs_1_, ...), custom_call_target="tpu_custom_call", output_to_operand_aliasing={{2}: (4, {}), {3}: (7, {})} | custom-call | flops 1503238528 | bytes 2306867 | tf_op jit(solution)/shard_map/unproject/pallas_call | solution.py:436
  489.3 27.8 %outer_rows.3 = (bf16[2048,768]{1,0:T(8,128)(2,1)}, bf16[512,2048]{1,0:T(8,128)(2,1)}, bf16[512,2048]{1,0:T(8,128)(2,1)}) custom-call(bf16[4096,2048]{1,0:T(8,128)(2,1)} %bitcast.27, bf16[1024,768]{1,0:T(8,128)(2,1)} %get-tuple-element.134.refs_1_, bf16[1024,768]{1,0:T(8,128)(2,1)} %get-tuple-element.135.refs_2_, ...), custom_call_target="tpu_custom_call" | custom-call | flops 1288490240 | bytes 2621440 | tf_op jit(solution)/shard_map/outer_rows/pallas_call | solution.py:436
  517.2 0.6 copy-done.5
  519.0 26.5 %finish.1 = (bf16[512,2048]{1,0:T(8,128)(2,1)}, bf16[512,2048]{1,0:T(8,128)(2,1)}) custom-call(bf16[512,2048]{1,0:T(8,128)(2,1)} %get-tuple-element.132.refs_4_.refs_0_, bf16[512,2048]{1,0:T(8,128)(2,1)} %get-tuple-element.133.refs_5_.refs_1_, bf16[512,2048]{1,0:T(8,128)(2,1)} %get-tuple-element.137.refs_2_, ...), custom_call_target="tpu_custom_call", output_to_operand_aliasing={{0}: (2, {}), {1}: (5, {})} | custom-call | flops 100000000 | bytes 100000 | tf_op jit(solution)/shard_map/finish/pallas_call | solution.py:436
  545.6 13.9 %closing.1 = (bf16[512,2048]{1,0:T(8,128)(2,1)}, bf16[512,2048]{1,0:T(8,128)(2,1)}, f32[1,2048]{1,0:T(1,128)}, f32[1,2048]{1,0:T(1,128)}, f32[256,512]{1,0:T(8,1...) custom-call(s32[1]{0:T(128)} %bitcast.flag, bf16[512,2048]{1,0:T(8,128)(2,1)} %x.1, bf16[512,2048]{1,0:T(8,128)(2,1)} %g.1, ...), custom_call_target="tpu_custom_call" | custom-call | flops 3145728 | bytes 1468006 | tf_op jit(solution)/shard_map/closing/pallas_call | solution.py:159
  559.5 13.5 %sum_everywhere.1 = (f32[8,2048]{1,0:T(8,128)}, f32[1,1792]{1,0:T(1,128)}) custom-call(f32[1,2048]{1,0:T(1,128)} %get-tuple-element.147.refs_0_, f32[1,2048]{1,0:T(1,128)} %get-tuple-element.148.refs_1_, f32[1,2048]{1,0:T(1,128)} %get-tuple-element.149.refs_2_, f32[1,768]{1,0:T(1,128)} %get-tuple-element.150.refs_3_, f32[1,768]{1,0:T(1,128)} %get-tuple-element.151.refs_4_, ...), custom_call_target="tpu_custom_call" | custom-call | tf_op jit(solution)/shard_map/sum_everywhere/pallas_call | solution.py:1338
  572.9 1.6 fusion.2
  574.5 1.3 slice.55
  575.8 1.3 fusion.3
  577.0 2.3 fusion.1
  (41 shorter events, 6.0 us)
Async XLA Ops:
  7.2 0.7 copy-start
  7.2 3.9 copy-start.3
  7.2 4.5 copy-start.4
  7.2 5.1 copy-start.7
  7.2 5.7 copy-start.8
  7.2 6.2 %copy-start.9 = (bf16[256]{0:T(256)(128)(2,1)S(1)}, bf16[256]{0:T(256)(128)(2,1)}, u32[]{:S(2)}) copy-start(bf16[256]{0:T(256)(128)(2,1)} %param.25) | copy-start | bytes 1540
  7.2 6.8 %copy-start.10 = (bf16[256]{0:T(256)(128)(2,1)S(1)}, bf16[256]{0:T(256)(128)(2,1)}, u32[]{:S(2)}) copy-start(bf16[256]{0:T(256)(128)(2,1)} %param.27) | copy-start | bytes 1540
  7.3 482.1 %reduce-scatter.6.cloned.1.call-start = ((), (), s32[]{:S(2)}) async-start(), calls=%async_computation.3 | async-start | bytes 5242880 | tf_op jit(solution)/shard_map/reduce_scatter | solution.py:1551
  400.5 145.1 %reduce-scatter.10.cloned.1.call-start = ((), (), s32[]{:S(2)}) async-start(), calls=%async_computation.5 | async-start | bytes 6553600
  463.4 113.7 %reduce-scatter.8.cloned.1.call-start = ((), (), s32[]{:S(2)}) async-start(), calls=%async_computation.4 | async-start | bytes 3932160 | tf_op jit(solution)/shard_map/reduce_scatter | solution.py:1599
  517.1 0.7 copy-start.5
  517.1 1.3 copy-start.6
  545.6 34.4 %copy-start.1 = (s32[4,1024]{1,0:T(4,128)S(1)}, s32[4,1024]{1,0:T(4,128)}, u32[]{:S(2)}) copy-start(s32[4,1024]{1,0:T(4,128)} %param.19) | copy-start | bytes 49156
  574.5 5.4 copy-start.2
Sparse Core Ops, SparseCore 0:
  400.6 51.4 reduce-scatter.5
  463.5 60.4 reduce-scatter.9
  527.2 45.3 reduce-scatter.7

commit v7 on v6

--- a/solution.py
+++ b/solution.py
@@ -1,4 +1,5 @@
 import functools
+import types
 
 import jax
 import jax.numpy as jnp
@@ -13,6 +14,7 @@
 SPAN = 256
 EPS = 1e-05
 F32 = jnp.float32
+DP, TENSOR = "dp", "tensor"
 BF16 = jnp.bfloat16
 VMEM_BYTES = 60 * 2**20
 
@@ -192,11 +194,11 @@
 
 
 def places():
-    me = lax.axis_index("tensor")
+    me = lax.axis_index(TENSOR)
     core, chip = lax.rem(me, 2), lax.div(me, 2)
     beside = chip + 1 - 2 * lax.rem(chip, 2)
     inner = jnp.logical_or(chip == 1, chip == 2)
-    return dict(
+    return types.SimpleNamespace(
         core=core,
         partner=me + 1 - 2 * core,
         beside=2 * beside + core,
@@ -209,7 +211,7 @@
 
 def greet(at, others=()):
     barrier = pltpu.get_barrier_semaphore()
-    ids = [{"tensor": at[name]} for name in ("partner", "beside", "opposite")] + list(others)
+    ids = [{TENSOR: getattr(at, name)} for name in ("partner", "beside", "opposite")] + list(others)
     for device in ids:
         pl.semaphore_signal(barrier, inc=1, device_id=device, device_id_type=MESH)
     pl.semaphore_wait(barrier, len(ids))
@@ -235,13 +237,13 @@
 
 def start_all(at, copies):
     for sender, _, copy in copies:
-        under(at[sender], copy.start)
+        under(getattr(at, sender), copy.start)
 
 
 def finish_all(at, copies):
     for sender, receiver, copy in copies:
-        under(at[receiver], copy.wait_recv)
-        under(at[sender], copy.wait_send)
+        under(getattr(at, receiver), copy.wait_recv)
+        under(getattr(at, sender), copy.wait_send)
 
 
 class Gather:
@@ -268,11 +270,11 @@
                     sender,
                     receiver,
                     to_device(
-                        full.at[src, at["core"], rows],
-                        full.at[dst, at["core"], rows],
+                        full.at[src, at.core, rows],
+                        full.at[dst, at.core, rows],
                         sent.at[i],
                         got.at[i],
-                        {"tensor": at[target]},
+                        {TENSOR: getattr(at, target)},
                     ),
                 )
             )
@@ -284,19 +286,22 @@
         self.ins, self.outs, self.aliased, self.count, self.copies = ins, outs, aliased, count, copies
         self.late = late
         self.scratch, self.summed = [], None
+        self.early, self.middle = 0, 0
 
 
 def like(array):
     return jax.ShapeDtypeStruct(array.shape, array.dtype)
 
 
-def gathering(full, *moves, late=()):
-    plan = Gather(*moves, *late)
+def gathering(full, *moves, late=(), early=(), middle=()):
+    plan = Gather(*early, *moves, *middle, *late)
 
     def copies(at, ins, outs, sent, got):
         return plan.copies(at, outs[0], sent, got)
 
-    return Riding([full], [like(full)], True, plan.count, copies, Gather(*late).count)
+    ride = Riding([full], [like(full)], True, plan.count, copies, Gather(*late).count)
+    ride.early, ride.middle = Gather(*early).count, Gather(*middle).count
+    return ride
 
 
 SENDS = {
@@ -312,7 +317,7 @@
     def copies(at, ins, outs, sent, got):
         rows = pl.ds(lo, hi - lo)
         copy = to_device(
-            ins[0].at[rows], outs[0].at[rows], sent.at[0], got.at[0], {"tensor": at[target]}
+            ins[0].at[rows], outs[0].at[rows], sent.at[0], got.at[0], {TENSOR: getattr(at, target)}
         )
         return [(sender, receiver, copy)]
 
@@ -324,7 +329,7 @@
 
     def copies(at, ins, outs, sent, got, total, other, sem):
         copy = to_device(
-            total, outs[0].at[pl.ds(lo, hi - lo)], sent.at[0], got.at[0], {"tensor": at[target]}
+            total, outs[0].at[pl.ds(lo, hi - lo)], sent.at[0], got.at[0], {TENSOR: getattr(at, target)}
         )
         return [(sender, receiver, copy)]
 
@@ -344,7 +349,7 @@
                 here = pl.ds(pl.multiple_of(i * 32, 32), 32)
                 term = other[here, :].astype(F32)
                 if inner_only:
-                    term = jnp.where(at["inner"], term, jnp.zeros_like(term))
+                    term = jnp.where(at.inner, term, jnp.zeros_like(term))
                 total[here, :] = (total[here, :].astype(F32) + term).astype(BF16)
 
         return loads, add
@@ -370,11 +375,40 @@
             cost_estimate=estimate,
             name=name,
         )(*args, *lazy)
-    args, n_own = list(args) + list(lazy), len(args)
+    stage = types.SimpleNamespace(
+        body=body,
+        args=args,
+        ins=ins,
+        outs=outs,
+        shapes=shapes,
+        grid=grid,
+        estimate=estimate,
+        scratch=scratch,
+        place=place,
+        lazy=lazy,
+        seen=seen,
+        in_turn=in_turn,
+    )
+    if ident == "defer":
+        return stage
+    return chain([stage], name, riding, ident, wait_for)
+
+
+class Made:
+    def __init__(self, stage, output):
+        self.at = stage, output
+
+
+def chain(stages, name, riding, ident, wait_for=()):
     riding = list(riding) + [Riding([a], [], False, 1, lambda *_: []) for a in wait_for]
+    plain = [[a for a in st.args if not isinstance(a, Made)] for st in stages]
+    operands = [a for st, own in zip(stages, plain) for a in own + list(st.lazy)]
+    shapes = [o for st in stages for o in st.shapes]
+    scratch = [x for st in stages for x in st.scratch]
+    lazies = [a for st in stages for a in st.lazy]
     extra_in = [a for r in riding for a in r.ins]
     extra_out = [o for r in riding for o in r.outs]
-    aliases, n_in, n_out = {}, len(args), len(shapes)
+    aliases, n_in, n_out = {}, len(operands), len(shapes)
     for r in riding:
         if r.aliased:
             aliases[n_in + len(r.ins) - 1] = n_out
@@ -383,65 +417,96 @@
     def kernel(*refs):
         take = iter(refs)
         some = lambda n: [next(take) for _ in range(n)]
-        own_ins, ride_ins = some(len(args)), [some(len(r.ins)) for r in riding]
-        own_outs, ride_outs = some(len(shapes)), [some(len(r.outs)) for r in riding]
-        own_scratch = some(len(scratch))
-        loaded = some(len(lazy))
+        own_ins, lazy_ins = [], []
+        for st, own in zip(stages, plain):
+            own_ins.append(some(len(own)))
+            lazy_ins.append(some(len(st.lazy)))
+        ride_ins = [some(len(r.ins)) for r in riding]
+        own_outs = [some(len(st.shapes)) for st in stages]
+        ride_outs = [some(len(r.outs)) for r in riding]
+        own_scratch = [some(len(st.scratch)) for st in stages]
+        loaded = [some(len(st.lazy)) for st in stages]
         loads = [
-            pltpu.make_async_copy(src, dst, some(1)[0])
-            for src, dst in zip(own_ins[n_own:], loaded)
+            [pltpu.make_async_copy(src, dst, some(1)[0]) for src, dst in zip(srcs, dsts)]
+            for srcs, dsts in zip(lazy_ins, loaded)
         ]
         at = places()
-        copies, late, sums = [], [], []
+        copies, middle, late, sums, early = [], [], [], [], []
         for r, i, o in zip(riding, ride_ins, ride_outs):
             sems, room = some(2), some(len(r.scratch))
             found = r.copies(at, i, o, *sems, *room)
             if r.summed is None:
-                copies += found[: len(found) - r.late]
-                late += found[len(found) - r.late :]
+                stop = len(found) - r.late
+                early += found[: r.early]
+                copies += found[r.early : stop - r.middle]
+                middle += found[stop - r.middle : stop]
+                late += found[stop:]
             else:
                 sums.append((*r.summed(at, i, *room), found))
         for first, _, _ in sums:
             for load in first:
                 load.start()
-        for load in loads:
-            load.start()
+        for many in loads:
+            for load in many:
+                load.start()
         greet(at)
+        start_all(at, early)
         start_all(at, copies)
         for _, add, found in sums:
             add()
             start_all(at, found)
             copies += found
 
-        def ready(*which):
-            @pl.when(pl.program_id(0) == 0)
-            def _():
-                for n in which:
-                    loads[n].wait()
-
-        def step(*blocks):
-            if not in_turn:
-                ready(*range(len(loads)))
-            n_in = n_own + len(seen)
-            body(*([at] if place else []), *([ready] if in_turn else []), *blocks[:n_in], *loaded, *blocks[n_in:], *own_scratch)
-
-        if shapes:
-            pltpu.emit_pipeline(
-                step, grid=(grid,), in_specs=ins + [spec for _, spec in seen], out_specs=outs
-            )(*own_ins[:n_own], *(ride_outs[r][0] for r, _ in seen), *own_outs)
+        for k, st in enumerate(stages):
+            if k == 1 and middle:
+                finish_all(at, early)
+                start_all(at, middle)
+                early, copies = [], copies + middle
+            own = iter(own_ins[k])
+            sources = [
+                own_outs[a.at[0]][a.at[1]] if isinstance(a, Made) else next(own) for a in st.args
+            ]
+
+            def ready(*which, k=k):
+                @pl.when(pl.program_id(0) == 0)
+                def _():
+                    for n in which:
+                        loads[k][n].wait()
+
+            def step(*blocks, k=k, st=st, ready=ready):
+                if not st.in_turn:
+                    ready(*range(len(loads[k])))
+                n_blocks = len(st.args) + len(st.seen)
+                st.body(
+                    *([at] if st.place else []),
+                    *([ready] if st.in_turn else []),
+                    *blocks[:n_blocks],
+                    *loaded[k],
+                    *blocks[n_blocks:],
+                    *own_scratch[k],
+                )
+
+            if st.shapes:
+                pltpu.emit_pipeline(
+                    step,
+                    grid=(st.grid,),
+                    in_specs=st.ins + [spec for _, spec in st.seen],
+                    out_specs=st.outs,
+                )(*sources, *(ride_outs[r][0] for r, _ in st.seen), *own_outs[k])
+        finish_all(at, early)
         finish_all(at, copies)
         start_all(at, late)
         finish_all(at, late)
 
     return pl.pallas_call(
         kernel,
-        in_specs=[ANYWHERE] * (len(args) + len(extra_in)),
+        in_specs=[ANYWHERE] * (len(operands) + len(extra_in)),
         out_specs=[ANYWHERE] * (len(shapes) + len(extra_out)),
         out_shape=shapes + extra_out,
         input_output_aliases=aliases,
-        scratch_shapes=list(scratch)
-        + [pltpu.VMEM(a.shape, a.dtype) for a in lazy]
-        + [pltpu.SemaphoreType.DMA] * len(lazy)
+        scratch_shapes=scratch
+        + [pltpu.VMEM(a.shape, a.dtype) for a in lazies]
+        + [pltpu.SemaphoreType.DMA] * len(lazies)
         + [
             entry
             for r in riding
@@ -450,9 +515,9 @@
         compiler_params=pltpu.CompilerParams(
             vmem_limit_bytes=VMEM_BYTES, collective_id=ident, has_side_effects=True
         ),
-        cost_estimate=estimate,
+        cost_estimate=stages[0].estimate,
         name=name,
-    )(*args, *extra_in)
+    )(*operands, *extra_in)
 
 
 def opening_kernel(tile, groups, width, cut, *refs):
@@ -463,8 +528,8 @@
     own, kept, first_kept, second_kept, w, bias, x_tile = refs[:7]
     staged, (local, x_sem, out_sem, w_sent, w_got), sems = refs[7:12], refs[12:17], refs[17:]
     at = places()
-    core, dp = at["core"], lax.axis_index("dp")
-    peers = [{"dp": jnp.bitwise_xor(dp, step)} for step in range(1, groups)]
+    core, dp = at.core, lax.axis_index(DP)
+    peers = [{DP: jnp.bitwise_xor(dp, step)} for step in range(1, groups)]
     share, depth = own.shape
     half = share // 2
     units = hidden.shape[1]
@@ -790,7 +855,7 @@
     ins, w, outs = refs[:n_in], refs[n_in], refs[n_in + 1 : n_in + 1 + count]
     sent, got, value, send_sem, got_sem = refs[n_in + 1 + count :]
     slot = pl.program_id(0)
-    core = at["core"]
+    core = at.core
     share = sent.shape[1]
     piece = share // pieces
 
@@ -805,7 +870,7 @@
             got.at[slot, rows],
             send_sem.at[slot, i],
             got_sem.at[slot, i],
-            {"tensor": at["partner"]},
+            {TENSOR: at.partner},
         )
 
     for i in range(pieces):
@@ -1207,7 +1272,8 @@
 def unattend_unproject(
     at, q, k, v, g, g_at, log_sums, sums_at, column_ids, row_ids, tables, hidden_grad, hidden_at, w, riding, ident, pieces=2
 ):
-    width, units = q.shape[1], hidden_grad.shape[1]
+    width = q.shape[1]
+    units = w.shape[1] - 3 * width
     length = row_ids.shape[2]
     depth = w.shape[0]
     heads = width // HEAD_DIM
@@ -1273,13 +1339,13 @@
         narrows.append(refs[:count])
         refs = refs[count:]
     wide, narrow, buf, in_dp, in_tensor, send_dp, got_dp, send_tensor, got_tensor = refs
-    dp, tensor = lax.axis_index("dp"), lax.axis_index("tensor")
+    dp, tensor = lax.axis_index(DP), lax.axis_index(TENSOR)
     mesh = pl.DeviceIdType.MESH
     barrier = pltpu.get_barrier_semaphore()
     for step in range(1, groups):
-        pl.semaphore_signal(barrier, inc=1, device_id={"dp": lax.rem(dp + step, groups)}, device_id_type=mesh)
+        pl.semaphore_signal(barrier, inc=1, device_id={DP: lax.rem(dp + step, groups)}, device_id_type=mesh)
     for step in range(1, members):
-        pl.semaphore_signal(barrier, inc=1, device_id={"tensor": lax.rem(tensor + step, members)}, device_id_type=mesh)
+        pl.semaphore_signal(barrier, inc=1, device_id={TENSOR: lax.rem(tensor + step, members)}, device_id_type=mesh)
     pl.semaphore_wait(barrier, groups + members - 2)
     lanes = buf.shape[2] // 4
     for k, ref in enumerate(vectors):
@@ -1322,8 +1388,9 @@
         narrow[:, start : start + lanes] = total[row : row + 1, 3 * lanes :]
         row += 1
     buf[1] = total
-    exchange("tensor", tensor, members, buf.at[1], in_tensor, send_tensor, got_tensor)
-    total = buf[1]
+    kept = pl.ds(0, 3 * lanes)
+    exchange("tensor", tensor, members, buf.at[1, :, kept], in_tensor, send_tensor, got_tensor)
+    total = total[:, : 3 * lanes]
     for step in range(members - 1):
         total = total + in_tensor[step]
     for k in range(3):
@@ -1346,7 +1413,7 @@
         scratch_shapes=[
             pltpu.VMEM((2, 8, depth // 2), F32),
             pltpu.VMEM((groups - 1, 8, depth // 2), F32),
-            pltpu.VMEM((members - 1, 8, depth // 2), F32),
+            pltpu.VMEM((members - 1, 8, 3 * depth // 8), F32),
             pltpu.SemaphoreType.DMA((groups - 1,)),
             pltpu.SemaphoreType.DMA((groups - 1,)),
             pltpu.SemaphoreType.DMA((members - 1,)),
@@ -1383,7 +1450,7 @@
     groups, members = lax.axis_size("dp"), lax.axis_size("tensor")
     gain, shift = norm_gain.astype(F32)[None, :], norm_bias.astype(F32)[None, :]
     paired = groups == 4 and members == 8 and seqs == 4 and 2 * share == length
-    me = lax.axis_index("tensor")
+    me = lax.axis_index(TENSOR)
     if paired:
         chip = me // 2
         order = jnp.arange(3, -1, -1, dtype=jnp.int32) ^ chip
@@ -1416,7 +1483,7 @@
         rows = rows.reshape(everything, depth)
         first_full = first_full.reshape(depth, 3 * width + units)
 
-        def unheads(at, count, g, g_at, sums, sums_at, riding, wait_for=()):
+        def unheads(at, count, g, g_at, sums, sums_at, riding, wait_for=(), defer=False):
             return unattend(
                 at,
                 count,
@@ -1431,7 +1498,7 @@
                 row_ids,
                 tables,
                 riding=riding,
-                ident=next(idents),
+                ident="defer" if defer else next(idents),
                 wait_for=wait_for,
             )
 
@@ -1461,35 +1528,25 @@
         )
 
         ends, part = end, cuts(0.44)
-        near_attended_grad, near_hidden_grad, near_up_sum, full, end, middle = unmix(
-            None,
-            second_full,
-            hidden,
-            width,
-            pair,
-            pair,
-            length,
-            riding=[
-                gathering(full, (3, 0, part), ("second", 0, share)),
-                sending(far[1], "in", 0, part),
-                summing(far[1], ends, "middle", 0, part),
+        near_attended_grad, near_hidden_grad, near_up_sum, near_grad, near_sum, full, end, middle = chain(
+            [
+                unmix(None, second_full, hidden, width, pair, pair, length, ident="defer"),
+                unheads(pair, pair, Made(0, 0), 0, near_sums, 0, [], defer=True),
             ],
-            ident=next(idents),
-        )
-        near_grad, near_sum, full, end, middle = unheads(
-            pair,
-            pair,
-            near_attended_grad,
-            0,
-            near_sums,
-            0,
+            "unmix_unattend",
             [
                 gathering(
-                    full, (3, part, share), ("third", 0, part), late=[("third", part, share)]
+                    full,
+                    (3, part, share),
+                    ("second", 0, share),
+                    early=[(3, 0, part)],
+                    middle=[("third", 0, part)],
+                    late=[("third", part, share)],
                 ),
-                sending(far[1], "in", part, share, end),
-                summing(far[1], ends, "middle", part, share, middle),
+                sending(far[1], "in", 0, share),
+                summing(far[1], ends, "middle", 0, share),
             ],
+            next(idents),
         )
         upstream = full.reshape(everything, depth)
 
@@ -1506,51 +1563,54 @@
         mine = near[1]
         part = cuts(0.4)
 
-        far_attended_grad, far_hidden_grad, far_up_sum, side, middle = unmix(
-            upstream,
-            second_full,
-            hidden,
-            width,
-            0,
-            pair,
-            length,
-            riding=send_out(0, part),
-            ident=next(idents),
-        )
-
-        def backward(at, riding, wait_for=()):
+        def backward(at, g, hidden_grad, riding, ident, wait_for=()):
             return unattend_unproject(
                 at,
                 q,
                 k,
                 v,
-                far_attended_grad,
+                g,
                 at,
                 far_sums,
                 at,
                 column_ids,
                 row_ids,
                 tables,
-                far_hidden_grad,
+                hidden_grad,
                 at,
                 first_full,
                 riding + [Riding([a], [], False, 1, lambda *_: []) for a in wait_for],
-                next(idents),
+                ident,
             )
 
-        grads_0, sum_0, far_0, side, middle = backward(0, send_out(part, share, side, middle))
+        far_attended_grad, far_hidden_grad, far_up_sum, grads_0, sum_0, far_0, side, middle = chain(
+            [
+                unmix(upstream, second_full, hidden, width, 0, pair, length, ident="defer"),
+                backward(0, Made(0, 0), Made(0, 1), [], "defer"),
+            ],
+            "unmix_unattend_unproject",
+            send_out(0, share),
+            next(idents),
+        )
         output_terms = [mine, side, middle]
 
-        part = cuts(0.45)
-        up_part, end = outer_rows(
-            rows,
-            [far_hidden_grad, near_hidden_grad],
+        part = cuts(0.5)
+        second_part, end = outer_columns(
+            [far_attended, near_attended],
+            active,
+            upstream,
+            groups,
             riding=[sending(far_0, "in", 0, part)],
             ident=next(idents),
         )
-        up_grad = lax.psum_scatter(up_part, "dp", scatter_dimension=0, tiled=True)
+        second_grad = lax.psum_scatter(second_part, DP, scatter_dimension=0)
         grads_1, sum_1, far_1, end = backward(
-            1, [sending(far_0, "in", part, share, end)], [up_part]
+            1,
+            far_attended_grad,
+            far_hidden_grad,
+            [sending(far_0, "in", part, share, end)],
+            next(idents),
+            [second_part],
         )
     else:
         tables = rotary_tables(length)
@@ -1564,21 +1624,19 @@
         q, k, v, active, hidden = project(rows, first_full, bias, tables, width, units, length)
         attended, log_sums = attend(0, seqs, q, k, v, column_ids, row_ids)
         whole = each_tile(mix_body, [attended, active], second_full, depth, "mix")
-        output_terms = [lax.psum_scatter(whole, "tensor", scatter_dimension=0, tiled=True)]
+        output_terms = [lax.psum_scatter(whole, TENSOR, scatter_dimension=0, tiled=True)]
         attended_grad, hidden_grad, up_sum = unmix(
             upstream, second_full, hidden, width, 0, seqs, length
         )
     if paired:
-        ends, part = end, cuts(0.56)
-        second_part, end, middle = outer_columns(
-            [far_attended, near_attended],
-            active,
-            upstream,
-            groups,
+        ends, part = end, cuts(0.52)
+        up_part, end, middle = outer_rows(
+            rows,
+            [far_hidden_grad, near_hidden_grad],
             riding=[sending(far_1, "in", 0, part), summing(far_1, ends, "middle", 0, part)],
             ident=next(idents),
         )
-        second_grad = lax.psum_scatter(second_part, "dp", scatter_dimension=0)
+        up_grad = lax.psum_scatter(up_part, DP, scatter_dimension=0, tiled=True)
         *near, end, middle = unprojected(
             pair,
             [(near_grad, 0), (near_hidden_grad, 0)],
@@ -1594,9 +1652,9 @@
             [grads_0, grads_1, near_grad],
             riding=send_out(0, part),
             ident=next(idents),
-            wait_for=[up_grad],
-        )
-        first_grad = lax.psum_scatter(first_part, "dp", scatter_dimension=0, tiled=True)
+            wait_for=[second_grad],
+        )
+        first_grad = lax.psum_scatter(first_part, DP, scatter_dimension=0, tiled=True)
         side, middle = launch(
             nothing,
             [],
@@ -1617,13 +1675,13 @@
             0, seqs, q, k, v, attended_grad, 0, log_sums, 0, column_ids, row_ids, tables
         )
         whole = each_tile(unproject_body, [qkv_grad, hidden_grad], first_full, depth, "unproject")
-        terms = [lax.psum_scatter(whole, "tensor", scatter_dimension=0, tiled=True)]
+        terms = [lax.psum_scatter(whole, TENSOR, scatter_dimension=0, tiled=True)]
         (second_part,) = outer_columns([attended], active, upstream, groups)
         (first_part,) = outer_rows(rows, [qkv_grad])
         (up_part,) = outer_rows(rows, [hidden_grad])
-        second_grad = lax.psum_scatter(second_part, "dp", scatter_dimension=0)
-        first_grad = lax.psum_scatter(first_part, "dp", scatter_dimension=0, tiled=True)
-        up_grad = lax.psum_scatter(up_part, "dp", scatter_dimension=0, tiled=True)
+        second_grad = lax.psum_scatter(second_part, DP, scatter_dimension=0)
+        first_grad = lax.psum_scatter(first_part, DP, scatter_dimension=0, tiled=True)
+        up_grad = lax.psum_scatter(up_part, DP, scatter_dimension=0, tiled=True)
 
     first_grad = first_grad.astype(F32)
     input_grad, output, gain_part, shift_part, out_grad, down_grad, up_grad = closing(

time: 594 us -> 591 us (level)
    pallas_call x12 -> x10, Pallas kernels: 365 us -> 364 us  [chain(): pl.pallas_call(kernel, in_specs=[ANYWHERE] * (len(operands) + len(extra_i...]
  transfers between devices with their start and end apart: 3 -> 3, of which waited for: 0 -> 0; matrix products, arithmetic and copies ran while one was open for 1% -> 1% of each run, Pallas kernels for 29% -> 28%
where the time goes in v7:
time: 591 us; the launch traced here: 584 us
  Pallas kernels  553 us (94%)
  local copies, waits for them, and re-layouts  16.1 us (3%)
  between operations  14.2 us (2%)
    pallas_call x10, Pallas kernels, chain(): pl.pallas_call(kernel, in_specs=[ANYWHERE] * (len(operands) + len(extra_i...  364 us
    pallas_call x1, Pallas kernels, opening(): pl.pallas_call(functools.partial(opening_kernel, tile, groups, width, cut...  163 us
    pallas_call x1, Pallas kernels, closing(): pl.pallas_call(functools.partial(closing_kernel, len(parts)), grid_spec=p...  14.3 us
  transfers between devices with their start and end apart: 3, of which 0 were waited for; matrix products, arithmetic and copies ran while one was open for 1% of the time, Pallas kernels for 28%

profile of v7, /device:TPU:0, one launch (start us, length us, event | category | flops | bytes accessed | tf_op | source)
XLA Modules:
  0.0 583.7 jit_solution(2190158572766415222)
XLA Ops:
  8.5 0.6 reshape.73.refs_4_.refs_7_.refs_8_.refs_6_
  9.1 2.0 copy.53
  11.1 0.6 broadcast_in_dim.33.refs_1_.gain
  11.7 0.6 broadcast_in_dim.36.refs_2_
  14.6 163.1 %opening.1 = (bf16[4,2,512,2048]{3,2,1,0:T(8,128)(2,1)}, bf16[4,2,512,2048]{3,2,1,0:T(8,128)(2,1)}, bf16[4,512,1792]{2,1,0:T(8,128)(2,1)}, bf16[1280,2048]{1,0:T...) custom-call(bf16[512,2048]{1,0:T(8,128)(2,1)} %x.1, ...), custom_call_target="tpu_custom_call" | custom-call | flops 3006477056 | bytes 6291456 | tf_op jit(solution)/shard_map/opening/pallas_call | solution.py:740
  177.7 35.5 %attend_mix.2 = (bf16[2048,256]{1,0:T(8,128)(2,1)}, f32[8,2048]{1,0:T(8,128)}, bf16[512,2048]{1,0:T(8,128)(2,1)}, bf16[512,2048]{1,0:T(8,128)(2,1)}, bf16[4,2,512,2048]{3,2,1,0:T(8,128)(2,1)}) custom-call(bf16[4096,256]{1,0:T(8,128)(2,1)} %get-tuple-element.84.refs_0_.refs_2_.refs_3_, ...), custom_call_target="tpu_custom_call", output_to_operand_aliasing={{4}: (7, {})} | custom-call | flops 1374389504 | bytes 419430 | tf_op jit(solution)/shard_map/attend_mix/pallas_call | solution.py:501
  213.2 49.3 %attend_mix.3 = (bf16[2048,256]{1,0:T(8,128)(2,1)}, f32[8,2048]{1,0:T(8,128)}, bf16[512,2048]{1,0:T(8,128)(2,1)}, bf16[512,2048]{1,0:T(8,128)(2,1)}, bf16[4,2,51...) custom-call(bf16[4096,256]{1,0:T(8,128)(2,1)} %get-tuple-element.84.refs_0_.refs_2_.refs_3_, ...), custom_call_target="tpu_custom_call", output_to_operand_aliasing={{4}: (7, {})} | custom-call | flops 1374389504 | bytes 419430 | tf_op jit(solution)/shard_map/attend_mix/pallas_call | solution.py:501
  262.6 55.5 %unmix_unattend.1 = (bf16[2048,256]{1,0:T(8,128)(2,1)}, bf16[2048,1024]{1,0:T(8,128)(2,1)}, f32[1,1024]{1,0:T(1,128)}, bf16[2048,768]{1,0:T(8,128)(2,1)}, f32[1,...) custom-call(f32[4096,1024]{1,0:T(8,128)} %get-tuple-element.82.refs_, ...), custom_call_target="tpu_custom_call", output_to_operand_aliasing={{5}: (11, {})} | custom-call | flops 1073741824 | bytes 2621440 | tf_op jit(solution)/shard_map/unmix_unattend/pallas_call | solution.py:501
  318.1 53.5 %unmix_unattend_unproject.1 = (bf16[2048,256]{1,0:T(8,128)(2,1)}, bf16[2048,1024]{1,0:T(8,128)(2,1)}, f32[1,1024]{1,0:T(1,128)}, bf16[1024,768]{1,0:T(8,128)(2,1...) custom-call(f32[4096,1024]{1,0:T(8,128)} %get-tuple-element.82.refs_0_,, ...), custom_call_target="tpu_custom_call" | custom-call | flops 1073741824 | bytes 2621440 | tf_op jit(solution)/shard_map/unmix_unattend_unproject/pallas_call | solution.py:501
  371.6 30.7 %outer_columns.1 = (bf16[4,1280,512]{2,1,0:T(8,128)(2,1)}, bf16[512,2048]{1,0:T(8,128)(2,1)}) custom-call(bf16[4096,2048]{1,0:T(8,128)(2,1)} %bitcast.20, bf16[2048,256]{1,0:T(8,128)(2,1)} %get-tuple-element.99.refs_1_, bf16[2048,256]{1,0:T(8,128)(2,1)} %get-tuple-element.100.refs_2_, bf16[4096,1024]{1,0:T(8,128)(2,1)} %get-tuple-element.87.refs_5_.refs_3_, ...), custom_call_target="tpu_custom_call" | custom-call | flops 2147483648 | bytes 3250585 | tf_op jit(solution)/shard_map/outer_columns/pallas_call | solution.py:501
  402.6 31.2 %unattend_unproject.1 = (bf16[1024,768]{1,0:T(8,128)(2,1)}, f32[1,768]{1,0:T(1,128)}, bf16[512,2048]{1,0:T(8,128)(2,1)}, bf16[512,2048]{1,0:T(8,128)(2,1)}) custom-call(bf16[4096,256]{1,0:T(8,128)(2,1)} %get-tuple-element.84.refs_0_.refs_2_.refs_3_, bf16[4096,256]{1,0:T(8,128)(2,1)} %get-tuple-element.85.refs_1_.refs_3_.refs_4_, ...), custom_call_target="tpu_custom_call", output_to_operand_aliasing={{3}: (13, {})} | custom-call | flops 1717986944 | bytes 367001 | tf_op jit(solution)/shard_map/unattend_unproject/pallas_call | solution.py:501
  433.8 27.6 %outer_rows.2 = (bf16[2048,1024]{1,0:T(8,128)(2,1)}, bf16[512,2048]{1,0:T(8,128)(2,1)}, bf16[512,2048]{1,0:T(8,128)(2,1)}) custom-call(bf16[4096,2048]{1,0:T(8,128)(2,1)} %bitcast.26, bf16[2048,1024]{1,0:T(8,128)(2,1)} %get-tuple-element.109.refs_10_.refs_1_, bf16[2048,1024]{1,0:T(8,128)(2,1)} %get-tuple-element.110.refs_2_.refs_1_, ...), custom_call_target="tpu_custom_call" | custom-call | flops 1717986944 | bytes 2936012 | tf_op jit(solution)/shard_map/outer_rows/pallas_call | solution.py:501
  461.7 26.1 %unproject.1 = (bf16[512,2048]{1,0:T(8,128)(2,1)}, bf16[512,2048]{1,0:T(8,128)(2,1)}, bf16[512,2048]{1,0:T(8,128)(2,1)}, bf16[512,2048]{1,0:T(8,128)(2,1)}) custom-call(bf16[2048,768]{1,0:T(8,128)(2,1)} %get-tuple-element.116.refs_0_.refs_3_, bf16[2048,1024]{1,0:T(8,128)(2,1)} %get-tuple-element.110.refs_2_.refs_1_, ...), custom_call_target="tpu_custom_call", output_to_operand_aliasing={{2}: (4, {}), {3}: (7, {})} | custom-call | flops 1503238528 | bytes 2306867 | tf_op jit(solution)/shard_map/unproject/pallas_call | solution.py:501
  487.9 27.9 %outer_rows.3 = (bf16[2048,768]{1,0:T(8,128)(2,1)}, bf16[512,2048]{1,0:T(8,128)(2,1)}, bf16[512,2048]{1,0:T(8,128)(2,1)}) custom-call(bf16[4096,2048]{1,0:T(8,128)(2,1)} %bitcast.27, bf16[1024,768]{1,0:T(8,128)(2,1)} %get-tuple-element.122.refs_1_, bf16[1024,768]{1,0:T(8,128)(2,1)} %get-tuple-element.123.refs_2_, ...), custom_call_target="tpu_custom_call" | custom-call | flops 1288490240 | bytes 2621440 | tf_op jit(solution)/shard_map/outer_rows/pallas_call | solution.py:501
  515.9 0.6 copy-done.5
  516.5 0.6 broadcast_in_dim.34.bias
  517.1 0.6 broadcast_in_dim.35.other_bias
  517.7 26.5 %finish.1 = (bf16[512,2048]{1,0:T(8,128)(2,1)}, bf16[512,2048]{1,0:T(8,128)(2,1)}) custom-call(bf16[512,2048]{1,0:T(8,128)(2,1)} %get-tuple-element.120.refs_4_.refs_0_, bf16[512,2048]{1,0:T(8,128)(2,1)} %get-tuple-element.121.refs_5_.refs_1_, bf16[512,2048]{1,0:T(8,128)(2,1)} %get-tuple-element.125.refs_2_, ...), custom_call_target="tpu_custom_call", output_to_operand_aliasing={{0}: (2, {}), {1}: (5, {})} | custom-call | flops 100000000 | bytes 100000 | tf_op jit(solution)/shard_map/finish/pallas_call | solution.py:501
  544.3 14.3 %closing.1 = (bf16[512,2048]{1,0:T(8,128)(2,1)}, bf16[512,2048]{1,0:T(8,128)(2,1)}, f32[1,2048]{1,0:T(1,128)}, f32[1,2048]{1,0:T(1,128)}, f32[256,512]{1,0:T(8,1...) custom-call(s32[1]{0:T(128)} %bitcast.flag, bf16[512,2048]{1,0:T(8,128)(2,1)} %x.1, bf16[512,2048]{1,0:T(8,128)(2,1)} %g.1, ...), custom_call_target="tpu_custom_call" | custom-call | flops 3145728 | bytes 1468006 | tf_op jit(solution)/shard_map/closing/pallas_call | solution.py:161
  558.6 11.4 %sum_everywhere.1 = (f32[8,2048]{1,0:T(8,128)}, f32[1,1792]{1,0:T(1,128)}) custom-call(f32[1,2048]{1,0:T(1,128)} %get-tuple-element.135.refs_0_, f32[1,2048]{1,0:T(1,128)} %get-tuple-element.136.refs_1_, f32[1,2048]{1,0:T(1,128)} %get-tuple-element.137.refs_2_, f32[1,768]{1,0:T(1,128)} %get-tuple-element.138.refs_3_, f32[1,768]{1,0:T(1,128)} %get-tuple-element.139.refs_4_, ...), custom_call_target="tpu_custom_call" | custom-call | tf_op jit(solution)/shard_map/sum_everywhere/pallas_call | solution.py:1405
  570.0 1.6 fusion.2
  571.6 1.3 slice.55
  572.8 1.3 fusion.3
  574.1 2.3 fusion.1
  (39 shorter events, 4.7 us)
Async XLA Ops:
  7.2 0.7 copy-start
  7.2 3.9 copy-start.3
  7.2 4.5 copy-start.4
  7.2 5.1 copy-start.7
  7.2 5.7 copy-start.8
  7.2 6.2 %copy-start.9 = (bf16[256]{0:T(256)(128)(2,1)S(1)}, bf16[256]{0:T(256)(128)(2,1)}, u32[]{:S(2)}) copy-start(bf16[256]{0:T(256)(128)(2,1)} %param.25) | copy-start | bytes 1540
  7.2 6.8 %copy-start.10 = (bf16[256]{0:T(256)(128)(2,1)S(1)}, bf16[256]{0:T(256)(128)(2,1)}, u32[]{:S(2)}) copy-start(bf16[256]{0:T(256)(128)(2,1)} %param.27) | copy-start | bytes 1540
  7.3 480.6 %reduce-scatter.10.cloned.1.call-start = ((), (), s32[]{:S(2)}) async-start(), calls=%async_computation.5 | async-start | bytes 6553600
  402.4 141.9 %reduce-scatter.6.cloned.1.call-start = ((), (), s32[]{:S(2)}) async-start(), calls=%async_computation.3 | async-start | bytes 5242880 | tf_op jit(solution)/shard_map/reduce_scatter | solution.py:1639
  461.5 112.6 %reduce-scatter.8.cloned.1.call-start = ((), (), s32[]{:S(2)}) async-start(), calls=%async_computation.4 | async-start | bytes 3932160 | tf_op jit(solution)/shard_map/reduce_scatter | solution.py:1657
  515.8 0.7 copy-start.5
  515.8 1.3 copy-start.6
  544.3 32.7 %copy-start.1 = (s32[4,1024]{1,0:T(4,128)S(1)}, s32[4,1024]{1,0:T(4,128)}, u32[]{:S(2)}) copy-start(s32[4,1024]{1,0:T(4,128)} %param.19) | copy-start | bytes 49156
  571.6 5.4 copy-start.2
Sparse Core Ops, SparseCore 0:
  402.5 60.2 reduce-scatter.9
  465.8 52.7 reduce-scatter.5
  521.8 45.3 reduce-scatter.7
